TPU v7x, 32 devices: a whole 2x2x4 slice. The times are simulated.
32 devices in a mesh: dp: 8 (over z, x), sp: 4 (over y, core).
Axes of the slice: x: 2, y: 2, z: 4, core: 2. Of those that a mesh axis runs over, the one named last changes fastest.
Arguments:
- inputs: bfloat16 [16, 512, 768], P('dp', 'sp'), may hold values from -6 to 6
- cotangent: bfloat16 [16, 512, 768], P('dp', 'sp'), may hold values from -6 to 6
- joined_weight: bfloat16 [768, 2304], P(('dp', 'sp')), may hold values from -0.21875 to 0.21875
- joined_bias: bfloat16 [2304], P(('dp', 'sp')), may hold values from -3 to 3
- dense_weight: bfloat16 [768, 768], P(('dp', 'sp')), may hold values from -1.75 to 1.75
- dense_bias: bfloat16 [768], P(('dp', 'sp')), may hold values from -3 to 3
- expand_weight: bfloat16 [768, 3072], P(('dp', 'sp')), may hold values from -0.21875 to 0.21875
- expand_bias: bfloat16 [3072], P(('dp', 'sp')), may hold values from -3 to 3
- shrink_weight: bfloat16 [3072, 768], P(('dp', 'sp')), may hold values from -0.109375 to 0.109375
- shrink_bias: bfloat16 [768], P(('dp', 'sp')), may hold values from -3 to 3
- attn_gain: bfloat16 [768], P(('dp', 'sp')), may hold values from 0.5 to 1.5
- attn_shift: bfloat16 [768], P(('dp', 'sp')), may hold values from -3 to 3
- mlp_gain: bfloat16 [768], P(('dp', 'sp')), may hold values from 0.5 to 1.5
- mlp_shift: bfloat16 [768], P(('dp', 'sp')), may hold values from -3 to 3
Outputs:
- output: bfloat16 [16, 512, 768], P('dp', 'sp')
- input_grad: float32 [16, 512, 768], P('dp', 'sp')
- joined_weight_grad: float32 [768, 2304], P(('dp', 'sp'))
- joined_bias_grad: float32 [2304], P(('dp', 'sp'))
- dense_weight_grad: float32 [768, 768], P(('dp', 'sp'))
- dense_bias_grad: float32 [768], P(('dp', 'sp'))
- expand_weight_grad: float32 [768, 3072], P(('dp', 'sp'))
- expand_bias_grad: float32 [3072], P(('dp', 'sp'))
- shrink_weight_grad: float32 [3072, 768], P(('dp', 'sp'))
- shrink_bias_grad: float32 [768], P(('dp', 'sp'))
- attn_gain_grad: float32 [768], P(('dp', 'sp'))
- attn_shift_grad: float32 [768], P(('dp', 'sp'))
- mlp_gain_grad: float32 [768], P(('dp', 'sp'))
- mlp_shift_grad: float32 [768], P(('dp', 'sp'))
All inputs are finite; a program needn't handle non-finite values.
Results may differ from a plain program's by a relative error of at most 0.011.
Values may be sent and summed in bfloat16 or wider, within the bound.
No kernel may reach another device: no remote copies, remote signals or barrier semaphores. Data moves between devices by JAX's collectives and lax.ppermute only.
A program may use at most 128 MiB of HBM per device.

v0:
```python
import functools

import jax
import jax.numpy as jnp
from jax import lax
from jax.experimental import pallas as pl
from jax.experimental.pallas import tpu as pltpu
from jax.sharding import PartitionSpec as P

HEADS = 12
HD = 64
ROT = 16
LANES = 128
NORM_EPS = 1e-05
BF = jnp.bfloat16
F32 = jnp.float32
VMEM_LIMIT = 60 * 1024 * 1024


def bits_of(count):
    assert count & (count - 1) == 0
    bit = 1
    out = []
    while bit < count:
        out.append(bit)
        bit *= 2
    return out


def cube_order(count):
    order = [0]
    for bit in reversed(bits_of(count)):
        order = order + [k ^ bit for k in order]
    return order


def swap(value, axis, bit):
    count = lax.axis_size(axis)
    return lax.ppermute(value, axis, [(i, i ^ bit) for i in range(count)])


def halves(block, axis):
    mine, got = None, block[None]
    for bit in reversed(bits_of(lax.axis_size(axis))):
        mine = got if mine is None else jnp.concatenate([mine, got], axis=0)
        got = swap(mine, axis, bit)
    return mine, got


def token_blocks(block, axis):
    blocks = [block]
    for bit in reversed(bits_of(lax.axis_size(axis))):
        blocks = blocks + [swap(b, axis, bit) for b in blocks]
    return blocks


def cube_scatter(value, axis, wire):
    for bit in bits_of(lax.axis_size(axis)):
        half = value.shape[0] // 2
        got = swap(value[half:].astype(wire), axis, bit)
        value = value[:half].astype(F32) + got.astype(F32)
    return value


def flip_bits(blocks, axis):
    count = lax.axis_size(axis)
    me = lax.axis_index(axis)
    rest = blocks.shape[1:]
    for bit in bits_of(count):
        pairs = blocks.reshape((count // (2 * bit), 2, bit) + rest)
        blocks = jnp.where((me & bit) > 0, pairs[:, ::-1], pairs).reshape((count,) + rest)
    return blocks


def turn_bits(blocks):
    count = blocks.shape[0]
    bits = len(bits_of(count))
    rest = blocks.shape[1:]
    blocks = blocks.reshape((2,) * bits + rest)
    axes = tuple(reversed(range(bits))) + tuple(range(bits, bits + len(rest)))
    return blocks.transpose(axes).reshape((count,) + rest)


def layer_norm(values):
    mean_val = jnp.mean(values, axis=-1, keepdims=True)
    centred = values - mean_val
    variance = jnp.mean(centred * centred, axis=-1, keepdims=True)
    inv_std = lax.rsqrt(variance + NORM_EPS)
    return centred * inv_std, inv_std


def dot(left, right, left_dim, right_dim):
    dims = (((left_dim,), (right_dim,)), ((), ()))
    return lax.dot_general(left, right, dims, preferred_element_type=F32)


def row_sum(value):
    return jnp.sum(value, axis=0, keepdims=True)


def copies_in(blocks, target, rows, sem):
    out = []
    for i, block in enumerate(blocks):
        out.append(pltpu.make_async_copy(block, target.at[pl.ds(i * rows, rows)], sem.at[i]))
    return out


def placed(ids, mine, got, target, rows, width, sem):
    out = []
    half = mine.shape[0]
    for p in range(2 * half):
        source = mine.at[p] if p < half else got.at[p - half]
        if source.shape != (rows, width):
            source = source.at[pl.ds(0, rows), pl.ds(0, width)]
        to = pl.multiple_of(ids[p] * rows, 8)
        out.append(pltpu.make_async_copy(source, target.at[pl.ds(to, rows)], sem.at[p]))
    return out


def sent(ids, source, out, rows, sem):
    todo = []
    for p in range(out.shape[0]):
        at = pl.multiple_of(ids[p] * rows, 8)
        to = out.at[p] if out.shape[1] == rows else out.at[p, pl.ds(0, rows)]
        todo.append(pltpu.make_async_copy(source.at[pl.ds(at, rows)], to, sem.at[p]))
    return todo


def run(copies):
    for copy in copies:
        copy.start()


def finish(copies):
    for copy in copies:
        copy.wait()


def grad_rows(left, right, out):
    rows = 256

    @pl.loop(0, left.shape[1] // rows)
    def _(r):
        at = pl.ds(pl.multiple_of(r * rows, rows), rows)
        out[at, :] = dot(left[:, at], right[...], 0, 0).astype(BF)


def mlp_kernel(sp, ids, *refs):
    xs, cots = refs[:sp], refs[sp : 2 * sp]
    ew_mine, ew_got, sw_mine, sw_got, ap, ea, vec, dense = refs[2 * sp : 2 * sp + 8]
    eg_out, sg_out, keep, send, sums = refs[2 * sp + 8 : 2 * sp + 13]
    x, cot, ew, sw, hid, act, pgr, eg, sg, sem = refs[2 * sp + 13 :]
    width = x.shape[1]
    chunk = x.shape[0] // sp
    rows = ew_mine.shape[1]
    units = sw_mine.shape[1]
    gets = (
        copies_in([b.at[pl.ds(0, chunk)] for b in xs], x, chunk, sem.at[0])
        + copies_in(cots, cot, chunk, sem.at[1])
        + placed(ids, ew_mine, ew_got, ew, rows, ew.shape[1], sem.at[2])
        + placed(ids, sw_mine, sw_got, sw, units, width, sem.at[3])
    )
    run(gets)
    sums[...] = jnp.zeros_like(sums)
    finish(gets)
    gain, shift, add = vec[0:1, :], vec[1:2, :], vec[2:3, : ew.shape[1]]

    @pl.loop(0, sp)
    def _(k):
        at = pl.ds(pl.multiple_of(k * chunk, chunk), chunk)
        normed, _ = layer_norm(x[at, :].astype(F32))
        hidden = (normed * gain + shift).astype(BF)
        hid[at, :] = hidden
        pre = dot(hidden, ew[...], 1, 0) + add
        cdf = 0.5 * (1.0 + lax.erf(pre * 0.7071067811865476))
        activated = (pre * cdf).astype(BF)
        act[at, :] = activated
        slope = cdf + pre * jnp.exp(-0.5 * pre * pre) * 0.3989422804014327
        pre_grad = dot(cot[at, :], sw[...], 1, 1) * slope
        sums[0:1, : ew.shape[1]] += row_sum(pre_grad)
        pre_grad_bf = pre_grad.astype(BF)
        pgr[at, :] = pre_grad_bf
        out_part = dot(activated, sw[...], 1, 0) + ap[k].astype(F32)
        hidden_grad = dot(pre_grad_bf, ew[...], 1, 1)
        sums[1:2, :] += row_sum(hidden_grad * normed)
        sums[2:3, :] += row_sum(hidden_grad)
        scaled = hidden_grad * gain + ea[k].astype(F32)

        @pl.when(k < sp // 2)
        def _():
            keep[k, 0] = out_part.astype(BF)
            keep[k, 1] = scaled.astype(BF)

        @pl.when(k >= sp // 2)
        def _():
            send[k - sp // 2, 0] = out_part.astype(BF)
            send[k - sp // 2, 1] = scaled.astype(BF)

    grad_rows(hid, pgr, eg)
    puts = sent(ids, eg, eg_out, rows, sem.at[0])
    run(puts)
    grad_rows(act, cot, sg)
    more = sent(ids, sg, sg_out, units, sem.at[1])
    for p in range(sg_out.shape[0]):
        to = sg_out.at[p, pl.ds(units, dense.shape[1])]
        more.append(pltpu.make_async_copy(dense.at[ids[p]], to, sem.at[2, p]))
    run(more)
    finish(puts + more)


def attn_kernel(sp, seqs, heads, ids, *refs):
    xs, cots = refs[:sp], refs[sp : 2 * sp]
    jw_mine, jw_got, dw, vec, jadd, cos_ref, sin_ref, posc, posr = refs[2 * sp : 2 * sp + 9]
    ap, ea, jg_out, dense_g, sums, jsum = refs[2 * sp + 9 : 2 * sp + 15]
    x, cot, jw, hid, rot, cg, ctx, jgf, jgb, ctk, gr, sem = refs[2 * sp + 15 :]
    width = x.shape[1]
    wide = jw.shape[1]
    cols = heads * 3 * HD
    chunk = x.shape[0] // sp
    part = chunk // seqs
    full = part * sp
    rows = jg_out.shape[1]
    scale = HD ** (-0.5)
    gets = (
        copies_in([b.at[pl.ds(0, chunk)] for b in xs], x, chunk, sem.at[0])
        + copies_in(cots, cot, chunk, sem.at[1])
        + placed(ids, jw_mine, jw_got, jw, rows, wide, sem.at[2])
    )
    run(gets)
    sums[...] = jnp.zeros_like(sums)
    jsum[...] = jnp.zeros_like(jsum)
    jgf[:, cols:] = jnp.zeros((jgf.shape[0], wide - cols), F32)
    finish(gets)
    gain, shift = vec[0:1, :], vec[1:2, :]

    def tables(g, k):
        at = pl.ds(pl.multiple_of(k * part, part), part)
        lane = lax.broadcasted_iota(jnp.int32, (part, LANES), 1)
        col = lane + g * LANES
        inner = col % HD
        turned = (inner < ROT) & ((col // HD) % 3 < 2) & (col < cols)
        cos_val, sin_val = cos_ref[at, :], sin_ref[at, :]
        low = jnp.where(turned & (inner < ROT // 2), sin_val, 0.0)
        high = jnp.where(turned & (inner >= ROT // 2), sin_val, 0.0)
        both = [jnp.where(turned, cos_val, 1.0), low, high]
        return [jnp.concatenate([t] * seqs, axis=0) for t in both]

    def rotate(value, g, k, sign):
        cos_val, low, high = tables(g, k)
        up = pltpu.roll(value, LANES - ROT // 2, 1)
        down = pltpu.roll(value, ROT // 2, 1)
        return value * cos_val + sign * (down * high - up * low)

    def spread(ref, k, lanes, value):
        for b in range(seqs):
            at = pl.ds(pl.multiple_of(b * full + k * part, part), part)
            ref[at, lanes] = value[b * part : (b + 1) * part]

    def collect(ref, k, lanes):
        at = [pl.ds(pl.multiple_of(b * full + k * part, part), part) for b in range(seqs)]
        return jnp.concatenate([ref[a, lanes] for a in at], axis=0)

    @pl.loop(0, sp)
    def _(k):
        at = pl.ds(pl.multiple_of(k * chunk, chunk), chunk)
        normed, _ = layer_norm(x[at, :].astype(F32))
        hidden = (normed * gain + shift).astype(BF)
        hid[at, :] = hidden
        joined = dot(hidden, jw[...], 1, 0) + jadd[...]
        for g in range(wide // LANES):
            lanes = slice(g * LANES, (g + 1) * LANES)
            spread(rot, k, lanes, rotate(joined[:, lanes], g, k, 1.0).astype(BF))
        spread(cg, k, slice(None), dot(cot[at, :], dw[...], 1, 1).astype(BF))

    allowed = posc[...] >= posr[...]

    @pl.loop(0, seqs)
    def _(b):
        at = pl.ds(pl.multiple_of(b * full, full), full)
        for h in range(heads):
            q0 = h * 3 * HD
            query = rot[at, q0 : q0 + HD]
            key = rot[at, q0 + HD : q0 + 2 * HD]
            value = rot[at, q0 + 2 * HD : q0 + 3 * HD]
            grad = cg[at, h * HD : (h + 1) * HD]
            scores = dot(query, key, 1, 1) * scale
            total = jnp.sum(jnp.where(allowed, jnp.exp(scores), 0.0), axis=-1, keepdims=True)
            probs = jnp.where(allowed, jnp.exp(scores - jnp.log(total)), 0.0)
            weights = probs.astype(BF)
            context = dot(weights, value, 1, 0)
            ctx[at, h * HD : (h + 1) * HD] = context.astype(BF)
            delta = jnp.sum(grad.astype(F32) * context, axis=-1, keepdims=True)
            jgf[at, q0 + 2 * HD : q0 + 3 * HD] = dot(weights, grad, 0, 0)
            score_grad = (probs * (dot(grad, value, 1, 1) - delta) * scale).astype(BF)
            jgf[at, q0 : q0 + HD] = dot(score_grad, key, 1, 0)
            jgf[at, q0 + HD : q0 + 2 * HD] = dot(score_grad, query, 0, 0)

    @pl.loop(0, sp)
    def _(k):
        at = pl.ds(pl.multiple_of(k * chunk, chunk), chunk)
        for g in range(wide // LANES):
            lanes = slice(g * LANES, (g + 1) * LANES)
            back = rotate(collect(jgf, k, lanes), g, k, -1.0).astype(BF)
            jgb[at, lanes] = back
            jsum[0:1, lanes] += row_sum(back.astype(F32))
        hidden_grad = dot(jgb[at, :], jw[...], 1, 1)
        normed, _ = layer_norm(x[at, :].astype(F32))
        sums[0:1, :] += row_sum(hidden_grad * normed)
        sums[1:2, :] += row_sum(hidden_grad)
        ea[k] = (hidden_grad * gain).astype(BF)
        context = collect(ctx, k, slice(None))
        ctk[at, :] = context
        ap[k] = dot(context, dw[...], 1, 0).astype(BF)

    grad_rows(hid, jgb, gr)
    puts = sent(ids, gr, jg_out, rows, sem.at[0])
    run(puts)
    dense_g[...] = dot(ctk[...], cot[...], 0, 0).astype(BF)
    finish(puts)


ANY = pl.BlockSpec(memory_space=pl.ANY)
IN_VMEM = pl.BlockSpec(memory_space=pltpu.VMEM)
IN_SMEM = pl.BlockSpec(memory_space=pltpu.SMEM)


def call(body, name, args, specs, outs, out_specs, scratch, flops):
    moved = sum(a.size * a.dtype.itemsize for a in args)
    moved += sum(o.size * o.dtype.itemsize for o in outs)
    return pl.pallas_call(
        body,
        name=name,
        in_specs=specs,
        out_shape=outs,
        out_specs=out_specs,
        scratch_shapes=scratch,
        compiler_params=pltpu.CompilerParams(vmem_limit_bytes=VMEM_LIMIT),
        cost_estimate=pl.CostEstimate(flops=flops, bytes_accessed=moved, transcendentals=0),
    )(*args)


def attention(ids, xs, cots, jw, dw, vec, jadd, tables, poss, seqs, heads):
    sp = len(xs)
    chunk, width = cots[0].shape
    tokens = sp * chunk
    wide = jadd.shape[1]
    dp = 2 * jw[0].shape[0]
    rows = width // dp
    shape = jax.ShapeDtypeStruct
    outs = [
        shape((sp, chunk, width), BF),
        shape((sp, chunk, width), BF),
        shape((dp, rows, wide), BF),
        shape((heads * HD, width), BF),
        shape((8, width), F32),
        shape((8, wide), F32),
    ]
    scratch = [
        pltpu.VMEM((tokens, width), BF),
        pltpu.VMEM((tokens, width), BF),
        pltpu.VMEM((width, wide), BF),
        pltpu.VMEM((tokens, width), BF),
        pltpu.VMEM((tokens, wide), BF),
        pltpu.VMEM((tokens, heads * HD), BF),
        pltpu.VMEM((tokens, heads * HD), BF),
        pltpu.VMEM((tokens, wide), F32),
        pltpu.VMEM((tokens, wide), BF),
        pltpu.VMEM((tokens, heads * HD), BF),
        pltpu.VMEM((width, wide), BF),
        pltpu.SemaphoreType.DMA((3, max(dp, sp))),
    ]
    return call(
        functools.partial(attn_kernel, sp, seqs, heads),
        "attention_branch",
        [ids, *xs, *cots, *jw, dw, vec, jadd, *tables, *poss],
        [IN_SMEM] + [ANY] * (2 * sp + 2) + [IN_VMEM] * 7,
        outs,
        [IN_VMEM, IN_VMEM, ANY, IN_VMEM, IN_VMEM, IN_VMEM],
        scratch,
        12 * tokens * width * wide,
    )


def feed_forward(ids, xs, cots, ew, sw, ap, ea, vec, dense):
    sp = len(xs)
    chunk, width = cots[0].shape
    tokens = sp * chunk
    units = ew[0].shape[2]
    dp = 2 * ew[0].shape[0]
    rows, per, extra = ew[0].shape[1], sw[0].shape[1], dense.shape[1]
    shape = jax.ShapeDtypeStruct
    outs = [
        shape((dp, rows, units), BF),
        shape((dp, per + extra + 8, width), BF),
        shape((sp // 2, 2, chunk, width), BF),
        shape((sp // 2, 2, chunk, width), BF),
        shape((8, width), F32),
    ]
    scratch = [
        pltpu.VMEM((tokens, width), BF),
        pltpu.VMEM((tokens, width), BF),
        pltpu.VMEM((width, units), BF),
        pltpu.VMEM((units, width), BF),
        pltpu.VMEM((tokens, width), BF),
        pltpu.VMEM((tokens, units), BF),
        pltpu.VMEM((tokens, units), BF),
        pltpu.VMEM((width, units), BF),
        pltpu.VMEM((units, width), BF),
        pltpu.SemaphoreType.DMA((4, max(dp, sp))),
    ]
    return call(
        functools.partial(mlp_kernel, sp),
        "feed_forward_branch",
        [ids, *xs, *cots, *ew, *sw, ap, ea, vec, dense],
        [IN_SMEM] + [ANY] * (2 * sp + 4) + [IN_VMEM] * 4,
        outs,
        [ANY, ANY, IN_VMEM, IN_VMEM, IN_VMEM],
        scratch,
        12 * tokens * width * units,
    )


def on_device(
    inputs,
    cotangent,
    joined_weight,
    joined_bias,
    dense_weight,
    dense_bias,
    expand_weight,
    expand_bias,
    shrink_weight,
    shrink_bias,
    attn_gain,
    attn_shift,
    mlp_gain,
    mlp_shift,
):
    seqs, local_len, width = inputs.shape
    sp, dp = lax.axis_size("sp"), lax.axis_size("dp")
    me, dp_me = lax.axis_index("sp"), lax.axis_index("dp")
    heads = HEADS // sp
    local = seqs * local_len
    cols = joined_weight.shape[1] // sp
    wide = -(-cols // LANES) * LANES
    row_n = joined_weight.shape[0]
    rows_d = row_n * sp
    ff_n = shrink_weight.shape[0]
    units = ff_n * dp
    sp_order, dp_order = cube_order(sp), cube_order(dp)
    ids = jnp.asarray(dp_order, jnp.int32) ^ dp_me

    expand_part = expand_weight.reshape(row_n, dp, sp, ff_n).transpose(2, 0, 1, 3)
    joined_part = joined_weight.reshape(row_n, sp, cols).transpose(1, 0, 2)
    joined_part = jnp.pad(joined_part, ((0, 0), (0, 0), (0, units - cols)))
    both = jnp.concatenate([expand_part.reshape(sp, row_n, units), joined_part], axis=1)
    both = lax.all_to_all(both, "sp", split_axis=0, concat_axis=0, tiled=True)
    expand_part = both[:, :row_n].reshape(rows_d, units)
    joined_part = both[:, row_n:, :cols].reshape(rows_d, cols)

    small_parts = (
        joined_bias,
        dense_bias,
        expand_bias,
        shrink_bias,
        attn_gain,
        attn_shift,
        mlp_gain,
        mlp_shift,
    )
    sizes = [part.shape[0] for part in small_parts]
    small = jnp.stack([jnp.pad(part, (0, width - part.shape[0])) for part in small_parts])
    xs = token_blocks(jnp.concatenate([inputs.reshape(local, width), small]), "sp")
    cots = token_blocks(cotangent.reshape(local, width), "sp")
    small = jnp.stack([block[local:, :LANES] for block in xs])
    small = flip_bits(turn_bits(small), "sp").transpose(1, 0, 2).reshape(8, sp * LANES)
    small = jnp.pad(small, ((0, 0), (0, width - sp * LANES)))

    dense_part = dense_weight.reshape(rows_d, width // sp)
    attn_pack = jnp.concatenate([joined_part, dense_part], axis=1)
    attn_pack = jnp.concatenate([attn_pack, small], axis=0)
    joined_w = halves(attn_pack, "dp")
    shrink_w = halves(shrink_weight, "dp")
    expand_w = halves(expand_part, "dp")

    def natural(lanes_at, lanes, rows_at, rows):
        got = [h[:, rows_at : rows_at + rows, lanes_at : lanes_at + lanes] for h in joined_w]
        return flip_bits(turn_bits(jnp.concatenate(got, axis=0)), "dp")

    dense_rows = natural(cols, width // sp, 0, rows_d).reshape(sp, dp // sp, rows_d, width // sp)
    dense_w = lax.all_to_all(dense_rows, "sp", split_axis=0, concat_axis=0, tiled=True)
    dense_w = dense_w.transpose(1, 0, 2, 3).reshape(heads * HD, width)
    small = natural(0, sp * LANES, rows_d, 8).reshape(dp, 8, sp, LANES).astype(F32)

    def whole(index):
        return small[:, index, :, : sizes[index]].reshape(-1)

    joined_add = lax.dynamic_slice_in_dim(whole(0), me * cols, cols)
    out_add = whole(1) + whole(3)
    expand_add = lax.dynamic_index_in_dim(small[:, 2], me, 1, keepdims=False)[:, : sizes[2]]

    def stacked(vectors):
        vectors = [jnp.pad(v.reshape(-1), (0, width - v.size)) for v in vectors]
        return jnp.stack(vectors + [jnp.zeros((width,), F32)] * (8 - len(vectors)))

    starts = (jnp.asarray(sp_order, jnp.int32) ^ me) * local_len
    pos = (starts[:, None] + jnp.arange(local_len, dtype=jnp.int32)).reshape(-1)
    lane = jnp.arange(LANES, dtype=jnp.int32) % (ROT // 2)
    freq = 1.0 / 10000.0 ** ((2 * lane).astype(F32) / ROT)
    angles = pos.astype(F32)[:, None] * freq[None, :]
    joined_row = jnp.pad(joined_add, (0, wide - cols))[None]
    ap, ea, joined_g, dense_g, a_sums, j_sums = attention(
        ids,
        xs,
        cots,
        joined_w,
        dense_w,
        stacked([whole(4), whole(5)]),
        joined_row,
        (jnp.cos(angles), jnp.sin(angles)),
        (pos[:, None], pos[None, :]),
        seqs,
        heads,
    )
    dense_g = dense_g.reshape(dp // sp, sp, row_n, width).transpose(1, 0, 2, 3)
    dense_g = dense_g.reshape(heads * HD, width)
    dense_g = lax.all_to_all(dense_g, "sp", split_axis=0, concat_axis=0, tiled=True)
    dense_g = jnp.pad(dense_g.reshape(dp, row_n, width), ((0, 0), (0, -row_n % 8), (0, 0)))
    expand_g, shrink_g, keep, send, m_sums = feed_forward(
        ids,
        xs,
        cots,
        expand_w,
        shrink_w,
        ap,
        ea,
        stacked([whole(6), whole(7), expand_add]),
        dense_g,
    )

    got = swap(send, "sp", 1)
    parts = keep.astype(F32) + got.astype(F32)
    for bit in bits_of(sp)[1:]:
        half = parts.shape[0] // 2
        got = swap(parts[half:].astype(BF), "sp", bit)
        parts = parts[:half] + got.astype(F32)
    out_sum, scaled = parts[0, 0], parts[0, 1]
    rows = inputs.reshape(local, width).astype(F32)
    output = (rows + out_sum + out_add).astype(BF).reshape(inputs.shape)
    own_normed, own_inv = layer_norm(rows)
    first = jnp.mean(scaled, axis=-1, keepdims=True)
    second = jnp.mean(scaled * own_normed, axis=-1, keepdims=True)
    cot_f = cotangent.reshape(local, width).astype(F32)
    input_grad = cot_f + own_inv * (scaled - first - own_normed * second)
    input_grad = input_grad.reshape(inputs.shape)

    joined_b_all = lax.dynamic_update_slice_in_dim(
        jnp.zeros((cols * sp,), F32), j_sums[0, :cols], me * cols, 0
    )
    mine = (jnp.arange(sp, dtype=jnp.int32) == me)[None, :, None]
    expand_b_all = jnp.where(mine, m_sums[0, :units].reshape(dp, 1, ff_n), 0.0)

    def split(vector):
        vector = vector.reshape(dp, sp, -1)
        return jnp.pad(vector, ((0, 0), (0, 0), (0, LANES - vector.shape[2])))

    vectors = [joined_b_all, expand_b_all, jnp.sum(cot_f, axis=0)]
    vectors += [a_sums[0], a_sums[1], m_sums[1], m_sums[2]]
    small_g = jnp.stack([split(v) for v in vectors] + [jnp.zeros((dp, sp, LANES), F32)], axis=1)
    small_g = turn_bits(flip_bits(small_g, "dp")).reshape(dp, 8, sp * LANES)
    small_g = jnp.pad(small_g, ((0, 0), (0, 0), (0, width - sp * LANES))).astype(BF)
    small_at = shrink_g.shape[1] - 8
    shrink_g = lax.dynamic_update_slice(shrink_g, small_g, (0, small_at, 0))

    joined_g = cube_scatter(joined_g, "dp", BF)[0, :, :cols].astype(BF)
    joined_g = lax.all_to_all(joined_g, "sp", split_axis=0, concat_axis=1, tiled=True)
    expand_g = cube_scatter(expand_g, "dp", BF)[0].astype(BF)
    expand_g = lax.all_to_all(expand_g, "sp", split_axis=0, concat_axis=1, tiled=True)
    expand_g = expand_g.reshape(row_n, sp, dp, ff_n).transpose(0, 2, 1, 3).reshape(row_n, -1)
    shrink_g = cube_scatter(shrink_g, "dp", BF)[0]
    small_g = shrink_g[small_at:, : sp * LANES].reshape(8, sp, LANES).transpose(1, 0, 2)
    small_g = cube_scatter(turn_bits(flip_bits(small_g, "sp")), "sp", F32)[0]
    names = [0, 2, 1, 4, 5, 6, 7]
    pieces = [small_g[i, : sizes[name]] for i, name in enumerate(names)]
    joined_bg, expand_bg, out_bg, gain_ag, shift_ag, gain_bg, shift_bg = pieces
    return (
        output,
        input_grad,
        joined_g.astype(F32),
        joined_bg,
        shrink_g[ff_n : ff_n + row_n],
        out_bg,
        expand_g.astype(F32),
        expand_bg,
        shrink_g[:ff_n],
        out_bg,
        gain_ag,
        shift_ag,
        gain_bg,
        shift_bg,
    )


def solution(mesh):
    token = P("dp", "sp", None)
    matrix = P(("dp", "sp"), None)
    vector = P(("dp", "sp"))
    params = (matrix, vector) * 4 + (vector,) * 4
    return jax.shard_map(
        on_device,
        mesh=mesh,
        in_specs=(token, token) + params,
        out_specs=(token, token) + params,
        check_vma=False,
    )
```

profile of v0, /device:TPU:0, one launch (start us, length us, event | category | flops | bytes accessed | tf_op | source)
XLA Modules:
  0.0 235.7 jit_solution(1055715551180694493)
XLA Ops:
  6.0 1.9 concatenate.41.refs_0_
  8.0 3.1 %collective-permute-start = (bf16[264,768]{1,0:T(8,128)(2,1)S(1)}, bf16[264,768]{1,0:T(8,128)(2,1)S(1)}, u32[]{:S(2)}, u32[]{:S(2)}) collective-permute-start(bf16[264,768]{1,0:T(8,128)(2,1)S(1)} %concatenate.41.refs_0_), channel_id=1, source_target_pairs={{0,2},{1,3},{2,0},{3,1},{4,6},{5,7},{6,4},{7,5},{8,10},{9,11},{10,... | collective-permute-start | bytes 1216520 | tf_op jit(solution)/shard_map/ppermute | solution.py:39
  11.6 1.1 reshape.316
  13.9 3.5 %all-to-all-start = ((bf16[4,48,768]{2,1,0:T(8,128)(2,1)}), bf16[4,48,768]{2,1,0:T(8,128)(2,1)S(1)}, u32[]{:S(2)}, u32[]{:S(2)}) async-start(bf16[4,48,768]{2,1,0:T(8,128)(2,1)} %fusion.11), calls=%async_computation | async-start | bytes 589824 | tf_op jit(solution)/shard_map/all_to_all | solution.py:457
  17.3 2.9 %collective-permute-start.9 = (bf16[1,96,768]{2,1,0:T(8,128)(2,1)S(1)}, bf16[1,96,768]{2,1,0:T(8,128)(2,1)S(1)}, u32[]{:S(2)}, u32[]{:S(2)}) collective-permute-start(bf16[1,96,768]{2,1,0:T(8,128)(2,1)S(1)} %bitcast.164), channel_id=1, source_target_pairs={{0,16},{4,20},{8,24},{12,28},{16,0},{20,4},{24,8},{28,12},{1,17},{... | collective-permute-start | bytes 442376 | tf_op jit(solution)/shard_map/ppermute | solution.py:39
  20.4 11.6 %all-to-all-done = bf16[4,48,768]{2,1,0:T(8,128)(2,1)S(1)} async-done(((bf16[4,48,768]{2,1,0:T(8,128)(2,1)}), bf16[4,48,768]{2,1,0:T(8,128)(2,1)S(1)}, u32[]{:S(2)}, u32[]{:S(2)}) %all-to-all-start) | async-done | bytes 294944 | tf_op jit(solution)/shard_map/all_to_all | solution.py:457
  32.2 1.7 collective-permute-done.2.refs_3_
  34.1 2.9 %collective-permute-start.12 = (bf16[1,104,768]{2,1,0:T(8,128)(2,1)S(1)}, bf16[1,104,768]{2,1,0:T(8,128)(2,1)S(1)}, u32[]{:S(2)}, u32[]{:S(2)}) collective-permute-start(bf16[1,104,768]{2,1,0:T(8,128)(2,1)S(1)} %fusion.15), channel_id=1, source_target_pairs={{0,16},{4,20},{8,24},{12,28},{16,0},{20,4},{24,8},{28,12},{1,17},{... | collective-permute-start | bytes 479240 | tf_op jit(solution)/shard_map/ppermute | solution.py:39
  37.0 7.8 %collective-permute-done.12 = bf16[1,104,768]{2,1,0:T(8,128)(2,1)S(1)} collective-permute-done((bf16[1,104,768]{2,1,0:T(8,128)(2,1)S(1)}, bf16[1,104,768]{2,1,0:T(8,128)(2,1)S(1)}, u32[]{:S(2)}, u32[]{:S(2)}) %collective-permute-start.12) | collective-permute-done | bytes 159776 | tf_op jit(solution)/shard_map/ppermute | solution.py:39
  45.6 1.8 multiply_sine_fusion
  47.4 0.9 copy.43.refs_15_
  48.4 3.4 %collective-permute-start.6 = (bf16[1,96,768]{2,1,0:T(8,128)(2,1)S(1)}, bf16[1,96,768]{2,1,0:T(8,128)(2,1)S(1)}, u32[]{:S(2)}, u32[]{:S(2)}) collective-permute-start(bf16[1,96,768]{2,1,0:T(8,128)(2,1)S(1)} %bitcast.160), channel_id=1, source_target_pairs={{0,16},{4,20},{8,24},{12,28},{16,0},{20,4},{24,8},{28,12},{1,17},{... | collective-permute-start | bytes 442376 | tf_op jit(solution)/shard_map/ppermute | solution.py:39
  51.8 5.5 %collective-permute-done.13 = bf16[2,104,768]{2,1,0:T(8,128)(2,1)S(1)} collective-permute-done((bf16[2,104,768]{2,1,0:T(8,128)(2,1)S(1)}, bf16[2,104,768]{2,1,0:T(8,128)(2,1)S(1)}, u32[]{:S(2)}, u32[]{:S(2)}) %collective-permute-start.13) | collective-permute-done | bytes 319520 | tf_op jit(solution)/shard_map/ppermute | solution.py:39
  57.4 2.2 collective-permute-start.14
  59.7 2.1 collective-permute-start.7
  62.3 4.3 %collective-permute-done.10 = bf16[2,96,768]{2,1,0:T(8,128)(2,1)S(1)} collective-permute-done((bf16[2,96,768]{2,1,0:T(8,128)(2,1)S(1)}, bf16[2,96,768]{2,1,0:T(8,128)(2,1)S(1)}, u32[]{:S(2)}, u32[]{:S(2)}) %collective-permute-start.10) | collective-permute-done | bytes 294944 | tf_op jit(solution)/shard_map/ppermute | solution.py:39
  66.7 1.6 collective-permute-start.11
  68.2 1.5 collective-permute-done.7
  69.8 1.6 collective-permute-start.8
  74.5 3.6 %all-to-all-start.1 = ((bf16[4,2,96,192]{3,2,1,0:T(8,128)(2,1)}), bf16[4,2,96,192]{3,2,1,0:T(8,128)(2,1)S(1)}, u32[]{:S(2)}, u32[]{:S(2)}) async-start(bf16[4,2,96,192]{3,2,1,0:T(8,128)(2,1)} %bitcast.22), calls=%async_computation.1 | async-start | bytes 786432 | tf_op jit(solution)/shard_map/all_to_all | solution.py:491
  78.8 6.5 %all-to-all-done.1 = bf16[4,2,96,192]{3,2,1,0:T(8,128)(2,1)S(1)} async-done(((bf16[4,2,96,192]{3,2,1,0:T(8,128)(2,1)}), bf16[4,2,96,192]{3,2,1,0:T(8,128)(2,1)S(1)}, u32[]{:S(2)}, u32[]{:S(2)}) %all-to-all-start.1) | async-done | bytes 294944 | tf_op jit(solution)/shard_map/all_to_all | solution.py:491
  85.3 1.1 reshape.325.refs_10_
  86.5 25.2 %attention_branch.1 = (bf16[4,256,768]{2,1,0:T(8,128)(2,1)}, bf16[4,256,768]{2,1,0:T(8,128)(2,1)}, bf16[8,96,640]{2,1,0:T(8,128)(2,1)}, bf16[192,768]{1,0:T(8,12...) custom-call(s32[8]{0:T(128)} %broadcast_xor_fusion.ids, bf16[264,768]{1,0:T(8,128)(2,1)} %copy-done.11, ...), custom_call_target="tpu_custom_call" | custom-call | flops 6039797760 | bytes 9792032 | tf_op jit(solution)/shard_map/attention_branch/pallas_call | solution.py:330
  111.7 1.7 copy.44
  113.4 3.7 %all-to-all-start.2 = ((bf16[4,48,768]{2,1,0:T(8,128)(2,1)}), bf16[4,48,768]{2,1,0:T(8,128)(2,1)S(1)}, u32[]{:S(2)}, u32[]{:S(2)}) async-start(bf16[4,48,768]{2,1,0:T(8,128)(2,1)} %bitcast.35), calls=%async_computation.2 | async-start | bytes 589824 | tf_op jit(solution)/shard_map/all_to_all | solution.py:527
  118.0 5.1 %all-to-all-done.2 = bf16[4,48,768]{2,1,0:T(8,128)(2,1)S(1)} async-done(((bf16[4,48,768]{2,1,0:T(8,128)(2,1)}), bf16[4,48,768]{2,1,0:T(8,128)(2,1)S(1)}, u32[]{:S(2)}, u32[]{:S(2)}) %all-to-all-start.2) | async-done | bytes 294944 | tf_op jit(solution)/shard_map/all_to_all | solution.py:527
  123.9 18.8 %feed_forward_branch.1 = (bf16[8,96,768]{2,1,0:T(8,128)(2,1)}, bf16[8,128,768]{2,1,0:T(8,128)(2,1)}, bf16[2,2,256,768]{3,2,1,0:T(8,128)(2,1)}, bf16[2,2,256,768]{3,2,1,0:T(8,128)(2,1)}, f32[8,768]{1,0:T(8,128)}) custom-call(s32[8]{0:T(128)} %broadcast_xor_fusion.ids, bf16[264,768]{1,0:T(8,128)(2,1)} %copy-done.11, bf16[264,768]{1,0:T(8,128)(2,1)} %copy-done.31, ...), custom_call_target="tpu_custom_call" | custom-call | flops 7247757312 | bytes 14942240 | tf_op jit(solution)/shard_map/feed_forward_branch/pallas_call | solution.py:330
  146.6 0.8 slice_reduce_fusion.2
  148.3 1.9 slice.230
  150.1 2.1 collective-permute-start.17
  152.8 0.9 slice.260
  153.7 1.5 slice_reduce_fusion
  155.9 1.2 copy-done.2
  157.0 2.2 convert_add_fusion
  159.3 1.0 slice.369
  160.6 4.0 %collective-permute-done.17 = bf16[4,96,640]{2,1,0:T(8,128)(2,1)} collective-permute-done((bf16[4,96,640]{2,1,0:T(8,128)(2,1)}, bf16[4,96,640]{2,1,0:T(8,128)(2,1)}, u32[]{:S(2)}, u32[]{:S(2)}) %collective-permute-start.17) | collective-permute-done | bytes 491552 | tf_op jit(solution)/shard_map/ppermute | solution.py:39
  164.6 1.1 convert_add_fusion.4
  165.8 1.0 copy-done.1
  167.4 2.2 collective-permute-start.18
  173.1 1.3 constant_dynamic-update-slice_fusion.6
  174.4 1.4 collective-permute-done.18
  175.8 1.1 slice_add_fusion.3
  177.7 3.8 %collective-permute-start.19 = (bf16[1,96,640]{2,1,0:T(8,128)(2,1)}, bf16[1,96,640]{2,1,0:T(8,128)(2,1)}, u32[]{:S(2)}, u32[]{:S(2)}) collective-permute-start(bf16[1,96,640]{2,1,0:T(8,128)(2,1)} %slice.375), channel_id=1, source_target_pairs={{0,16},{4,20},{8,24},{12,28},{16,0},{20,4},{24,8},{28,12},{1,17},{... | collective-permute-start | bytes 368648 | tf_op jit(solution)/shard_map/ppermute | solution.py:39
  181.5 1.3 slice_add_fusion
  183.9 1.3 convert_reduce_fusion.1
  186.3 1.2 slice.301
  187.5 1.5 collective-permute-start.20
  189.0 1.2 convert_add_fusion.3
  190.3 1.8 collective-permute-start.26
  192.1 1.6 fusion.13
  193.6 3.3 %all-to-all-start.3 = ((bf16[4,24,576]{2,1,0:T(8,128)(2,1)}), bf16[4,24,576]{2,1,0:T(8,128)(2,1)S(1)}, u32[]{:S(2)}, u32[]{:S(2)}) async-start(bf16[4,24,576]{2,1,0:T(8,128)(2,1)} %bitcast.44), calls=%async_computation.3 | async-start | bytes 245760 | tf_op jit(solution)/shard_map/all_to_all | solution.py:576
  197.5 3.9 %collective-permute-start.27 = (bf16[1,96,768]{2,1,0:T(8,128)(2,1)S(1)}, bf16[1,96,768]{2,1,0:T(8,128)(2,1)}, u32[]{:S(2)}, u32[]{:S(2)}) collective-permute-start(bf16[1,96,768]{2,1,0:T(8,128)(2,1)S(1)} %slice.374), channel_id=1, source_target_pairs={{0,16},{4,20},{8,24},{12,28},{16,0},{20,4},{24,8},{28,12},{1,17},{... | collective-permute-start | bytes 442376 | tf_op jit(solution)/shard_map/ppermute | solution.py:39
  201.5 4.5 %collective-permute-done.20 = bf16[4,128,768]{2,1,0:T(8,128)(2,1)} collective-permute-done((bf16[4,128,768]{2,1,0:T(8,128)(2,1)S(1)}, bf16[4,128,768]{2,1,0:T(8,128)(2,1)}, u32[]{:S(2)}, u32[]{:S(2)}) %collective-permute-start.20) | collective-permute-done | bytes 786464 | tf_op jit(solution)/shard_map/ppermute | solution.py:39
  206.0 1.5 convert_add_fusion.1
  207.6 1.5 collective-permute-start.21
  209.2 0.9 reshape.334
  210.1 1.6 fusion.12
  211.7 3.3 %all-to-all-start.4 = ((bf16[4,24,768]{2,1,0:T(8,128)(2,1)}), bf16[4,24,768]{2,1,0:T(8,128)(2,1)S(1)}, u32[]{:S(2)}, u32[]{:S(2)}) async-start(bf16[4,24,768]{2,1,0:T(8,128)(2,1)} %bitcast.72), calls=%async_computation.4 | async-start | bytes 294912 | tf_op jit(solution)/shard_map/all_to_all | solution.py:578
  215.0 1.6 collective-permute-done.21
  216.7 4.1 %collective-permute-start.22 = (bf16[1,128,768]{2,1,0:T(8,128)(2,1)S(1)}, bf16[1,128,768]{2,1,0:T(8,128)(2,1)S(1)}, u32[]{:S(2)}, u32[]{:S(2)}) collective-permute-start(bf16[1,128,768]{2,1,0:T(8,128)(2,1)S(1)} %slice.373), channel_id=1, source_target_pairs={{0,16},{4,20},{8,24},{12,28},{16,0},{20,4},{24,8},{28,12},{1,17},{... | collective-permute-start | bytes 589832 | tf_op jit(solution)/shard_map/ppermute | solution.py:39
  221.3 1.1 reshape.335
  222.4 6.3 %collective-permute-done.22 = bf16[1,128,768]{2,1,0:T(8,128)(2,1)S(1)} collective-permute-done((bf16[1,128,768]{2,1,0:T(8,128)(2,1)S(1)}, bf16[1,128,768]{2,1,0:T(8,128)(2,1)S(1)}, u32[]{:S(2)}, u32[]{:S(2)}) %collective-permute-start.22) | collective-permute-done | bytes 196640 | tf_op jit(solution)/shard_map/ppermute | solution.py:39
  230.0 1.1 collective-permute-start.24
  231.8 1.9 collective-permute-done.24
  (249 shorter events, 33.0 us)
Async XLA Ops:
  0.6 12.3 %copy-start.14 = (bf16[24,2304]{1,0:T(8,128)(2,1)S(1)}, bf16[24,2304]{1,0:T(8,128)(2,1)}, u32[]{:S(2)}) copy-start(bf16[24,2304]{1,0:T(8,128)(2,1)} %param.18) | copy-start | bytes 331780
  6.0 11.3 %copy-start.8 = (bf16[96,768]{1,0:T(8,128)(2,1)S(1)}, bf16[96,768]{1,0:T(8,128)(2,1)}, u32[]{:S(2)}) copy-start(bf16[96,768]{1,0:T(8,128)(2,1)} %param.24) | copy-start | bytes 442372
  8.0 25.9 %copy-start.11 = (bf16[264,768]{1,0:T(8,128)(2,1)}, bf16[264,768]{1,0:T(8,128)(2,1)S(1)}, u32[]{:S(2)}) copy-start(bf16[264,768]{1,0:T(8,128)(2,1)S(1)} %concatenate.41.refs_0_) | copy-start | bytes 1216516
  8.0 12.3 %copy-start.17 = (bf16[24,768]{1,0:T(8,128)(2,1)S(1)}, bf16[24,768]{1,0:T(8,128)(2,1)}, u32[]{:S(2)}) copy-start(bf16[24,768]{1,0:T(8,128)(2,1)} %param.20) | copy-start | bytes 110596
  8.0 12.4 %copy-start.35 = (s32[4]{0:T(128)S(1)}, s32[4]{0:T(128)}, u32[]{:S(2)}) copy-start(s32[4]{0:T(128)} %constant.76.clone) | copy-start | bytes 52
  8.0 24.0 %collective-permute-start = (bf16[264,768]{1,0:T(8,128)(2,1)S(1)}, bf16[264,768]{1,0:T(8,128)(2,1)S(1)}, u32[]{:S(2)}, u32[]{:S(2)}) collective-permute-start(bf16[264,768]{1,0:T(8,128)(2,1)S(1)} %concatenate.41.refs_0_), channel_id=1, source_target_pairs={{0,2},{1,3},{2,0},{3,1},{4,6},{5,7},{6,4},{7,5},{8,10},{9,11},{10,... | collective-permute-start | bytes 1216520 | tf_op jit(solution)/shard_map/ppermute | solution.py:39
  11.1 21.1 %collective-permute-start.1 = (bf16[264,768]{1,0:T(8,128)(2,1)S(1)}, bf16[264,768]{1,0:T(8,128)(2,1)S(1)}, u32[]{:S(2)}, u32[]{:S(2)}) collective-permute-start(bf16[264,768]{1,0:T(8,128)(2,1)S(1)} %concatenate.41.refs_0_), channel_id=1, source_target_pairs={{0,1},{1,0},{2,3},{3,2},{4,5},{5,4},{6,7},{7,6},{8,9},{9,8},{10,11... | collective-permute-start | bytes 1216520 | tf_op jit(solution)/shard_map/ppermute | solution.py:39
  11.1 51.2 %collective-permute-start.3 = (bf16[256,768]{1,0:T(8,128)(2,1)}, bf16[256,768]{1,0:T(8,128)(2,1)}, u32[]{:S(2)}, u32[]{:S(2)}) collective-permute-start(bf16[256,768]{1,0:T(8,128)(2,1)} %bitcast.169), channel_id=1, source_target_pairs={{0,2},{1,3},{2,0},{3,1},{4,6},{5,7},{6,4},{7,5},{8,10},{9,11},{10,... | collective-permute-start | bytes 1179656 | tf_op jit(solution)/shard_map/ppermute | solution.py:39
  11.2 75.2 %collective-permute-start.4 = (bf16[256,768]{1,0:T(8,128)(2,1)}, bf16[256,768]{1,0:T(8,128)(2,1)}, u32[]{:S(2)}, u32[]{:S(2)}) collective-permute-start(bf16[256,768]{1,0:T(8,128)(2,1)} %bitcast.170), channel_id=1, source_target_pairs={{0,1},{1,0},{2,3},{3,2},{4,5},{5,4},{6,7},{7,6},{8,9},{9,8},{10,11... | collective-permute-start | bytes 1179656 | tf_op jit(solution)/shard_map/ppermute | solution.py:39
  13.9 18.2 %all-to-all-start = ((bf16[4,48,768]{2,1,0:T(8,128)(2,1)}), bf16[4,48,768]{2,1,0:T(8,128)(2,1)S(1)}, u32[]{:S(2)}, u32[]{:S(2)}) async-start(bf16[4,48,768]{2,1,0:T(8,128)(2,1)} %fusion.11), calls=%async_computation | async-start | bytes 589824 | tf_op jit(solution)/shard_map/all_to_all | solution.py:457
  17.3 42.2 %collective-permute-start.9 = (bf16[1,96,768]{2,1,0:T(8,128)(2,1)S(1)}, bf16[1,96,768]{2,1,0:T(8,128)(2,1)S(1)}, u32[]{:S(2)}, u32[]{:S(2)}) collective-permute-start(bf16[1,96,768]{2,1,0:T(8,128)(2,1)S(1)} %bitcast.164), channel_id=1, source_target_pairs={{0,16},{4,20},{8,24},{12,28},{16,0},{20,4},{24,8},{28,12},{1,17},{... | collective-permute-start | bytes 442376 | tf_op jit(solution)/shard_map/ppermute | solution.py:39
  32.1 2.0 copy-start.31
  32.1 1.8 collective-permute-start.2
  32.2 12.6 %copy-start.32 = (bf16[264,768]{1,0:T(8,128)(2,1)}, bf16[264,768]{1,0:T(8,128)(2,1)S(1)}, u32[]{:S(2)}) copy-start(bf16[264,768]{1,0:T(8,128)(2,1)S(1)} %collective-permute-done.1.refs_2_) | copy-start | bytes 1216516
  33.9 23.4 %copy-start.33 = (bf16[264,768]{1,0:T(8,128)(2,1)}, bf16[264,768]{1,0:T(8,128)(2,1)S(1)}, u32[]{:S(2)}) copy-start(bf16[264,768]{1,0:T(8,128)(2,1)S(1)} %collective-permute-done.2.refs_3_) | copy-start | bytes 1216516
  34.1 10.7 %collective-permute-start.12 = (bf16[1,104,768]{2,1,0:T(8,128)(2,1)S(1)}, bf16[1,104,768]{2,1,0:T(8,128)(2,1)S(1)}, u32[]{:S(2)}, u32[]{:S(2)}) collective-permute-start(bf16[1,104,768]{2,1,0:T(8,128)(2,1)S(1)} %fusion.15), channel_id=1, source_target_pairs={{0,16},{4,20},{8,24},{12,28},{16,0},{20,4},{24,8},{28,12},{1,17},{... | collective-permute-start | bytes 479240 | tf_op jit(solution)/shard_map/ppermute | solution.py:39
  37.0 22.6 %copy-start.24 = (s32[4,128]{1,0:T(4,128)}, s32[4,128]{1,0:T(4,128)S(1)}, u32[]{:S(2)}) copy-start(s32[4,128]{1,0:T(4,128)S(1)} %get-tuple-element.63) | copy-start | bytes 6148
  44.8 12.5 %collective-permute-start.13 = (bf16[2,104,768]{2,1,0:T(8,128)(2,1)S(1)}, bf16[2,104,768]{2,1,0:T(8,128)(2,1)S(1)}, u32[]{:S(2)}, u32[]{:S(2)}) collective-permute-start(bf16[2,104,768]{2,1,0:T(8,128)(2,1)S(1)} %pad_maximum_fusion.4), channel_id=1, source_target_pairs={{0,8},{4,12},{8,0},{12,4},{16,24},{20,28},{24,16},{28,20},{1,9},{5... | collective-permute-start | bytes 958472 | tf_op jit(solution)/shard_map/ppermute | solution.py:39
  47.4 14.4 %copy-start.34 = (s32[8]{0:T(128)S(1)}, s32[8]{0:T(128)}, u32[]{:S(2)}) copy-start(s32[8]{0:T(128)} %constant.75.clone) | copy-start | bytes 100
  48.4 11.3 %collective-permute-start.6 = (bf16[1,96,768]{2,1,0:T(8,128)(2,1)S(1)}, bf16[1,96,768]{2,1,0:T(8,128)(2,1)S(1)}, u32[]{:S(2)}, u32[]{:S(2)}) collective-permute-start(bf16[1,96,768]{2,1,0:T(8,128)(2,1)S(1)} %bitcast.160), channel_id=1, source_target_pairs={{0,16},{4,20},{8,24},{12,28},{16,0},{20,4},{24,8},{28,12},{1,17},{... | collective-permute-start | bytes 442376 | tf_op jit(solution)/shard_map/ppermute | solution.py:39
  57.3 14.0 %copy-start.4 = (bf16[4,104,768]{2,1,0:T(8,128)(2,1)}, bf16[4,104,768]{2,1,0:T(8,128)(2,1)S(1)}, u32[]{:S(2)}) copy-start(bf16[4,104,768]{2,1,0:T(8,128)(2,1)S(1)} %pad_maximum_fusion.refs_8_) | copy-start | bytes 1916932
  57.4 14.7 %collective-permute-start.14 = (bf16[4,104,768]{2,1,0:T(8,128)(2,1)S(1)}, bf16[4,104,768]{2,1,0:T(8,128)(2,1)S(1)}, u32[]{:S(2)}, u32[]{:S(2)}) collective-permute-start(bf16[4,104,768]{2,1,0:T(8,128)(2,1)S(1)} %pad_maximum_fusion.refs_8_), channel_id=1, source_target_pairs={{0,4},{4,0},{8,12},{12,8},{16,20},{20,16},{24,28},{28,24},{1,5},{5... | collective-permute-start | bytes 1916936 | tf_op jit(solution)/shard_map/ppermute | solution.py:39
  59.6 7.0 %collective-permute-start.10 = (bf16[2,96,768]{2,1,0:T(8,128)(2,1)S(1)}, bf16[2,96,768]{2,1,0:T(8,128)(2,1)S(1)}, u32[]{:S(2)}, u32[]{:S(2)}) collective-permute-start(bf16[2,96,768]{2,1,0:T(8,128)(2,1)S(1)} %pad_maximum_fusion.6), channel_id=1, source_target_pairs={{0,8},{4,12},{8,0},{12,4},{16,24},{20,28},{24,16},{28,20},{1,9},{5... | collective-permute-start | bytes 884744 | tf_op jit(solution)/shard_map/ppermute | solution.py:39
  59.7 10.0 %collective-permute-start.7 = (bf16[2,96,768]{2,1,0:T(8,128)(2,1)S(1)}, bf16[2,96,768]{2,1,0:T(8,128)(2,1)S(1)}, u32[]{:S(2)}, u32[]{:S(2)}) collective-permute-start(bf16[2,96,768]{2,1,0:T(8,128)(2,1)S(1)} %pad_maximum_fusion.5), channel_id=1, source_target_pairs={{0,8},{4,12},{8,0},{12,4},{16,24},{20,28},{24,16},{28,20},{1,9},{5... | collective-permute-start | bytes 884744 | tf_op jit(solution)/shard_map/ppermute | solution.py:39
  62.3 24.1 %collective-permute-start.5 = (bf16[256,768]{1,0:T(8,128)(2,1)}, bf16[256,768]{1,0:T(8,128)(2,1)}, u32[]{:S(2)}, u32[]{:S(2)}) collective-permute-start(bf16[256,768]{1,0:T(8,128)(2,1)} %collective-permute-done.3.refs_5_), channel_id=1, source_target_pairs={{0,1},{1,0},{2,3},{3,2},{4,5},{5,4},{6,7},{7,6},{8,9},{9,8},{10,11... | collective-permute-start | bytes 1179656 | tf_op jit(solution)/shard_map/ppermute | solution.py:39
  66.7 6.7 %copy-start.9 = (bf16[4,96,768]{2,1,0:T(8,128)(2,1)}, bf16[4,96,768]{2,1,0:T(8,128)(2,1)S(1)}, u32[]{:S(2)}) copy-start(bf16[4,96,768]{2,1,0:T(8,128)(2,1)S(1)} %pad_maximum_fusion.2.refs_10_) | copy-start | bytes 1769476
  66.7 51.3 %collective-permute-start.11 = (bf16[4,96,768]{2,1,0:T(8,128)(2,1)S(1)}, bf16[4,96,768]{2,1,0:T(8,128)(2,1)}, u32[]{:S(2)}, u32[]{:S(2)}) collective-permute-start(bf16[4,96,768]{2,1,0:T(8,128)(2,1)S(1)} %pad_maximum_fusion.2.refs_10_), channel_id=1, source_target_pairs={{0,4},{4,0},{8,12},{12,8},{16,20},{20,16},{24,28},{28,24},{1,5},{5... | collective-permute-start | bytes 1769480 | tf_op jit(solution)/shard_map/ppermute | solution.py:39
  69.8 3.7 %copy-start.10 = (bf16[4,96,768]{2,1,0:T(8,128)(2,1)}, bf16[4,96,768]{2,1,0:T(8,128)(2,1)S(1)}, u32[]{:S(2)}) copy-start(bf16[4,96,768]{2,1,0:T(8,128)(2,1)S(1)} %pad_maximum_fusion.1.refs_8_) | copy-start | bytes 1769476
  69.8 48.2 %collective-permute-start.8 = (bf16[4,96,768]{2,1,0:T(8,128)(2,1)S(1)}, bf16[4,96,768]{2,1,0:T(8,128)(2,1)}, u32[]{:S(2)}, u32[]{:S(2)}) collective-permute-start(bf16[4,96,768]{2,1,0:T(8,128)(2,1)S(1)} %pad_maximum_fusion.1.refs_8_), channel_id=1, source_target_pairs={{0,4},{4,0},{8,12},{12,8},{16,20},{20,16},{24,28},{28,24},{1,5},{5... | collective-permute-start | bytes 1769480 | tf_op jit(solution)/shard_map/ppermute | solution.py:39
  72.0 1.5 copy-start.16
  74.5 10.8 %all-to-all-start.1 = ((bf16[4,2,96,192]{3,2,1,0:T(8,128)(2,1)}), bf16[4,2,96,192]{3,2,1,0:T(8,128)(2,1)S(1)}, u32[]{:S(2)}, u32[]{:S(2)}) async-start(bf16[4,2,96,192]{3,2,1,0:T(8,128)(2,1)} %bitcast.22), calls=%async_computation.1 | async-start | bytes 786432 | tf_op jit(solution)/shard_map/all_to_all | solution.py:491
  113.4 9.8 %all-to-all-start.2 = ((bf16[4,48,768]{2,1,0:T(8,128)(2,1)}), bf16[4,48,768]{2,1,0:T(8,128)(2,1)S(1)}, u32[]{:S(2)}, u32[]{:S(2)}) async-start(bf16[4,48,768]{2,1,0:T(8,128)(2,1)} %bitcast.35), calls=%async_computation.2 | async-start | bytes 589824 | tf_op jit(solution)/shard_map/all_to_all | solution.py:527
  123.9 19.4 %copy-start = (bf16[2,128,768]{2,1,0:T(8,128)(2,1)S(1)}, bf16[2,128,768]{2,1,0:T(8,128)(2,1)}, u32[]{:S(2)}) copy-start(bf16[2,128,768]{2,1,0:T(8,128)(2,1)} %param.16) | copy-start | bytes 1179652
  142.6 10.2 %copy-start.5 = (bf16[8,96,768]{2,1,0:T(8,128)(2,1)S(1)}, bf16[8,96,768]{2,1,0:T(8,128)(2,1)}, u32[]{:S(2)}) copy-start(bf16[8,96,768]{2,1,0:T(8,128)(2,1)} %get-tuple-element.35) | copy-start | bytes 3538948
  142.6 13.2 %collective-permute-start.15 = (bf16[2,2,256,768]{3,2,1,0:T(8,128)(2,1)}, bf16[2,2,256,768]{3,2,1,0:T(8,128)(2,1)S(1)}, u32[]{:S(2)}, u32[]{:S(2)}) collective-permute-start(bf16[2,2,256,768]{3,2,1,0:T(8,128)(2,1)} %get-tuple-element.29), channel_id=1, source_target_pairs={{0,1},{1,0},{2,3},{3,2},{4,5},{5,4},{6,7},{7,6},{8,9},{9,8},{10,11... | collective-permute-start | bytes 4718600 | tf_op jit(solution)/shard_map/ppermute | solution.py:39
  144.0 2.3 copy-start.22
  150.1 14.5 %collective-permute-start.17 = (bf16[4,96,640]{2,1,0:T(8,128)(2,1)}, bf16[4,96,640]{2,1,0:T(8,128)(2,1)}, u32[]{:S(2)}, u32[]{:S(2)}) collective-permute-start(bf16[4,96,640]{2,1,0:T(8,128)(2,1)} %slice.230), channel_id=1, source_target_pairs={{0,4},{4,0},{8,12},{12,8},{16,20},{20,16},{24,28},{28,24},{1,5},{5... | collective-permute-start | bytes 1474568 | tf_op jit(solution)/shard_map/ppermute | solution.py:39
  153.7 35.3 %collective-permute-start.25 = (bf16[4,96,768]{2,1,0:T(8,128)(2,1)}, bf16[4,96,768]{2,1,0:T(8,128)(2,1)}, u32[]{:S(2)}, u32[]{:S(2)}) collective-permute-start(bf16[4,96,768]{2,1,0:T(8,128)(2,1)} %slice.260), channel_id=1, source_target_pairs={{0,4},{4,0},{8,12},{12,8},{16,20},{20,16},{24,28},{28,24},{1,5},{5... | collective-permute-start | bytes 1769480 | tf_op jit(solution)/shard_map/ppermute | solution.py:39
  155.9 1.2 copy-start.2
  159.3 5.4 %copy-start.7 = (bf16[8,96,640]{2,1,0:T(8,128)(2,1)S(1)}, bf16[8,96,640]{2,1,0:T(8,128)(2,1)}, u32[]{:S(2)}) copy-start(bf16[8,96,640]{2,1,0:T(8,128)(2,1)} %get-tuple-element.30) | copy-start | bytes 2949124
  160.2 9.5 %copy-start.25 = (bf16[8,96]{1,0:T(8,128)(2,1)S(1)}, bf16[8,96]{1,0:T(8,128)(2,1)}, u32[]{:S(2)}) copy-start(bf16[8,96]{1,0:T(8,128)(2,1)} %broadcast_in_dim.49) | copy-start | bytes 4612
  160.2 9.5 %copy-start.30 = (pred[4]{0:T(512)(128)(4,1)S(1)}, pred[4]{0:T(512)(128)(4,1)}, u32[]{:S(2)}) copy-start(pred[4]{0:T(512)(128)(4,1)} %iota_compare_fusion.2) | copy-start | bytes 16
  160.2 21.3 %collective-permute-start.16 = (bf16[1,2,256,768]{3,2,1,0:T(8,128)(2,1)}, bf16[1,2,256,768]{3,2,1,0:T(8,128)(2,1)}, u32[]{:S(2)}, u32[]{:S(2)}) collective-permute-start(bf16[1,2,256,768]{3,2,1,0:T(8,128)(2,1)} %slice.369), channel_id=1, source_target_pairs={{0,2},{1,3},{2,0},{3,1},{4,6},{5,7},{6,4},{7,5},{8,10},{9,11},{10,... | collective-permute-start | bytes 2359304 | tf_op jit(solution)/shard_map/ppermute | solution.py:39
  167.4 8.4 %collective-permute-start.18 = (bf16[2,96,640]{2,1,0:T(8,128)(2,1)}, bf16[2,96,640]{2,1,0:T(8,128)(2,1)}, u32[]{:S(2)}, u32[]{:S(2)}) collective-permute-start(bf16[2,96,640]{2,1,0:T(8,128)(2,1)} %slice.372), channel_id=1, source_target_pairs={{0,8},{4,12},{8,0},{12,4},{16,24},{20,28},{24,16},{28,20},{1,9},{5... | collective-permute-start | bytes 737288 | tf_op jit(solution)/shard_map/ppermute | solution.py:39
  177.0 4.6 %copy-start.3 = (f32[2,96,640]{2,1,0:T(8,128)}, f32[2,96,640]{2,1,0:T(8,128)S(1)}, u32[]{:S(2)}) copy-start(f32[2,96,640]{2,1,0:T(8,128)S(1)} %slice_add_fusion.3) | copy-start | bytes 1474564
  177.7 14.4 %collective-permute-start.19 = (bf16[1,96,640]{2,1,0:T(8,128)(2,1)}, bf16[1,96,640]{2,1,0:T(8,128)(2,1)}, u32[]{:S(2)}, u32[]{:S(2)}) collective-permute-start(bf16[1,96,640]{2,1,0:T(8,128)(2,1)} %slice.375), channel_id=1, source_target_pairs={{0,16},{4,20},{8,24},{12,28},{16,0},{20,4},{24,8},{28,12},{1,17},{... | collective-permute-start | bytes 368648 | tf_op jit(solution)/shard_map/ppermute | solution.py:39
  182.9 1.0 copy-start.12
  182.9 1.0 copy-start.21
  183.9 1.5 copy-start.15
  183.9 1.5 copy-start.18
  183.9 1.5 copy-start.19
  183.9 1.6 copy-start.20
  185.2 3.8 %copy-start.6 = (bf16[8,96,768]{2,1,0:T(8,128)(2,1)S(1)}, bf16[8,96,768]{2,1,0:T(8,128)(2,1)}, u32[]{:S(2)}) copy-start(bf16[8,96,768]{2,1,0:T(8,128)(2,1)} %get-tuple-element.35) | copy-start | bytes 3538948
  187.5 4.6 %slice-start = ((f32[2,96,640]{2,1,0:T(8,128)}), f32[1,96,640]{2,1,0:T(8,128)S(1)}, s32[]{:S(2)}) async-start(f32[2,96,640]{2,1,0:T(8,128)} %copy-done.3), calls=%async_computation.5 | async-start | bytes 491520 | tf_op jit(solution)/shard_map/slice | solution.py:61
  187.5 18.5 %collective-permute-start.20 = (bf16[4,128,768]{2,1,0:T(8,128)(2,1)S(1)}, bf16[4,128,768]{2,1,0:T(8,128)(2,1)}, u32[]{:S(2)}, u32[]{:S(2)}) collective-permute-start(bf16[4,128,768]{2,1,0:T(8,128)(2,1)S(1)} %slice.301), channel_id=1, source_target_pairs={{0,4},{4,0},{8,12},{12,8},{16,20},{20,16},{24,28},{28,24},{1,5},{5... | collective-permute-start | bytes 2359304 | tf_op jit(solution)/shard_map/ppermute | solution.py:39
  190.3 7.2 %collective-permute-start.26 = (bf16[2,96,768]{2,1,0:T(8,128)(2,1)S(1)}, bf16[2,96,768]{2,1,0:T(8,128)(2,1)S(1)}, u32[]{:S(2)}, u32[]{:S(2)}) collective-permute-start(bf16[2,96,768]{2,1,0:T(8,128)(2,1)S(1)} %slice.371), channel_id=1, source_target_pairs={{0,8},{4,12},{8,0},{12,4},{16,24},{20,28},{24,16},{28,20},{1,9},{5... | collective-permute-start | bytes 884744 | tf_op jit(solution)/shard_map/ppermute | solution.py:39
  193.6 15.4 %all-to-all-start.3 = ((bf16[4,24,576]{2,1,0:T(8,128)(2,1)}), bf16[4,24,576]{2,1,0:T(8,128)(2,1)S(1)}, u32[]{:S(2)}, u32[]{:S(2)}) async-start(bf16[4,24,576]{2,1,0:T(8,128)(2,1)} %bitcast.44), calls=%async_computation.3 | async-start | bytes 245760 | tf_op jit(solution)/shard_map/all_to_all | solution.py:576
  197.5 12.5 %collective-permute-start.27 = (bf16[1,96,768]{2,1,0:T(8,128)(2,1)S(1)}, bf16[1,96,768]{2,1,0:T(8,128)(2,1)}, u32[]{:S(2)}, u32[]{:S(2)}) collective-permute-start(bf16[1,96,768]{2,1,0:T(8,128)(2,1)S(1)} %slice.374), channel_id=1, source_target_pairs={{0,16},{4,20},{8,24},{12,28},{16,0},{20,4},{24,8},{28,12},{1,17},{... | collective-permute-start | bytes 442376 | tf_op jit(solution)/shard_map/ppermute | solution.py:39
  207.6 9.1 %collective-permute-start.21 = (bf16[2,128,768]{2,1,0:T(8,128)(2,1)S(1)}, bf16[2,128,768]{2,1,0:T(8,128)(2,1)S(1)}, u32[]{:S(2)}, u32[]{:S(2)}) collective-permute-start(bf16[2,128,768]{2,1,0:T(8,128)(2,1)S(1)} %slice.370), channel_id=1, source_target_pairs={{0,8},{4,12},{8,0},{12,4},{16,24},{20,28},{24,16},{28,20},{1,9},{5... | collective-permute-start | bytes 1179656 | tf_op jit(solution)/shard_map/ppermute | solution.py:39
  211.7 9.1 %all-to-all-start.4 = ((bf16[4,24,768]{2,1,0:T(8,128)(2,1)}), bf16[4,24,768]{2,1,0:T(8,128)(2,1)S(1)}, u32[]{:S(2)}, u32[]{:S(2)}) async-start(bf16[4,24,768]{2,1,0:T(8,128)(2,1)} %bitcast.72), calls=%async_computation.4 | async-start | bytes 294912 | tf_op jit(solution)/shard_map/all_to_all | solution.py:578
  216.7 12.0 %collective-permute-start.22 = (bf16[1,128,768]{2,1,0:T(8,128)(2,1)S(1)}, bf16[1,128,768]{2,1,0:T(8,128)(2,1)S(1)}, u32[]{:S(2)}, u32[]{:S(2)}) collective-permute-start(bf16[1,128,768]{2,1,0:T(8,128)(2,1)S(1)} %slice.373), channel_id=1, source_target_pairs={{0,16},{4,20},{8,24},{12,28},{16,0},{20,4},{24,8},{28,12},{1,17},{... | collective-permute-start | bytes 589832 | tf_op jit(solution)/shard_map/ppermute | solution.py:39
  228.8 1.2 collective-permute-start.23
  230.0 3.6 %collective-permute-start.24 = (f32[1,8,128]{2,1,0:T(8,128)S(1)}, f32[1,8,128]{2,1,0:T(8,128)S(1)}, u32[]{:S(2)}, u32[]{:S(2)}) collective-permute-start(f32[1,8,128]{2,1,0:T(8,128)S(1)} %slice.310), channel_id=1, source_target_pairs={{0,2},{1,3},{2,0},{3,1},{4,6},{5,7},{6,4},{7,5},{8,10},{9,11},{10,... | collective-permute-start | bytes 12296 | tf_op jit(solution)/shard_map/ppermute | solution.py:39
  234.2 1.5 copy-start.29
  (6 other events, 5.0 us)
where the time goes:
time: 237 us; the launch traced here: 236 us
  waiting for transfers between devices  65.2 us (28%)
  starting transfers between devices  61.2 us (26%)
  Pallas kernels  44 us (19%)
  local copies, waits for them, and re-layouts  42.5 us (18%)
  other arithmetic  21.2 us (9%)
    pallas_call x2, Pallas kernels, call(): pl.pallas_call(body, name=name, in_specs=specs, out_shape=outs, out_specs...  44 us
    ppermute x28, starting transfers between devices, swap(): return lax.ppermute(value, axis, [(i, i ^ bit) for i in range(count)])  43.8 us
    ppermute x28, waiting for transfers between devices, swap(): return lax.ppermute(value, axis, [(i, i ^ bit) for i in range(count)])  41.9 us
    all_to_all x1, waiting for transfers between devices, on_device(): both = lax.all_to_all(both, 'sp', split_axis=0, concat_axis=0, tiled=True)  11.6 us
    all_to_all x1, waiting for transfers between devices, on_device(): lax.all_to_all(dense_rows, 'sp', split_axis=0, concat_axis=0, tiled=True)  6.5 us
    unnamed x80, local copies, waits for them, and re-layouts  5.99 us
    slice x11, local copies, waits for them, and re-layouts, cube_scatter(): got = swap(value[half:].astype(wire), axis, bit)  5.48 us
    pad x8, local copies, waits for them, and re-layouts, on_device(): jnp.pad(part, (0, width - part.shape[0]))  5.31 us
  transfers between devices with their start and end apart: 33, of which 17 were waited for; matrix products, arithmetic and copies ran while one was open for 22% of the time, Pallas kernels for 11%

commit v1 on v0

--- a/solution.py
+++ b/solution.py
@@ -6,6 +6,7 @@
 from jax.experimental import pallas as pl
 from jax.experimental.pallas import tpu as pltpu
 from jax.sharding import PartitionSpec as P
+
 
 HEADS = 12
 HD = 64
@@ -50,16 +51,29 @@
 def token_blocks(block, axis):
     blocks = [block]
     for bit in reversed(bits_of(lax.axis_size(axis))):
-        blocks = blocks + [swap(b, axis, bit) for b in blocks]
+        more = []
+        for b in blocks:
+            more.append(swap(b, axis, bit))
+        blocks = blocks + more
     return blocks
 
 
-def cube_scatter(value, axis, wire):
+def transposed(value, back):
+    dp, sp = lax.axis_size("dp"), lax.axis_size("sp")
+    perm = [(s * dp + b, b * sp + s) for s in range(sp) for b in range(dp)]
+    if back:
+        perm = [(to, at) for at, to in perm]
+    return lax.ppermute(value, ("dp", "sp"), perm)
+
+
+def cube_scatter(keep, send, axis):
     for bit in bits_of(lax.axis_size(axis)):
-        half = value.shape[0] // 2
-        got = swap(value[half:].astype(wire), axis, bit)
-        value = value[:half].astype(F32) + got.astype(F32)
-    return value
+        got = swap(send, axis, bit)
+        half = keep.shape[0] // 2
+        if half:
+            send = (keep[half:].astype(F32) + got[half:].astype(F32)).astype(BF)
+            keep = keep[:half].astype(F32) + got[:half].astype(F32)
+    return keep[0], got[0]
 
 
 def flip_bits(blocks, axis):
@@ -117,11 +131,14 @@
     return out
 
 
-def sent(ids, source, out, rows, sem):
+def sent(ids, source, keep, send, rows, sem):
     todo = []
-    for p in range(out.shape[0]):
+    half = keep.shape[0]
+    for p in range(2 * half):
         at = pl.multiple_of(ids[p] * rows, 8)
-        to = out.at[p] if out.shape[1] == rows else out.at[p, pl.ds(0, rows)]
+        to = keep.at[p] if p < half else send.at[p - half]
+        if to.shape[0] != rows:
+            to = to.at[pl.ds(0, rows)]
         todo.append(pltpu.make_async_copy(source.at[pl.ds(at, rows)], to, sem.at[p]))
     return todo
 
@@ -142,21 +159,21 @@
     @pl.loop(0, left.shape[1] // rows)
     def _(r):
         at = pl.ds(pl.multiple_of(r * rows, rows), rows)
-        out[at, :] = dot(left[:, at], right[...], 0, 0).astype(BF)
+        out[at, : right.shape[1]] = dot(left[:, at], right[...], 0, 0).astype(BF)
 
 
 def mlp_kernel(sp, ids, *refs):
     xs, cots = refs[:sp], refs[sp : 2 * sp]
-    ew_mine, ew_got, sw_mine, sw_got, ap, ea, vec, dense = refs[2 * sp : 2 * sp + 8]
-    eg_out, sg_out, keep, send, sums = refs[2 * sp + 8 : 2 * sp + 13]
-    x, cot, ew, sw, hid, act, pgr, eg, sg, sem = refs[2 * sp + 13 :]
+    ew_mine, ew_got, sw_mine, sw_got, vec = refs[2 * sp : 2 * sp + 5]
+    outs = refs[2 * sp + 5 : 2 * sp + 12]
+    eg_keep, eg_send, sg_keep, sg_send, out_part, in_part, sums = outs
+    x, cot, ew, sw, hid, act, pgr, eg, sg, sem = refs[2 * sp + 12 :]
     width = x.shape[1]
     chunk = x.shape[0] // sp
-    rows = ew_mine.shape[1]
-    units = sw_mine.shape[1]
+    rows, units = eg_keep.shape[1], sg_keep.shape[1]
     gets = (
         copies_in([b.at[pl.ds(0, chunk)] for b in xs], x, chunk, sem.at[0])
-        + copies_in(cots, cot, chunk, sem.at[1])
+        + copies_in([b.at[pl.ds(0, chunk)] for b in cots], cot, chunk, sem.at[1])
         + placed(ids, ew_mine, ew_got, ew, rows, ew.shape[1], sem.at[2])
         + placed(ids, sw_mine, sw_got, sw, units, width, sem.at[3])
     )
@@ -180,30 +197,17 @@
         sums[0:1, : ew.shape[1]] += row_sum(pre_grad)
         pre_grad_bf = pre_grad.astype(BF)
         pgr[at, :] = pre_grad_bf
-        out_part = dot(activated, sw[...], 1, 0) + ap[k].astype(F32)
+        out_part[k] = dot(activated, sw[...], 1, 0).astype(BF)
         hidden_grad = dot(pre_grad_bf, ew[...], 1, 1)
         sums[1:2, :] += row_sum(hidden_grad * normed)
         sums[2:3, :] += row_sum(hidden_grad)
-        scaled = hidden_grad * gain + ea[k].astype(F32)
-
-        @pl.when(k < sp // 2)
-        def _():
-            keep[k, 0] = out_part.astype(BF)
-            keep[k, 1] = scaled.astype(BF)
-
-        @pl.when(k >= sp // 2)
-        def _():
-            send[k - sp // 2, 0] = out_part.astype(BF)
-            send[k - sp // 2, 1] = scaled.astype(BF)
+        in_part[k] = (hidden_grad * gain).astype(BF)
 
     grad_rows(hid, pgr, eg)
-    puts = sent(ids, eg, eg_out, rows, sem.at[0])
+    puts = sent(ids, eg, eg_keep, eg_send, rows, sem.at[0])
     run(puts)
     grad_rows(act, cot, sg)
-    more = sent(ids, sg, sg_out, units, sem.at[1])
-    for p in range(sg_out.shape[0]):
-        to = sg_out.at[p, pl.ds(units, dense.shape[1])]
-        more.append(pltpu.make_async_copy(dense.at[ids[p]], to, sem.at[2, p]))
+    more = sent(ids, sg, sg_keep, sg_send, units, sem.at[1])
     run(more)
     finish(puts + more)
 
@@ -211,24 +215,25 @@
 def attn_kernel(sp, seqs, heads, ids, *refs):
     xs, cots = refs[:sp], refs[sp : 2 * sp]
     jw_mine, jw_got, dw, vec, jadd, cos_ref, sin_ref, posc, posr = refs[2 * sp : 2 * sp + 9]
-    ap, ea, jg_out, dense_g, sums, jsum = refs[2 * sp + 9 : 2 * sp + 15]
-    x, cot, jw, hid, rot, cg, ctx, jgf, jgb, ctk, gr, sem = refs[2 * sp + 15 :]
+    out_part, in_part, m_sums, g_keep, g_send, keep, send = refs[2 * sp + 9 : 2 * sp + 16]
+    x, cot, jw, hid, rot, cg, ctx, jgf, jgb, ctk, gr, sums, small, sem = refs[2 * sp + 16 :]
     width = x.shape[1]
     wide = jw.shape[1]
     cols = heads * 3 * HD
     chunk = x.shape[0] // sp
     part = chunk // seqs
     full = part * sp
-    rows = jg_out.shape[1]
+    half = g_keep.shape[0]
+    rows = width // (2 * half)
+    per = rows // sp
     scale = HD ** (-0.5)
     gets = (
         copies_in([b.at[pl.ds(0, chunk)] for b in xs], x, chunk, sem.at[0])
-        + copies_in(cots, cot, chunk, sem.at[1])
+        + copies_in([b.at[pl.ds(0, chunk)] for b in cots], cot, chunk, sem.at[1])
         + placed(ids, jw_mine, jw_got, jw, rows, wide, sem.at[2])
     )
     run(gets)
     sums[...] = jnp.zeros_like(sums)
-    jsum[...] = jnp.zeros_like(jsum)
     jgf[:, cols:] = jnp.zeros((jgf.shape[0], wide - cols), F32)
     finish(gets)
     gain, shift = vec[0:1, :], vec[1:2, :]
@@ -302,21 +307,45 @@
             lanes = slice(g * LANES, (g + 1) * LANES)
             back = rotate(collect(jgf, k, lanes), g, k, -1.0).astype(BF)
             jgb[at, lanes] = back
-            jsum[0:1, lanes] += row_sum(back.astype(F32))
+            sums[5:6, lanes] += row_sum(back.astype(F32))
         hidden_grad = dot(jgb[at, :], jw[...], 1, 1)
         normed, _ = layer_norm(x[at, :].astype(F32))
         sums[0:1, :] += row_sum(hidden_grad * normed)
         sums[1:2, :] += row_sum(hidden_grad)
-        ea[k] = (hidden_grad * gain).astype(BF)
         context = collect(ctx, k, slice(None))
         ctk[at, :] = context
-        ap[k] = dot(context, dw[...], 1, 0).astype(BF)
-
+        scaled = (hidden_grad * gain + in_part[k].astype(F32)).astype(BF)
+        out_sum = (dot(context, dw[...], 1, 0) + out_part[k].astype(F32)).astype(BF)
+
+        @pl.when(k < sp // 2)
+        def _():
+            keep[k, 0] = out_sum
+            keep[k, 1] = scaled
+
+        @pl.when(k >= sp // 2)
+        def _():
+            send[k - sp // 2, 0] = out_sum
+            send[k - sp // 2, 1] = scaled
+
+    sums[2:4, :] = m_sums[1:3, :]
+    sums[4:5, :] = row_sum(cot[0:chunk, :].astype(F32))
+    sums[6:7, :] = m_sums[0:1, :]
+    small[...] = sums[...].astype(BF)
+    puts = []
+    for p in range(2 * half):
+        to = g_keep.at[p] if p < half else g_send.at[p - half]
+        puts.append(pltpu.make_async_copy(small, to.at[pl.ds(rows, 8)], sem.at[1, p]))
+    run(puts)
     grad_rows(hid, jgb, gr)
-    puts = sent(ids, gr, jg_out, rows, sem.at[0])
-    run(puts)
-    dense_g[...] = dot(ctk[...], cot[...], 0, 0).astype(BF)
-    finish(puts)
+    dense_g = dot(ctk[...], cot[...], 0, 0).astype(BF)
+    lanes = width - cols
+    for d in range(2 * half):
+        for q in range(sp):
+            piece = dense_g[d * per : (d + 1) * per, q * lanes : (q + 1) * lanes]
+            gr[d * rows + q * per : d * rows + (q + 1) * per, cols:] = piece
+    more = sent(ids, gr, g_keep, g_send, rows, sem.at[0])
+    run(more)
+    finish(puts + more)
 
 
 ANY = pl.BlockSpec(memory_space=pl.ANY)
@@ -324,12 +353,11 @@
 IN_SMEM = pl.BlockSpec(memory_space=pltpu.SMEM)
 
 
-def call(body, name, args, specs, outs, out_specs, scratch, flops):
+def call(body, args, specs, outs, out_specs, scratch, flops):
     moved = sum(a.size * a.dtype.itemsize for a in args)
     moved += sum(o.size * o.dtype.itemsize for o in outs)
     return pl.pallas_call(
         body,
-        name=name,
         in_specs=specs,
         out_shape=outs,
         out_specs=out_specs,
@@ -339,21 +367,84 @@
     )(*args)
 
 
-def attention(ids, xs, cots, jw, dw, vec, jadd, tables, poss, seqs, heads):
+def tidy(body, args, outs):
+    specs = [IN_SMEM if a.dtype == jnp.int32 else IN_VMEM for a in args]
+    return call(body, args, specs, outs, [IN_VMEM] * len(outs), [], 0)
+
+
+def split_weights(sp, dp, expand, joined, out):
+    rows = expand.shape[0]
+    each = expand.shape[1] // (sp * dp)
+    cols = joined.shape[1] // sp
+    for s in range(sp):
+        for d in range(dp):
+            at = (d * sp + s) * each
+            out[s, :rows, d * each : (d + 1) * each] = expand[:, at : at + each]
+        out[s, rows:, :cols] = joined[:, s * cols : (s + 1) * cols]
+        out[s, rows:, cols:] = jnp.zeros((rows, out.shape[2] - cols), out.dtype)
+
+
+def split_grads(sp, cols, keep, got, last, dense):
+    value = (keep[...] + got[...].astype(F32)).astype(BF)
+    rows = value.shape[0] - 8
+    per = rows // sp
+    lanes = value.shape[1] - cols
+    for s in range(sp):
+        last[s, :per] = value[s * per : (s + 1) * per]
+        last[s, per:] = value[rows:]
+        dense[:, s * lanes : (s + 1) * lanes] = value[s * per : (s + 1) * per, cols:]
+
+
+def join_grads(sp, cols, at, last, out, small):
+    per = out.shape[0]
+    width = last.shape[2]
+    total = jnp.zeros((8, width), F32)
+    joined = jnp.zeros((8, width), F32)
+    for s in range(sp):
+        out[:, s * cols : (s + 1) * cols] = last[s, :per, :cols].astype(F32)
+        block = last[s, per:].astype(F32)
+        total = total + block
+        joined = joined + jnp.where(at[0] == s, block, 0.0)
+    row = lax.broadcasted_iota(jnp.int32, (8, LANES), 0)
+    mine = last[at[4], per:].astype(F32)
+    sums = pltpu.roll(total, at[1], 1)[:, :LANES]
+    joined = pltpu.roll(joined, at[2], 1)[:, :LANES]
+    mine = pltpu.roll(mine, at[3], 1)[:, :LANES]
+    small[...] = jnp.where(row < 5, sums, jnp.where(row == 5, joined, mine))
+
+
+def join_expand(sp, dp, parts, out):
+    each = parts.shape[2] // dp
+    for s in range(sp):
+        for d in range(dp):
+            at = (d * sp + s) * each
+            out[:, at : at + each] = parts[s, :, d * each : (d + 1) * each].astype(F32)
+
+
+def finish_tokens(x, cot, keep, got, add, out, grad):
+    rows = x[...].astype(F32)
+    sums = keep[...].astype(F32) + got[...].astype(F32)
+    out[...] = (rows + sums[0] + add[...]).astype(BF)
+    scaled = sums[1]
+    normed, inv = layer_norm(rows)
+    first = jnp.mean(scaled, axis=-1, keepdims=True)
+    second = jnp.mean(scaled * normed, axis=-1, keepdims=True)
+    grad[...] = cot[...].astype(F32) + inv * (scaled - first - normed * second)
+
+
+def attention(ids, xs, cots, jw, dw, vec, jadd, tables, poss, parts, seqs, heads):
     sp = len(xs)
-    chunk, width = cots[0].shape
+    chunk, width = parts[0].shape[1:]
     tokens = sp * chunk
     wide = jadd.shape[1]
     dp = 2 * jw[0].shape[0]
     rows = width // dp
     shape = jax.ShapeDtypeStruct
     outs = [
-        shape((sp, chunk, width), BF),
-        shape((sp, chunk, width), BF),
-        shape((dp, rows, wide), BF),
-        shape((heads * HD, width), BF),
-        shape((8, width), F32),
-        shape((8, wide), F32),
+        shape((dp // 2, rows + 8, width), BF),
+        shape((dp // 2, rows + 8, width), BF),
+        shape((sp // 2, 2, chunk, width), BF),
+        shape((sp // 2, 2, chunk, width), BF),
     ]
     scratch = [
         pltpu.VMEM((tokens, width), BF),
@@ -366,34 +457,37 @@
         pltpu.VMEM((tokens, wide), F32),
         pltpu.VMEM((tokens, wide), BF),
         pltpu.VMEM((tokens, heads * HD), BF),
-        pltpu.VMEM((width, wide), BF),
+        pltpu.VMEM((width, width), BF),
+        pltpu.VMEM((8, width), F32),
+        pltpu.VMEM((8, width), BF),
         pltpu.SemaphoreType.DMA((3, max(dp, sp))),
     ]
     return call(
         functools.partial(attn_kernel, sp, seqs, heads),
-        "attention_branch",
-        [ids, *xs, *cots, *jw, dw, vec, jadd, *tables, *poss],
-        [IN_SMEM] + [ANY] * (2 * sp + 2) + [IN_VMEM] * 7,
+        [ids, *xs, *cots, *jw, dw, vec, jadd, *tables, *poss, *parts],
+        [IN_SMEM] + [ANY] * (2 * sp + 2) + [IN_VMEM] * 10,
         outs,
-        [IN_VMEM, IN_VMEM, ANY, IN_VMEM, IN_VMEM, IN_VMEM],
+        [ANY, ANY, IN_VMEM, IN_VMEM],
         scratch,
-        12 * tokens * width * wide,
-    )
-
-
-def feed_forward(ids, xs, cots, ew, sw, ap, ea, vec, dense):
+        24 * tokens * width * wide,
+    )
+
+
+def feed_forward(ids, xs, cots, ew, sw, vec, chunk):
     sp = len(xs)
-    chunk, width = cots[0].shape
+    width = xs[0].shape[1]
     tokens = sp * chunk
     units = ew[0].shape[2]
     dp = 2 * ew[0].shape[0]
-    rows, per, extra = ew[0].shape[1], sw[0].shape[1], dense.shape[1]
+    rows, per = width // dp, sw[0].shape[1]
     shape = jax.ShapeDtypeStruct
     outs = [
-        shape((dp, rows, units), BF),
-        shape((dp, per + extra + 8, width), BF),
-        shape((sp // 2, 2, chunk, width), BF),
-        shape((sp // 2, 2, chunk, width), BF),
+        shape((dp // 2, rows, units), BF),
+        shape((dp // 2, rows, units), BF),
+        shape((dp // 2, per, width), BF),
+        shape((dp // 2, per, width), BF),
+        shape((sp, chunk, width), BF),
+        shape((sp, chunk, width), BF),
         shape((8, width), F32),
     ]
     scratch = [
@@ -410,13 +504,12 @@
     ]
     return call(
         functools.partial(mlp_kernel, sp),
-        "feed_forward_branch",
-        [ids, *xs, *cots, *ew, *sw, ap, ea, vec, dense],
-        [IN_SMEM] + [ANY] * (2 * sp + 4) + [IN_VMEM] * 4,
+        [ids, *xs, *cots, *ew, *sw, vec],
+        [IN_SMEM] + [ANY] * (2 * sp + 4) + [IN_VMEM],
         outs,
-        [ANY, ANY, IN_VMEM, IN_VMEM, IN_VMEM],
+        [ANY, ANY, ANY, ANY, IN_VMEM, IN_VMEM, IN_VMEM],
         scratch,
-        12 * tokens * width * units,
+        20 * tokens * width * units,
     )
 
 
@@ -450,13 +543,13 @@
     sp_order, dp_order = cube_order(sp), cube_order(dp)
     ids = jnp.asarray(dp_order, jnp.int32) ^ dp_me
 
-    expand_part = expand_weight.reshape(row_n, dp, sp, ff_n).transpose(2, 0, 1, 3)
-    joined_part = joined_weight.reshape(row_n, sp, cols).transpose(1, 0, 2)
-    joined_part = jnp.pad(joined_part, ((0, 0), (0, 0), (0, units - cols)))
-    both = jnp.concatenate([expand_part.reshape(sp, row_n, units), joined_part], axis=1)
+    shape = jax.ShapeDtypeStruct
+    split = functools.partial(split_weights, sp, dp)
+    outs = [shape((sp, 2 * row_n, units), BF)]
+    (both,) = tidy(split, [expand_weight, joined_weight], outs)
     both = lax.all_to_all(both, "sp", split_axis=0, concat_axis=0, tiled=True)
     expand_part = both[:, :row_n].reshape(rows_d, units)
-    joined_part = both[:, row_n:, :cols].reshape(rows_d, cols)
+    joined_part = both[:, row_n:, :wide].reshape(rows_d, wide)
 
     small_parts = (
         joined_bias,
@@ -469,28 +562,25 @@
         mlp_shift,
     )
     sizes = [part.shape[0] for part in small_parts]
-    small = jnp.stack([jnp.pad(part, (0, width - part.shape[0])) for part in small_parts])
-    xs = token_blocks(jnp.concatenate([inputs.reshape(local, width), small]), "sp")
-    cots = token_blocks(cotangent.reshape(local, width), "sp")
-    small = jnp.stack([block[local:, :LANES] for block in xs])
+    row = jnp.arange(8, dtype=jnp.int32)[:, None]
+    small = jnp.zeros((8, width), BF)
+    for i, part in enumerate(small_parts):
+        small = jnp.where(row == i, jnp.pad(part, (0, width - part.shape[0]))[None], small)
+    xs = token_blocks(inputs.reshape(local, width), "sp")
+    cots = token_blocks(jnp.concatenate([cotangent.reshape(local, width), small]), "sp")
+    small = jnp.stack([block[local:, :LANES] for block in cots])
     small = flip_bits(turn_bits(small), "sp").transpose(1, 0, 2).reshape(8, sp * LANES)
-    small = jnp.pad(small, ((0, 0), (0, width - sp * LANES)))
-
-    dense_part = dense_weight.reshape(rows_d, width // sp)
-    attn_pack = jnp.concatenate([joined_part, dense_part], axis=1)
-    attn_pack = jnp.concatenate([attn_pack, small], axis=0)
-    joined_w = halves(attn_pack, "dp")
+    small = halves(small, "dp")
+    small = flip_bits(turn_bits(jnp.concatenate(small, axis=0)), "dp")
+    small = small.reshape(dp, 8, sp, LANES).astype(F32)
+
+    dense_part = transposed(dense_weight, False)
     shrink_w = halves(shrink_weight, "dp")
-    expand_w = halves(expand_part, "dp")
-
-    def natural(lanes_at, lanes, rows_at, rows):
-        got = [h[:, rows_at : rows_at + rows, lanes_at : lanes_at + lanes] for h in joined_w]
-        return flip_bits(turn_bits(jnp.concatenate(got, axis=0)), "dp")
-
-    dense_rows = natural(cols, width // sp, 0, rows_d).reshape(sp, dp // sp, rows_d, width // sp)
-    dense_w = lax.all_to_all(dense_rows, "sp", split_axis=0, concat_axis=0, tiled=True)
-    dense_w = dense_w.transpose(1, 0, 2, 3).reshape(heads * HD, width)
-    small = natural(0, sp * LANES, rows_d, 8).reshape(dp, 8, sp, LANES).astype(F32)
+    expand_w = halves(jnp.concatenate([expand_part, dense_part]), "dp")
+    joined_w = halves(joined_part, "dp")
+
+    dense_w = jnp.concatenate([half[:, rows_d:] for half in expand_w], axis=0)
+    dense_w = flip_bits(turn_bits(dense_w), "dp").reshape(heads * HD, width)
 
     def whole(index):
         return small[:, index, :, : sizes[index]].reshape(-1)
@@ -509,7 +599,16 @@
     freq = 1.0 / 10000.0 ** ((2 * lane).astype(F32) / ROT)
     angles = pos.astype(F32)[:, None] * freq[None, :]
     joined_row = jnp.pad(joined_add, (0, wide - cols))[None]
-    ap, ea, joined_g, dense_g, a_sums, j_sums = attention(
+    e_keep, e_send, s_keep, s_send, *parts = feed_forward(
+        ids,
+        xs,
+        cots,
+        expand_w,
+        shrink_w,
+        stacked([whole(6), whole(7), expand_add]),
+        local,
+    )
+    a_keep, a_send, keep, send = attention(
         ids,
         xs,
         cots,
@@ -519,80 +618,63 @@
         joined_row,
         (jnp.cos(angles), jnp.sin(angles)),
         (pos[:, None], pos[None, :]),
+        parts,
         seqs,
         heads,
     )
-    dense_g = dense_g.reshape(dp // sp, sp, row_n, width).transpose(1, 0, 2, 3)
-    dense_g = dense_g.reshape(heads * HD, width)
-    dense_g = lax.all_to_all(dense_g, "sp", split_axis=0, concat_axis=0, tiled=True)
-    dense_g = jnp.pad(dense_g.reshape(dp, row_n, width), ((0, 0), (0, -row_n % 8), (0, 0)))
-    expand_g, shrink_g, keep, send, m_sums = feed_forward(
-        ids,
-        xs,
-        cots,
-        expand_w,
-        shrink_w,
-        ap,
-        ea,
-        stacked([whole(6), whole(7), expand_add]),
-        dense_g,
-    )
-
-    got = swap(send, "sp", 1)
-    parts = keep.astype(F32) + got.astype(F32)
-    for bit in bits_of(sp)[1:]:
-        half = parts.shape[0] // 2
-        got = swap(parts[half:].astype(BF), "sp", bit)
-        parts = parts[:half] + got.astype(F32)
-    out_sum, scaled = parts[0, 0], parts[0, 1]
-    rows = inputs.reshape(local, width).astype(F32)
-    output = (rows + out_sum + out_add).astype(BF).reshape(inputs.shape)
-    own_normed, own_inv = layer_norm(rows)
-    first = jnp.mean(scaled, axis=-1, keepdims=True)
-    second = jnp.mean(scaled * own_normed, axis=-1, keepdims=True)
-    cot_f = cotangent.reshape(local, width).astype(F32)
-    input_grad = cot_f + own_inv * (scaled - first - own_normed * second)
-    input_grad = input_grad.reshape(inputs.shape)
-
-    joined_b_all = lax.dynamic_update_slice_in_dim(
-        jnp.zeros((cols * sp,), F32), j_sums[0, :cols], me * cols, 0
-    )
-    mine = (jnp.arange(sp, dtype=jnp.int32) == me)[None, :, None]
-    expand_b_all = jnp.where(mine, m_sums[0, :units].reshape(dp, 1, ff_n), 0.0)
-
-    def split(vector):
-        vector = vector.reshape(dp, sp, -1)
-        return jnp.pad(vector, ((0, 0), (0, 0), (0, LANES - vector.shape[2])))
-
-    vectors = [joined_b_all, expand_b_all, jnp.sum(cot_f, axis=0)]
-    vectors += [a_sums[0], a_sums[1], m_sums[1], m_sums[2]]
-    small_g = jnp.stack([split(v) for v in vectors] + [jnp.zeros((dp, sp, LANES), F32)], axis=1)
-    small_g = turn_bits(flip_bits(small_g, "dp")).reshape(dp, 8, sp * LANES)
-    small_g = jnp.pad(small_g, ((0, 0), (0, 0), (0, width - sp * LANES))).astype(BF)
-    small_at = shrink_g.shape[1] - 8
-    shrink_g = lax.dynamic_update_slice(shrink_g, small_g, (0, small_at, 0))
-
-    joined_g = cube_scatter(joined_g, "dp", BF)[0, :, :cols].astype(BF)
-    joined_g = lax.all_to_all(joined_g, "sp", split_axis=0, concat_axis=1, tiled=True)
-    expand_g = cube_scatter(expand_g, "dp", BF)[0].astype(BF)
-    expand_g = lax.all_to_all(expand_g, "sp", split_axis=0, concat_axis=1, tiled=True)
-    expand_g = expand_g.reshape(row_n, sp, dp, ff_n).transpose(0, 2, 1, 3).reshape(row_n, -1)
-    shrink_g = cube_scatter(shrink_g, "dp", BF)[0]
-    small_g = shrink_g[small_at:, : sp * LANES].reshape(8, sp, LANES).transpose(1, 0, 2)
-    small_g = cube_scatter(turn_bits(flip_bits(small_g, "sp")), "sp", F32)[0]
-    names = [0, 2, 1, 4, 5, 6, 7]
-    pieces = [small_g[i, : sizes[name]] for i, name in enumerate(names)]
-    joined_bg, expand_bg, out_bg, gain_ag, shift_ag, gain_bg, shift_bg = pieces
+
+    keep, got = cube_scatter(keep, send, "sp")
+    output, input_grad = tidy(
+        finish_tokens,
+        [
+            inputs.reshape(local, width),
+            cotangent.reshape(local, width),
+            keep,
+            got,
+            out_add[None],
+        ],
+        [shape((local, width), BF), shape((local, width), F32)],
+    )
+    output, input_grad = output.reshape(inputs.shape), input_grad.reshape(inputs.shape)
+
+    keep, got = cube_scatter(s_keep, s_send, "dp")
+    shrink_g = keep + got.astype(F32)
+    keep, got = cube_scatter(e_keep, e_send, "dp")
+    expand_g = (keep + got.astype(F32)).astype(BF).reshape(sp, row_n, units)
+    expand_g = lax.all_to_all(expand_g, "sp", split_axis=0, concat_axis=0, tiled=True)
+    (expand_g,) = tidy(
+        functools.partial(join_expand, sp, dp), [expand_g], [shape(expand_weight.shape, F32)]
+    )
+    keep, got = cube_scatter(a_keep, a_send, "dp")
+    last, dense_g = tidy(
+        functools.partial(split_grads, sp, cols),
+        [keep, got],
+        [shape((sp, row_n + 8, width), BF), shape((row_n, width), BF)],
+    )
+    last = lax.all_to_all(last, "sp", split_axis=0, concat_axis=0, tiled=True)
+    dense_g = transposed(dense_g, True)
+    own_b = joined_bias.shape[0]
+    linear = dp_me * sp + me
+    holder = linear * own_b // cols
+    starts = [linear * row_n, linear * own_b - holder * cols, dp_me * ff_n]
+    at = [holder] + [(width - start) % width for start in starts] + [me]
+    joined_g, small_g = tidy(
+        functools.partial(join_grads, sp, cols),
+        [jnp.stack(at).astype(jnp.int32), last],
+        [shape(joined_weight.shape, F32), shape((8, LANES), F32)],
+    )
+    joined_bg, expand_bg = small_g[5, :own_b], small_g[6, :ff_n]
+    gain_ag, shift_ag, gain_bg, shift_bg, out_bg = [small_g[i, :row_n] for i in range(5)]
     return (
         output,
         input_grad,
-        joined_g.astype(F32),
+        joined_g,
         joined_bg,
-        shrink_g[ff_n : ff_n + row_n],
+        dense_g.astype(F32),
         out_bg,
-        expand_g.astype(F32),
+        expand_g,
         expand_bg,
-        shrink_g[:ff_n],
+        shrink_g,
         out_bg,
         gain_ag,
         shift_ag,

time: 237 us -> 241 us (1.017)
  waiting for transfers between devices: 65.2 us -> 107 us
  local copies, waits for them, and re-layouts: 42.5 us -> 18.7 us
  starting transfers between devices: 61.2 us -> 43.4 us
  Pallas kernels: 44 us -> 54.8 us
  other arithmetic: 21.2 us -> 14.5 us
    ppermute x28 -> x29, waiting for transfers between devices: 41.9 us -> 94.7 us  [swap(): return lax.ppermute(value, axis, [(i, i ^ bit) for i in range(count)])]
    ppermute x28 -> x29, starting transfers between devices: 43.8 us -> 31.1 us  [swap(): return lax.ppermute(value, axis, [(i, i ^ bit) for i in range(count)])]
    all_to_all x1, waiting for transfers between devices: 11.6 us -> 0.01 us  [on_device(): both = lax.all_to_all(both, 'sp', split_axis=0, concat_axis=0, tiled=True)]
    pallas_call x2 -> x7, Pallas kernels: 44 us -> 54.8 us  [call(): pl.pallas_call(body, in_specs=specs, out_shape=outs, out_specs=out_specs,...]
    slice x25 -> x3, local copies, waits for them, and re-layouts: 11.1 us -> 0.94 us  [the longest x2 0.93 us: on_device(): dense_w = jnp.concatenate([half[:, rows_d:] for half in expand_w], axis=0)]
    all_to_all x4 -> x2, starting transfers between devices: 14 us -> 6.7 us  [the longest x1 3.37 us: on_device(): last = lax.all_to_all(last, 'sp', split_axis=0, concat_axis=0, tiled=True)]
    add x10 -> x1, other arithmetic: 8.64 us -> 1.67 us  [on_device(): shrink_g = keep + got.astype(F32)]
    convert_element_type x4 -> x10, other arithmetic: 1.66 us -> 7.31 us  [the longest x7 5.94 us: cube_scatter(): send = (keep[half:].astype(F32) + got[half:].astype(F32)).astype(BF)]
  transfers between devices with their start and end apart: 33 -> 34, of which waited for: 17 -> 12; matrix products, arithmetic and copies ran while one was open for 22% -> 10% of each run, Pallas kernels for 11% -> 21%
where the time goes in v1:
time: 241 us; the launch traced here: 240 us
  waiting for transfers between devices  107 us (44%)
  Pallas kernels  54.8 us (23%)
  starting transfers between devices  43.4 us (18%)
  local copies, waits for them, and re-layouts  18.7 us (8%)
  other arithmetic  14.5 us (6%)
    ppermute x29, waiting for transfers between devices, swap(): return lax.ppermute(value, axis, [(i, i ^ bit) for i in range(count)])  94.7 us
    pallas_call x7, Pallas kernels, call(): pl.pallas_call(body, in_specs=specs, out_shape=outs, out_specs=out_specs,...  54.8 us
    ppermute x29, starting transfers between devices, swap(): return lax.ppermute(value, axis, [(i, i ^ bit) for i in range(count)])  31.1 us
    all_to_all x1, waiting for transfers between devices, on_device(): last = lax.all_to_all(last, 'sp', split_axis=0, concat_axis=0, tiled=True)  12.5 us
    convert_element_type x7, other arithmetic, cube_scatter(): send = (keep[half:].astype(F32) + got[half:].astype(F32)).astype(BF)  5.94 us
    pad x8, local copies, waits for them, and re-layouts, on_device(): jnp.pad(part, (0, width - part.shape[0]))[None]  5.36 us
  transfers between devices with their start and end apart: 34, of which 12 were waited for; matrix products, arithmetic and copies ran while one was open for 10% of the time, Pallas kernels for 21%

profile of v1, /device:TPU:0, one launch (start us, length us, event | category | flops | bytes accessed | tf_op | source)
XLA Modules:
  0.0 239.8 jit_solution(18381531334186927835)
XLA Ops:
  0.8 0.7 pad.31
  1.5 0.7 pad.32
  2.2 0.7 pad.33
  2.8 0.7 pad.34
  3.5 0.7 pad.35
  4.1 0.7 pad.36
  4.8 0.7 pad.37
  5.5 0.7 pad.38
  6.2 1.0 pad_maximum_fusion.3.refs_4_
  7.2 3.1 %collective-permute-start.3 = (bf16[264,768]{1,0:T(8,128)(2,1)S(1)}, bf16[264,768]{1,0:T(8,128)(2,1)S(1)}, u32[]{:S(2)}, u32[]{:S(2)}) collective-permute-start(bf16[264,768]{1,0:T(8,128)(2,1)S(1)} %pad_maximum_fusion.3.refs_4_), channel_id=1, source_target_pairs={{0,2},{1,3},{2,0},{3,1},{4,6},{5,7},{6,4},{7,5},{8,10},{9,11},{10,... | collective-permute-start | bytes 1216520 | tf_op jit(solution)/shard_map/ppermute | solution.py:40
  10.3 1.8 shard_map.263
  12.1 3.5 %all-to-all-start = ((bf16[4,48,768]{2,1,0:T(8,128)(2,1)}), bf16[4,48,768]{2,1,0:T(8,128)(2,1)S(1)}, u32[]{:S(2)}, u32[]{:S(2)}) async-start(bf16[4,48,768]{2,1,0:T(8,128)(2,1)} %shard_map.263), calls=%async_computation | async-start | bytes 589824 | tf_op jit(solution)/shard_map/all_to_all | solution.py:550
  15.6 0.7 collective-permute-start.9
  16.3 5.6 %collective-permute-start.16 = (bf16[1,96,768]{2,1,0:T(8,128)(2,1)S(1)}, bf16[1,96,768]{2,1,0:T(8,128)(2,1)S(1)}, u32[]{:S(2)}, u32[]{:S(2)}) collective-permute-start(bf16[1,96,768]{2,1,0:T(8,128)(2,1)S(1)} %bitcast.97), channel_id=1, source_target_pairs={{0,16},{4,20},{8,24},{12,28},{16,0},{20,4},{24,8},{28,12},{1,17},{... | collective-permute-start | bytes 442376 | tf_op jit(solution)/shard_map/ppermute | solution.py:40
  21.9 0.7 collective-permute-start
  22.7 1.8 multiply_sine_fusion
  25.0 0.9 copy.38.refs_15_
  26.0 4.9 %collective-permute-done.16 = bf16[1,96,768]{2,1,0:T(8,128)(2,1)S(1)} collective-permute-done((bf16[1,96,768]{2,1,0:T(8,128)(2,1)S(1)}, bf16[1,96,768]{2,1,0:T(8,128)(2,1)S(1)}, u32[]{:S(2)}, u32[]{:S(2)}) %collective-permute-start.16) | collective-permute-done | bytes 147488 | tf_op jit(solution)/shard_map/ppermute | solution.py:40
  31.3 8.2 %collective-permute-done.6 = bf16[1,96,640]{2,1,0:T(8,128)(2,1)S(1)} collective-permute-done((bf16[1,96,640]{2,1,0:T(8,128)(2,1)S(1)}, bf16[1,96,640]{2,1,0:T(8,128)(2,1)S(1)}, u32[]{:S(2)}, u32[]{:S(2)}) %collective-permute-start.6) | collective-permute-done | bytes 122912 | tf_op jit(solution)/shard_map/ppermute | solution.py:40
  39.7 2.2 collective-permute-start.10
  41.8 0.7 slice_bitcast_fusion.1
  42.5 8.3 %collective-permute-done.10 = bf16[1,120,768]{2,1,0:T(8,128)(2,1)S(1)} collective-permute-done((bf16[1,120,768]{2,1,0:T(8,128)(2,1)S(1)}, bf16[1,120,768]{2,1,0:T(8,128)(2,1)S(1)}, u32[]{:S(2)}, u32[]{:S(2)}) %collective-permute-start.10) | collective-permute-done | bytes 184352 | tf_op jit(solution)/shard_map/ppermute | solution.py:40
  50.9 2.6 %collective-permute-start.11 = (bf16[2,120,768]{2,1,0:T(8,128)(2,1)S(1)}, bf16[2,120,768]{2,1,0:T(8,128)(2,1)S(1)}, u32[]{:S(2)}, u32[]{:S(2)}) collective-permute-start(bf16[2,120,768]{2,1,0:T(8,128)(2,1)S(1)} %pad_maximum_fusion.4), channel_id=1, source_target_pairs={{0,8},{4,12},{8,0},{12,4},{16,24},{20,28},{24,16},{28,20},{1,9},{5... | collective-permute-start | bytes 1105928 | tf_op jit(solution)/shard_map/ppermute | solution.py:40
  53.6 0.9 collective-permute-start.13
  54.6 8.9 %collective-permute-done.13 = bf16[1,8,512]{2,1,0:T(8,128)(2,1)S(1)} collective-permute-done((bf16[1,8,512]{2,1,0:T(8,128)(2,1)S(1)}, bf16[1,8,512]{2,1,0:T(8,128)(2,1)S(1)}, u32[]{:S(2)}, u32[]{:S(2)}) %collective-permute-start.13) | collective-permute-done | bytes 8224 | tf_op jit(solution)/shard_map/ppermute | solution.py:40
  64.0 2.3 collective-permute-start.14
  66.4 1.6 collective-permute-done.14
  68.1 1.9 collective-permute-start.8
  70.3 19.2 %collective-permute-done.15 = bf16[4,8,512]{2,1,0:T(8,128)(2,1)S(1)} collective-permute-done((bf16[4,8,512]{2,1,0:T(8,128)(2,1)S(1)}, bf16[4,8,512]{2,1,0:T(8,128)(2,1)S(1)}, u32[]{:S(2)}, u32[]{:S(2)}) %collective-permute-start.15) | collective-permute-done | bytes 32800 | tf_op jit(solution)/shard_map/ppermute | solution.py:40
  92.1 0.7 pad_maximum_fusion.10.refs_11_
  92.8 13.9 %collective-permute-done.12.refs_9_ = bf16[4,120,768]{2,1,0:T(8,128)(2,1)} collective-permute-done((bf16[4,120,768]{2,1,0:T(8,128)(2,1)S(1)}, bf16[4,120,768]{2,1,0:T(8,128)(2,1)}, u32[]{:S(2)}, u32[]{:S(2)}) %collective-permute-start.12) | collective-permute-done | bytes 737312 | tf_op jit(solution)/shard_map/ppermute | solution.py:40
  106.7 17.0 %shard_map.264 = (bf16[4,96,768]{2,1,0:T(8,128)(2,1)}, bf16[4,96,768]{2,1,0:T(8,128)(2,1)}, bf16[4,96,768]{2,1,0:T(8,128)(2,1)}, bf16[4,96,768]{2,1,0:T(8,128)(2...) custom-call(s32[8]{0:T(128)} %broadcast_xor_fusion.ids, ...), custom_call_target="tpu_custom_call" | custom-call | flops 12079595520 | bytes 11403296 | tf_op jit(solution)/shard_map/pallas_call | solution.py:359
  124.1 1.7 collective-permute-start.25
  125.8 0.9 slice.211
  126.9 0.8 reverse_select_fusion
  127.6 27.4 %shard_map.265 = (bf16[4,104,768]{2,1,0:T(8,128)(2,1)}, bf16[4,104,768]{2,1,0:T(8,128)(2,1)}, bf16[2,2,256,768]{3,2,1,0:T(8,128)(2,1)}, bf16[2,2,256,768]{3,2,1,0:T(8,128)(2,1)}) custom-call(s32[8]{0:T(128)} %broadcast_xor_fusion.ids, bf16[256,768]{1,0:T(8,128)(2,1)} %bitcast.102, bf16[256,768]{1,0:T(8,128)(2,1)} %collective-permute-done.refs_1_, ...), custom_call_target="tpu_custom_call" | custom-call | flops 12079595520 | bytes 12622368 | tf_op jit(solution)/shard_map/pallas_call | solution.py:359
  156.1 0.7 add.164
  156.8 0.8 copy-done.10
  157.6 1.2 add_convert_fusion.2
  158.8 2.6 %collective-permute-start.29 = (bf16[2,96,768]{2,1,0:T(8,128)(2,1)S(1)}, bf16[2,96,768]{2,1,0:T(8,128)(2,1)S(1)}, u32[]{:S(2)}, u32[]{:S(2)}) collective-permute-start(bf16[2,96,768]{2,1,0:T(8,128)(2,1)S(1)} %get-tuple-element.52), channel_id=1, source_target_pairs={{0,8},{4,12},{8,0},{12,4},{16,24},{20,28},{24,16},{28,20},{1,9},{5... | collective-permute-start | bytes 884744 | tf_op jit(solution)/shard_map/ppermute | solution.py:40
  161.6 7.3 %collective-permute-done.21 = bf16[4,104,768]{2,1,0:T(8,128)(2,1)S(1)} collective-permute-done((bf16[4,104,768]{2,1,0:T(8,128)(2,1)}, bf16[4,104,768]{2,1,0:T(8,128)(2,1)S(1)}, u32[]{:S(2)}, u32[]{:S(2)}) %collective-permute-start.21) | collective-permute-done | bytes 639008 | tf_op jit(solution)/shard_map/ppermute | solution.py:40
  169.1 2.0 collective-permute-start.22
  171.1 0.7 fusion.2
  172.3 6.4 %collective-permute-done.26 = bf16[2,96,768]{2,1,0:T(8,128)(2,1)S(1)} collective-permute-done((bf16[2,96,768]{2,1,0:T(8,128)(2,1)S(1)}, bf16[2,96,768]{2,1,0:T(8,128)(2,1)S(1)}, u32[]{:S(2)}, u32[]{:S(2)}) %collective-permute-start.26) | collective-permute-done | bytes 294944 | tf_op jit(solution)/shard_map/ppermute | solution.py:40
  178.9 8.2 %collective-permute-done.22 = bf16[2,104,768]{2,1,0:T(8,128)(2,1)S(1)} collective-permute-done((bf16[2,104,768]{2,1,0:T(8,128)(2,1)S(1)}, bf16[2,104,768]{2,1,0:T(8,128)(2,1)S(1)}, u32[]{:S(2)}, u32[]{:S(2)}) %collective-permute-start.22) | collective-permute-done | bytes 319520 | tf_op jit(solution)/shard_map/ppermute | solution.py:40
  187.1 0.8 fusion
  188.0 7.6 %collective-permute-done.27 = bf16[1,96,768]{2,1,0:T(8,128)(2,1)S(1)} collective-permute-done((bf16[1,96,768]{2,1,0:T(8,128)(2,1)S(1)}, bf16[1,96,768]{2,1,0:T(8,128)(2,1)S(1)}, u32[]{:S(2)}, u32[]{:S(2)}) %collective-permute-start.27) | collective-permute-done | bytes 147488 | tf_op jit(solution)/shard_map/ppermute | solution.py:40
  195.6 0.7 fusion.7
  196.3 3.3 %all-to-all-start.2 = ((bf16[4,24,768]{2,1,0:T(8,128)(2,1)}), bf16[4,24,768]{2,1,0:T(8,128)(2,1)S(1)}, u32[]{:S(2)}, u32[]{:S(2)}) async-start(bf16[4,24,768]{2,1,0:T(8,128)(2,1)} %bitcast.45), calls=%async_computation.2 | async-start | bytes 294912 | tf_op jit(solution)/shard_map/all_to_all | solution.py:644
  200.3 1.7 shard_map.267
  202.1 1.4 collective-permute-start.24
  203.5 2.9 %add_convert_fusion = (bf16[1,2,256,768]{3,2,1,0:T(8,128)(2,1)S(1)}, f32[2,256,768]{2,1,0:T(8,128)}) fusion(bf16[2,2,256,768]{3,2,1,0:T(8,128)(2,1)} %collective-permute-done.19, bf16[2,2,256,768]{3,2,1,0:T(8,128)(2,1)S(1)} %copy-done), kind=kLoop, calls=%fused_computation | loop fusion | flops 2752512 | bytes 5505024 | tf_op jit(solution)/shard_map/convert_element_type | solution.py:74
  206.4 2.5 %collective-permute-start.20 = (bf16[1,2,256,768]{3,2,1,0:T(8,128)(2,1)S(1)}, bf16[1,2,256,768]{3,2,1,0:T(8,128)(2,1)S(1)}, u32[]{:S(2)}, u32[]{:S(2)}) collective-permute-start(bf16[1,2,256,768]{3,2,1,0:T(8,128)(2,1)S(1)} %get-tuple-element.48), channel_id=1, source_target_pairs={{0,2},{1,3},{2,0},{3,1},{4,6},{5,7},{6,4},{7,5},{8,10},{9,11},{10,... | collective-permute-start | bytes 2359304 | tf_op jit(solution)/shard_map/ppermute | solution.py:40
  208.9 3.4 %all-to-all-start.1 = ((bf16[4,32,768]{2,1,0:T(8,128)(2,1)}), bf16[4,32,768]{2,1,0:T(8,128)(2,1)S(1)}, u32[]{:S(2)}, u32[]{:S(2)}) async-start(bf16[4,32,768]{2,1,0:T(8,128)(2,1)} %get-tuple-element.40), calls=%async_computation.1 | async-start | bytes 393216 | tf_op jit(solution)/shard_map/all_to_all | solution.py:654
  212.2 1.7 fusion.4
  213.9 1.7 shard_map.269
  216.3 12.5 %all-to-all-done.1.last = bf16[4,32,768]{2,1,0:T(8,128)(2,1)S(1)} async-done(((bf16[4,32,768]{2,1,0:T(8,128)(2,1)}), bf16[4,32,768]{2,1,0:T(8,128)(2,1)S(1)}, u32[]{:S(2)}, u32[]{:S(2)}) %all-to-all-start.1) | async-done | bytes 196640 | tf_op jit(solution)/shard_map/all_to_all | solution.py:654
  228.8 0.7 copy-done.2
  229.5 1.7 shard_map.268
  231.2 1.4 slice_bitcast_fusion.4
  232.6 1.2 slice_bitcast_fusion.10
  233.8 1.2 slice_bitcast_fusion.8
  235.0 0.9 copy-done.3
  235.9 3.4 %shard_map.266 = (bf16[256,768]{1,0:T(8,128)(2,1)}, f32[256,768]{1,0:T(8,128)}) custom-call(bf16[256,768]{1,0:T(8,128)(2,1)} %bitcast.103, bf16[256,768]{1,0:T(8,128)(2,1)} %bitcast.88, f32[2,256,768]{2,1,0:T(8,128)} %get-tuple-element.49.keep, bf16[2,256,768]{2,1,0:T(8,128)(2,1)} %bitcast.96, f32[1,768]{1,0:T(1,128)} %add.164), custom_call_target="tpu_custom_call" | custom-call | bytes 4328448 | tf_op jit(solution)/shard_map/pallas_call | solution.py:359
  (143 shorter events, 9.4 us)
Async XLA Ops:
  0.6 22.0 %copy-start.21 = (s32[4]{0:T(128)S(1)}, s32[4]{0:T(128)}, u32[]{:S(2)}) copy-start(s32[4]{0:T(128)} %constant.100.clone) | copy-start | bytes 52
  0.7 23.9 %copy-start.20 = (s32[8]{0:T(128)S(1)}, s32[8]{0:T(128)}, u32[]{:S(2)}) copy-start(s32[8]{0:T(128)} %constant.99.clone) | copy-start | bytes 100
  0.7 14.9 %copy-start.19 = (bf16[24,768]{1,0:T(8,128)(2,1)S(1)}, bf16[24,768]{1,0:T(8,128)(2,1)}, u32[]{:S(2)}) copy-start(bf16[24,768]{1,0:T(8,128)(2,1)} %param.20) | copy-start | bytes 110596
  0.7 15.6 %copy-start.5 = (bf16[96,768]{1,0:T(8,128)(2,1)S(1)}, bf16[96,768]{1,0:T(8,128)(2,1)}, u32[]{:S(2)}) copy-start(bf16[96,768]{1,0:T(8,128)(2,1)} %param.24) | copy-start | bytes 442372
  0.7 21.3 %copy-start.13 = (bf16[2,128,768]{2,1,0:T(8,128)(2,1)S(1)}, bf16[2,128,768]{2,1,0:T(8,128)(2,1)}, u32[]{:S(2)}) copy-start(bf16[2,128,768]{2,1,0:T(8,128)(2,1)} %param.16) | copy-start | bytes 1179652
  7.2 24.0 %copy-start.12 = (bf16[264,768]{1,0:T(8,128)(2,1)}, bf16[264,768]{1,0:T(8,128)(2,1)S(1)}, u32[]{:S(2)}) copy-start(bf16[264,768]{1,0:T(8,128)(2,1)S(1)} %pad_maximum_fusion.3.refs_4_) | copy-start | bytes 1216516
  7.2 32.3 %collective-permute-start.3 = (bf16[264,768]{1,0:T(8,128)(2,1)S(1)}, bf16[264,768]{1,0:T(8,128)(2,1)S(1)}, u32[]{:S(2)}, u32[]{:S(2)}) collective-permute-start(bf16[264,768]{1,0:T(8,128)(2,1)S(1)} %pad_maximum_fusion.3.refs_4_), channel_id=1, source_target_pairs={{0,2},{1,3},{2,0},{3,1},{4,6},{5,7},{6,4},{7,5},{8,10},{9,11},{10,... | collective-permute-start | bytes 1216520 | tf_op jit(solution)/shard_map/ppermute | solution.py:40
  10.3 29.4 %collective-permute-start.4 = (bf16[264,768]{1,0:T(8,128)(2,1)S(1)}, bf16[264,768]{1,0:T(8,128)(2,1)}, u32[]{:S(2)}, u32[]{:S(2)}) collective-permute-start(bf16[264,768]{1,0:T(8,128)(2,1)S(1)} %pad_maximum_fusion.3.refs_4_), channel_id=1, source_target_pairs={{0,1},{1,0},{2,3},{3,2},{4,5},{5,4},{6,7},{7,6},{8,9},{9,8},{10,11... | collective-permute-start | bytes 1216520 | tf_op jit(solution)/shard_map/ppermute | solution.py:40
  12.1 13.8 %all-to-all-start = ((bf16[4,48,768]{2,1,0:T(8,128)(2,1)}), bf16[4,48,768]{2,1,0:T(8,128)(2,1)S(1)}, u32[]{:S(2)}, u32[]{:S(2)}) async-start(bf16[4,48,768]{2,1,0:T(8,128)(2,1)} %shard_map.263), calls=%async_computation | async-start | bytes 589824 | tf_op jit(solution)/shard_map/all_to_all | solution.py:550
  15.6 15.4 %collective-permute-start.9 = (bf16[24,768]{1,0:T(8,128)(2,1)S(1)}, bf16[24,768]{1,0:T(8,128)(2,1)S(1)}, u32[]{:S(2)}, u32[]{:S(2)}) collective-permute-start(bf16[24,768]{1,0:T(8,128)(2,1)S(1)} %copy-done.19), channel_id=1, source_target_pairs={{0,0},{1,4},{2,8},{3,12},{4,16},{5,20},{6,24},{7,28},{8,1},{9,5},{... | collective-permute-start | bytes 110600 | tf_op jit(solution)/shard_map/ppermute | solution.py:66
  16.3 14.6 %collective-permute-start.16 = (bf16[1,96,768]{2,1,0:T(8,128)(2,1)S(1)}, bf16[1,96,768]{2,1,0:T(8,128)(2,1)S(1)}, u32[]{:S(2)}, u32[]{:S(2)}) collective-permute-start(bf16[1,96,768]{2,1,0:T(8,128)(2,1)S(1)} %bitcast.97), channel_id=1, source_target_pairs={{0,16},{4,20},{8,24},{12,28},{16,0},{20,4},{24,8},{28,12},{1,17},{... | collective-permute-start | bytes 442376 | tf_op jit(solution)/shard_map/ppermute | solution.py:40
  21.9 20.6 %collective-permute-start = (bf16[256,768]{1,0:T(8,128)(2,1)S(1)}, bf16[256,768]{1,0:T(8,128)(2,1)}, u32[]{:S(2)}, u32[]{:S(2)}) collective-permute-start(bf16[256,768]{1,0:T(8,128)(2,1)S(1)} %bitcast.104), channel_id=1, source_target_pairs={{0,2},{1,3},{2,0},{3,1},{4,6},{5,7},{6,4},{7,5},{8,10},{9,11},{10,... | collective-permute-start | bytes 1179656 | tf_op jit(solution)/shard_map/ppermute | solution.py:40
  22.7 28.2 %copy-start.15 = (s32[4,128]{1,0:T(4,128)}, s32[4,128]{1,0:T(4,128)S(1)}, u32[]{:S(2)}) copy-start(s32[4,128]{1,0:T(4,128)S(1)} %get-tuple-element.70) | copy-start | bytes 6148
  30.9 8.6 %collective-permute-start.6 = (bf16[1,96,640]{2,1,0:T(8,128)(2,1)S(1)}, bf16[1,96,640]{2,1,0:T(8,128)(2,1)S(1)}, u32[]{:S(2)}, u32[]{:S(2)}) collective-permute-start(bf16[1,96,640]{2,1,0:T(8,128)(2,1)S(1)} %bitcast.93), channel_id=1, source_target_pairs={{0,16},{4,20},{8,24},{12,28},{16,0},{20,4},{24,8},{28,12},{1,17},{... | collective-permute-start | bytes 368648 | tf_op jit(solution)/shard_map/ppermute | solution.py:40
  31.0 61.8 %collective-permute-start.1 = (bf16[256,768]{1,0:T(8,128)(2,1)S(1)}, bf16[256,768]{1,0:T(8,128)(2,1)}, u32[]{:S(2)}, u32[]{:S(2)}) collective-permute-start(bf16[256,768]{1,0:T(8,128)(2,1)S(1)} %bitcast.105), channel_id=1, source_target_pairs={{0,1},{1,0},{2,3},{3,2},{4,5},{5,4},{6,7},{7,6},{8,9},{9,8},{10,11... | collective-permute-start | bytes 1179656 | tf_op jit(solution)/shard_map/ppermute | solution.py:40
  39.5 14.1 %collective-permute-start.17 = (bf16[2,96,768]{2,1,0:T(8,128)(2,1)S(1)}, bf16[2,96,768]{2,1,0:T(8,128)(2,1)S(1)}, u32[]{:S(2)}, u32[]{:S(2)}) collective-permute-start(bf16[2,96,768]{2,1,0:T(8,128)(2,1)S(1)} %pad_maximum_fusion.6), channel_id=1, source_target_pairs={{0,8},{4,12},{8,0},{12,4},{16,24},{20,28},{24,16},{28,20},{1,9},{5... | collective-permute-start | bytes 884744 | tf_op jit(solution)/shard_map/ppermute | solution.py:40
  39.5 24.5 %copy-start.17 = (bf16[264,768]{1,0:T(8,128)(2,1)}, bf16[264,768]{1,0:T(8,128)(2,1)S(1)}, u32[]{:S(2)}) copy-start(bf16[264,768]{1,0:T(8,128)(2,1)S(1)} %collective-permute-done.3.refs_5_) | copy-start | bytes 1216516
  39.6 11.3 %collective-permute-start.5 = (bf16[264,768]{1,0:T(8,128)(2,1)S(1)}, bf16[264,768]{1,0:T(8,128)(2,1)S(1)}, u32[]{:S(2)}, u32[]{:S(2)}) collective-permute-start(bf16[264,768]{1,0:T(8,128)(2,1)S(1)} %collective-permute-done.3.refs_5_), channel_id=1, source_target_pairs={{0,1},{1,0},{2,3},{3,2},{4,5},{5,4},{6,7},{7,6},{8,9},{9,8},{10,11... | collective-permute-start | bytes 1216520 | tf_op jit(solution)/shard_map/ppermute | solution.py:40
  39.7 11.2 %collective-permute-start.10 = (bf16[1,120,768]{2,1,0:T(8,128)(2,1)S(1)}, bf16[1,120,768]{2,1,0:T(8,128)(2,1)S(1)}, u32[]{:S(2)}, u32[]{:S(2)}) collective-permute-start(bf16[1,120,768]{2,1,0:T(8,128)(2,1)S(1)} %maximum_bitcast_fusion), channel_id=1, source_target_pairs={{0,16},{4,20},{8,24},{12,28},{16,0},{20,4},{24,8},{28,12},{1,17},{... | collective-permute-start | bytes 552968 | tf_op jit(solution)/shard_map/ppermute | solution.py:40
  42.5 21.5 %collective-permute-start.7 = (bf16[2,96,640]{2,1,0:T(8,128)(2,1)S(1)}, bf16[2,96,640]{2,1,0:T(8,128)(2,1)S(1)}, u32[]{:S(2)}, u32[]{:S(2)}) collective-permute-start(bf16[2,96,640]{2,1,0:T(8,128)(2,1)S(1)} %pad_maximum_fusion.7), channel_id=1, source_target_pairs={{0,8},{4,12},{8,0},{12,4},{16,24},{20,28},{24,16},{28,20},{1,9},{5... | collective-permute-start | bytes 737288 | tf_op jit(solution)/shard_map/ppermute | solution.py:40
  50.8 41.9 %collective-permute-start.2 = (bf16[256,768]{1,0:T(8,128)(2,1)}, bf16[256,768]{1,0:T(8,128)(2,1)}, u32[]{:S(2)}, u32[]{:S(2)}) collective-permute-start(bf16[256,768]{1,0:T(8,128)(2,1)} %collective-permute-done.refs_1_), channel_id=1, source_target_pairs={{0,1},{1,0},{2,3},{3,2},{4,5},{5,4},{6,7},{7,6},{8,9},{9,8},{10,11... | collective-permute-start | bytes 1179656 | tf_op jit(solution)/shard_map/ppermute | solution.py:40
  50.9 19.0 %copy-start.18 = (bf16[264,768]{1,0:T(8,128)(2,1)}, bf16[264,768]{1,0:T(8,128)(2,1)S(1)}, u32[]{:S(2)}) copy-start(bf16[264,768]{1,0:T(8,128)(2,1)S(1)} %collective-permute-done.5.refs_7_) | copy-start | bytes 1216516
  50.9 19.0 %collective-permute-start.11 = (bf16[2,120,768]{2,1,0:T(8,128)(2,1)S(1)}, bf16[2,120,768]{2,1,0:T(8,128)(2,1)S(1)}, u32[]{:S(2)}, u32[]{:S(2)}) collective-permute-start(bf16[2,120,768]{2,1,0:T(8,128)(2,1)S(1)} %pad_maximum_fusion.4), channel_id=1, source_target_pairs={{0,8},{4,12},{8,0},{12,4},{16,24},{20,28},{24,16},{28,20},{1,9},{5... | collective-permute-start | bytes 1105928 | tf_op jit(solution)/shard_map/ppermute | solution.py:40
  53.6 9.9 %collective-permute-start.13 = (bf16[1,8,512]{2,1,0:T(8,128)(2,1)S(1)}, bf16[1,8,512]{2,1,0:T(8,128)(2,1)S(1)}, u32[]{:S(2)}, u32[]{:S(2)}) collective-permute-start(bf16[1,8,512]{2,1,0:T(8,128)(2,1)S(1)} %bitcast.112), channel_id=1, source_target_pairs={{0,16},{4,20},{8,24},{12,28},{16,0},{20,4},{24,8},{28,12},{1,17},{... | collective-permute-start | bytes 24584 | tf_op jit(solution)/shard_map/ppermute | solution.py:40
  54.6 35.4 %copy-start.7 = (bf16[4,96,768]{2,1,0:T(8,128)(2,1)}, bf16[4,96,768]{2,1,0:T(8,128)(2,1)S(1)}, u32[]{:S(2)}) copy-start(bf16[4,96,768]{2,1,0:T(8,128)(2,1)S(1)} %pad_maximum_fusion.1.refs_10_) | copy-start | bytes 1769476
  63.5 29.2 %collective-permute-start.18 = (bf16[4,96,768]{2,1,0:T(8,128)(2,1)S(1)}, bf16[4,96,768]{2,1,0:T(8,128)(2,1)}, u32[]{:S(2)}, u32[]{:S(2)}) collective-permute-start(bf16[4,96,768]{2,1,0:T(8,128)(2,1)S(1)} %pad_maximum_fusion.1.refs_10_), channel_id=1, source_target_pairs={{0,4},{4,0},{8,12},{12,8},{16,20},{20,16},{24,28},{28,24},{1,5},{5... | collective-permute-start | bytes 1769480 | tf_op jit(solution)/shard_map/ppermute | solution.py:40
  64.0 4.0 %collective-permute-start.14 = (bf16[2,8,512]{2,1,0:T(8,128)(2,1)S(1)}, bf16[2,8,512]{2,1,0:T(8,128)(2,1)S(1)}, u32[]{:S(2)}, u32[]{:S(2)}) collective-permute-start(bf16[2,8,512]{2,1,0:T(8,128)(2,1)S(1)} %pad_maximum_fusion.11), channel_id=1, source_target_pairs={{0,8},{4,12},{8,0},{12,4},{16,24},{20,28},{24,16},{28,20},{1,9},{5... | collective-permute-start | bytes 49160 | tf_op jit(solution)/shard_map/ppermute | solution.py:40
  66.4 23.8 %copy-start.11 = (bf16[4,96,640]{2,1,0:T(8,128)(2,1)}, bf16[4,96,640]{2,1,0:T(8,128)(2,1)S(1)}, u32[]{:S(2)}) copy-start(bf16[4,96,640]{2,1,0:T(8,128)(2,1)S(1)} %pad_maximum_fusion.2.refs_8_) | copy-start | bytes 1474564
  68.1 59.6 %collective-permute-start.8 = (bf16[4,96,640]{2,1,0:T(8,128)(2,1)S(1)}, bf16[4,96,640]{2,1,0:T(8,128)(2,1)}, u32[]{:S(2)}, u32[]{:S(2)}) collective-permute-start(bf16[4,96,640]{2,1,0:T(8,128)(2,1)S(1)} %pad_maximum_fusion.2.refs_8_), channel_id=1, source_target_pairs={{0,4},{4,0},{8,12},{12,8},{16,20},{20,16},{24,28},{28,24},{1,5},{5... | collective-permute-start | bytes 1474568 | tf_op jit(solution)/shard_map/ppermute | solution.py:40
  69.9 19.5 %collective-permute-start.15 = (bf16[4,8,512]{2,1,0:T(8,128)(2,1)S(1)}, bf16[4,8,512]{2,1,0:T(8,128)(2,1)S(1)}, u32[]{:S(2)}, u32[]{:S(2)}) collective-permute-start(bf16[4,8,512]{2,1,0:T(8,128)(2,1)S(1)} %pad_maximum_fusion.9), channel_id=1, source_target_pairs={{0,4},{4,0},{8,12},{12,8},{16,20},{20,16},{24,28},{28,24},{1,5},{5... | collective-permute-start | bytes 98312 | tf_op jit(solution)/shard_map/ppermute | solution.py:40
  70.2 36.4 %copy-start.1 = (bf16[4,120,768]{2,1,0:T(8,128)(2,1)}, bf16[4,120,768]{2,1,0:T(8,128)(2,1)S(1)}, u32[]{:S(2)}) copy-start(bf16[4,120,768]{2,1,0:T(8,128)(2,1)S(1)} %pad_maximum_fusion.refs_8_) | copy-start | bytes 2211844
  89.5 17.2 %collective-permute-start.12 = (bf16[4,120,768]{2,1,0:T(8,128)(2,1)S(1)}, bf16[4,120,768]{2,1,0:T(8,128)(2,1)}, u32[]{:S(2)}, u32[]{:S(2)}) collective-permute-start(bf16[4,120,768]{2,1,0:T(8,128)(2,1)S(1)} %pad_maximum_fusion.refs_8_), channel_id=1, source_target_pairs={{0,4},{4,0},{8,12},{12,8},{16,20},{20,16},{24,28},{28,24},{1,5},{5... | collective-permute-start | bytes 2211848 | tf_op jit(solution)/shard_map/ppermute | solution.py:40
  123.7 33.1 %collective-permute-start.28 = (bf16[4,96,768]{2,1,0:T(8,128)(2,1)}, bf16[4,96,768]{2,1,0:T(8,128)(2,1)S(1)}, u32[]{:S(2)}, u32[]{:S(2)}) collective-permute-start(bf16[4,96,768]{2,1,0:T(8,128)(2,1)} %get-tuple-element.47), channel_id=1, source_target_pairs={{0,4},{4,0},{8,12},{12,8},{16,20},{20,16},{24,28},{28,24},{1,5},{5... | collective-permute-start | bytes 1769480 | tf_op jit(solution)/shard_map/ppermute | solution.py:40
  124.1 37.3 %collective-permute-start.25 = (bf16[4,96,768]{2,1,0:T(8,128)(2,1)}, bf16[4,96,768]{2,1,0:T(8,128)(2,1)S(1)}, u32[]{:S(2)}, u32[]{:S(2)}) collective-permute-start(bf16[4,96,768]{2,1,0:T(8,128)(2,1)} %get-tuple-element.45), channel_id=1, source_target_pairs={{0,4},{4,0},{8,12},{12,8},{16,20},{20,16},{24,28},{28,24},{1,5},{5... | collective-permute-start | bytes 1769480 | tf_op jit(solution)/shard_map/ppermute | solution.py:40
  127.6 29.9 %copy-start.9 = (bf16[4,96,768]{2,1,0:T(8,128)(2,1)S(1)}, bf16[4,96,768]{2,1,0:T(8,128)(2,1)}, u32[]{:S(2)}) copy-start(bf16[4,96,768]{2,1,0:T(8,128)(2,1)} %get-tuple-element.46) | copy-start | bytes 1769476
  155.0 6.4 %copy-start.8 = (bf16[4,96,768]{2,1,0:T(8,128)(2,1)S(1)}, bf16[4,96,768]{2,1,0:T(8,128)(2,1)}, u32[]{:S(2)}) copy-start(bf16[4,96,768]{2,1,0:T(8,128)(2,1)} %get-tuple-element.44) | copy-start | bytes 1769476
  155.1 13.9 %collective-permute-start.21 = (bf16[4,104,768]{2,1,0:T(8,128)(2,1)}, bf16[4,104,768]{2,1,0:T(8,128)(2,1)S(1)}, u32[]{:S(2)}, u32[]{:S(2)}) collective-permute-start(bf16[4,104,768]{2,1,0:T(8,128)(2,1)} %get-tuple-element.39), channel_id=1, source_target_pairs={{0,4},{4,0},{8,12},{12,8},{16,20},{20,16},{24,28},{28,24},{1,5},{5... | collective-permute-start | bytes 1916936 | tf_op jit(solution)/shard_map/ppermute | solution.py:40
  156.7 46.7 %collective-permute-start.19 = (bf16[2,2,256,768]{3,2,1,0:T(8,128)(2,1)}, bf16[2,2,256,768]{3,2,1,0:T(8,128)(2,1)}, u32[]{:S(2)}, u32[]{:S(2)}) collective-permute-start(bf16[2,2,256,768]{3,2,1,0:T(8,128)(2,1)} %get-tuple-element.35), channel_id=1, source_target_pairs={{0,1},{1,0},{2,3},{3,2},{4,5},{5,4},{6,7},{7,6},{8,9},{9,8},{10,11... | collective-permute-start | bytes 4718600 | tf_op jit(solution)/shard_map/ppermute | solution.py:40
  156.7 0.8 copy-start.10
  157.6 11.3 %copy-start.4 = (bf16[4,104,768]{2,1,0:T(8,128)(2,1)S(1)}, bf16[4,104,768]{2,1,0:T(8,128)(2,1)}, u32[]{:S(2)}) copy-start(bf16[4,104,768]{2,1,0:T(8,128)(2,1)} %get-tuple-element.38) | copy-start | bytes 1916932
  158.8 12.2 %collective-permute-start.29 = (bf16[2,96,768]{2,1,0:T(8,128)(2,1)S(1)}, bf16[2,96,768]{2,1,0:T(8,128)(2,1)S(1)}, u32[]{:S(2)}, u32[]{:S(2)}) collective-permute-start(bf16[2,96,768]{2,1,0:T(8,128)(2,1)S(1)} %get-tuple-element.52), channel_id=1, source_target_pairs={{0,8},{4,12},{8,0},{12,4},{16,24},{20,28},{24,16},{28,20},{1,9},{5... | collective-permute-start | bytes 884744 | tf_op jit(solution)/shard_map/ppermute | solution.py:40
  161.5 17.2 %collective-permute-start.26 = (bf16[2,96,768]{2,1,0:T(8,128)(2,1)S(1)}, bf16[2,96,768]{2,1,0:T(8,128)(2,1)S(1)}, u32[]{:S(2)}, u32[]{:S(2)}) collective-permute-start(bf16[2,96,768]{2,1,0:T(8,128)(2,1)S(1)} %get-tuple-element.54), channel_id=1, source_target_pairs={{0,8},{4,12},{8,0},{12,4},{16,24},{20,28},{24,16},{28,20},{1,9},{5... | collective-permute-start | bytes 884744 | tf_op jit(solution)/shard_map/ppermute | solution.py:40
  169.1 18.0 %collective-permute-start.22 = (bf16[2,104,768]{2,1,0:T(8,128)(2,1)S(1)}, bf16[2,104,768]{2,1,0:T(8,128)(2,1)S(1)}, u32[]{:S(2)}, u32[]{:S(2)}) collective-permute-start(bf16[2,104,768]{2,1,0:T(8,128)(2,1)S(1)} %get-tuple-element.50), channel_id=1, source_target_pairs={{0,8},{4,12},{8,0},{12,4},{16,24},{20,28},{24,16},{28,20},{1,9},{5... | collective-permute-start | bytes 958472 | tf_op jit(solution)/shard_map/ppermute | solution.py:40
  171.8 40.5 %collective-permute-start.30 = (bf16[1,96,768]{2,1,0:T(8,128)(2,1)}, bf16[1,96,768]{2,1,0:T(8,128)(2,1)}, u32[]{:S(2)}, u32[]{:S(2)}) collective-permute-start(bf16[1,96,768]{2,1,0:T(8,128)(2,1)} %fusion.2), channel_id=1, source_target_pairs={{0,16},{4,20},{8,24},{12,28},{16,0},{20,4},{24,8},{28,12},{1,17},{... | collective-permute-start | bytes 442376 | tf_op jit(solution)/shard_map/ppermute | solution.py:40
  178.8 24.7 %copy-start = (bf16[2,2,256,768]{3,2,1,0:T(8,128)(2,1)S(1)}, bf16[2,2,256,768]{3,2,1,0:T(8,128)(2,1)}, u32[]{:S(2)}) copy-start(bf16[2,2,256,768]{3,2,1,0:T(8,128)(2,1)} %get-tuple-element.34) | copy-start | bytes 4718596
  178.8 16.8 %collective-permute-start.27 = (bf16[1,96,768]{2,1,0:T(8,128)(2,1)S(1)}, bf16[1,96,768]{2,1,0:T(8,128)(2,1)S(1)}, u32[]{:S(2)}, u32[]{:S(2)}) collective-permute-start(bf16[1,96,768]{2,1,0:T(8,128)(2,1)S(1)} %fusion.5), channel_id=1, source_target_pairs={{0,16},{4,20},{8,24},{12,28},{16,0},{20,4},{24,8},{28,12},{1,17},{... | collective-permute-start | bytes 442376 | tf_op jit(solution)/shard_map/ppermute | solution.py:40
  187.9 11.7 %collective-permute-start.23 = (bf16[1,104,768]{2,1,0:T(8,128)(2,1)}, bf16[1,104,768]{2,1,0:T(8,128)(2,1)S(1)}, u32[]{:S(2)}, u32[]{:S(2)}) collective-permute-start(bf16[1,104,768]{2,1,0:T(8,128)(2,1)} %get-tuple-element.56), channel_id=1, source_target_pairs={{0,16},{4,20},{8,24},{12,28},{16,0},{20,4},{24,8},{28,12},{1,17},{... | collective-permute-start | bytes 479240 | tf_op jit(solution)/shard_map/ppermute | solution.py:40
  196.3 12.5 %all-to-all-start.2 = ((bf16[4,24,768]{2,1,0:T(8,128)(2,1)}), bf16[4,24,768]{2,1,0:T(8,128)(2,1)S(1)}, u32[]{:S(2)}, u32[]{:S(2)}) async-start(bf16[4,24,768]{2,1,0:T(8,128)(2,1)} %bitcast.45), calls=%async_computation.2 | async-start | bytes 294912 | tf_op jit(solution)/shard_map/all_to_all | solution.py:644
  199.7 0.7 copy-start.14
  202.1 13.6 %collective-permute-start.24 = (bf16[24,768]{1,0:T(8,128)(2,1)}, bf16[24,768]{1,0:T(8,128)(2,1)S(1)}, u32[]{:S(2)}, u32[]{:S(2)}) collective-permute-start(bf16[24,768]{1,0:T(8,128)(2,1)} %get-tuple-element.43), channel_id=1, source_target_pairs={{0,0},{4,1},{8,2},{12,3},{16,4},{20,5},{24,6},{28,7},{1,8},{5,9},{... | collective-permute-start | bytes 110600 | tf_op jit(solution)/shard_map/ppermute | solution.py:66
  206.4 28.7 %collective-permute-start.20 = (bf16[1,2,256,768]{3,2,1,0:T(8,128)(2,1)S(1)}, bf16[1,2,256,768]{3,2,1,0:T(8,128)(2,1)S(1)}, u32[]{:S(2)}, u32[]{:S(2)}) collective-permute-start(bf16[1,2,256,768]{3,2,1,0:T(8,128)(2,1)S(1)} %get-tuple-element.48), channel_id=1, source_target_pairs={{0,2},{1,3},{2,0},{3,1},{4,6},{5,7},{6,4},{7,5},{8,10},{9,11},{10,... | collective-permute-start | bytes 2359304 | tf_op jit(solution)/shard_map/ppermute | solution.py:40
  208.9 5.1 %copy-start.6 = (bf16[4,24,768]{2,1,0:T(8,128)(2,1)}, bf16[4,24,768]{2,1,0:T(8,128)(2,1)S(1)}, u32[]{:S(2)}) copy-start(bf16[4,24,768]{2,1,0:T(8,128)(2,1)S(1)} %all-to-all-done.2.parts) | copy-start | bytes 442372
  208.9 20.0 %all-to-all-start.1 = ((bf16[4,32,768]{2,1,0:T(8,128)(2,1)}), bf16[4,32,768]{2,1,0:T(8,128)(2,1)S(1)}, u32[]{:S(2)}, u32[]{:S(2)}) async-start(bf16[4,32,768]{2,1,0:T(8,128)(2,1)} %get-tuple-element.40), calls=%async_computation.1 | async-start | bytes 393216 | tf_op jit(solution)/shard_map/all_to_all | solution.py:654
  228.8 0.7 copy-start.2
  232.6 6.7 %copy-start.16 = (f32[24]{0:T(128)}, f32[24]{0:T(128)S(1)}, u32[]{:S(2)}) copy-start(f32[24]{0:T(128)S(1)} %get-tuple-element.103) | copy-start | bytes 292
  235.0 0.9 copy-start.3

commit v2 on v1

--- a/solution.py
+++ b/solution.py
@@ -12,6 +12,7 @@
 HD = 64
 ROT = 16
 LANES = 128
+SPLITS = 2
 NORM_EPS = 1e-05
 BF = jnp.bfloat16
 F32 = jnp.float32
@@ -28,11 +29,16 @@
     return out
 
 
-def cube_order(count):
+def cube_order(bits):
     order = [0]
-    for bit in reversed(bits_of(count)):
+    for bit in reversed(bits):
         order = order + [k ^ bit for k in order]
     return order
+
+
+def side_first(count):
+    bits = bits_of(count)
+    return [bits[1], bits[0], *bits[2:]]
 
 
 def swap(value, axis, bit):
@@ -40,9 +46,9 @@
     return lax.ppermute(value, axis, [(i, i ^ bit) for i in range(count)])
 
 
-def halves(block, axis):
+def halves(block, axis, bits):
     mine, got = None, block[None]
-    for bit in reversed(bits_of(lax.axis_size(axis))):
+    for bit in reversed(bits):
         mine = got if mine is None else jnp.concatenate([mine, got], axis=0)
         got = swap(mine, axis, bit)
     return mine, got
@@ -66,8 +72,8 @@
     return lax.ppermute(value, ("dp", "sp"), perm)
 
 
-def cube_scatter(keep, send, axis):
-    for bit in bits_of(lax.axis_size(axis)):
+def cube_scatter(keep, send, axis, bits):
+    for bit in bits:
         got = swap(send, axis, bit)
         half = keep.shape[0] // 2
         if half:
@@ -119,23 +125,23 @@
     return out
 
 
-def placed(ids, mine, got, target, rows, width, sem):
+def placed(ids, mine, got, target, rows, width, sem, first=0):
     out = []
     half = mine.shape[0]
     for p in range(2 * half):
         source = mine.at[p] if p < half else got.at[p - half]
         if source.shape != (rows, width):
             source = source.at[pl.ds(0, rows), pl.ds(0, width)]
-        to = pl.multiple_of(ids[p] * rows, 8)
+        to = pl.multiple_of(ids[first + p] * rows, 8)
         out.append(pltpu.make_async_copy(source, target.at[pl.ds(to, rows)], sem.at[p]))
     return out
 
 
-def sent(ids, source, keep, send, rows, sem):
+def sent(ids, source, keep, send, rows, sem, first=0):
     todo = []
     half = keep.shape[0]
     for p in range(2 * half):
-        at = pl.multiple_of(ids[p] * rows, 8)
+        at = pl.multiple_of(ids[first + p] * rows, 8)
         to = keep.at[p] if p < half else send.at[p - half]
         if to.shape[0] != rows:
             to = to.at[pl.ds(0, rows)]
@@ -162,25 +168,51 @@
         out[at, : right.shape[1]] = dot(left[:, at], right[...], 0, 0).astype(BF)
 
 
-def mlp_kernel(sp, ids, *refs):
+def unpack(sp, me, small, row_n, own_b, vecs, eadd, jadd):
+    dp = small.shape[0]
+    ff_n = eadd.shape[1] // dp
+    for d in range(dp):
+        block = small[d].astype(F32)
+        for s in range(sp):
+            at = (d * sp + s) * row_n
+            vecs[:, at : at + row_n] = block[:, s * LANES : s * LANES + row_n]
+        lanes = pl.ds(pl.multiple_of(me * LANES, LANES), LANES)
+        mine = small[d, :, lanes].astype(F32)
+        eadd[:, d * ff_n : (d + 1) * ff_n] = mine[2:3, :ff_n]
+    for i in range(dp // sp):
+        block = small[me * (dp // sp) + i].astype(F32)
+        for s in range(sp):
+            at = (i * sp + s) * own_b
+            jadd[0:1, at : at + own_b] = block[0:1, s * LANES : s * LANES + own_b]
+
+
+def mlp_kernel(sp, row_n, own_b, ids, *refs):
     xs, cots = refs[:sp], refs[sp : 2 * sp]
-    ew_mine, ew_got, sw_mine, sw_got, vec = refs[2 * sp : 2 * sp + 5]
-    outs = refs[2 * sp + 5 : 2 * sp + 12]
-    eg_keep, eg_send, sg_keep, sg_send, out_part, in_part, sums = outs
-    x, cot, ew, sw, hid, act, pgr, eg, sg, sem = refs[2 * sp + 12 :]
+    ew_mine, ew_got, sw_mine, sw_got = refs[2 * sp : 2 * sp + 4]
+    outs = refs[2 * sp + 4 : 2 * sp + 13]
+    eg_keep, eg_send, sg_keep, sg_send, out_part, in_part, sums, vecs, jadd = outs
+    x, cot, ew, sw, hid, act, pgr, eg, sg, small, eadd, sem = refs[2 * sp + 13 :]
     width = x.shape[1]
     chunk = x.shape[0] // sp
     rows, units = eg_keep.shape[1], sg_keep.shape[1]
+    half = ew_mine.shape[0]
+    side = 2 * half + sp + 1
     gets = (
         copies_in([b.at[pl.ds(0, chunk)] for b in xs], x, chunk, sem.at[0])
         + copies_in([b.at[pl.ds(0, chunk)] for b in cots], cot, chunk, sem.at[1])
         + placed(ids, ew_mine, ew_got, ew, rows, ew.shape[1], sem.at[2])
         + placed(ids, sw_mine, sw_got, sw, units, width, sem.at[3])
     )
+    for p in range(2 * half):
+        block = ew_mine.at[p] if p < half else ew_got.at[p - half]
+        block = block.at[pl.ds(ew_mine.shape[1] - 8, 8)]
+        gets.append(pltpu.make_async_copy(block, small.at[ids[p]], sem.at[4, p]))
     run(gets)
     sums[...] = jnp.zeros_like(sums)
+    jadd[...] = jnp.zeros_like(jadd)
     finish(gets)
-    gain, shift, add = vec[0:1, :], vec[1:2, :], vec[2:3, : ew.shape[1]]
+    unpack(sp, ids[2 * half + sp], small, row_n, own_b, vecs, eadd, jadd)
+    gain, shift, add = vecs[6:7, :], vecs[7:8, :], eadd[...]
 
     @pl.loop(0, sp)
     def _(k):
@@ -204,7 +236,7 @@
         in_part[k] = (hidden_grad * gain).astype(BF)
 
     grad_rows(hid, pgr, eg)
-    puts = sent(ids, eg, eg_keep, eg_send, rows, sem.at[0])
+    puts = sent(ids, eg, eg_keep, eg_send, rows, sem.at[0], side)
     run(puts)
     grad_rows(act, cot, sg)
     more = sent(ids, sg, sg_keep, sg_send, units, sem.at[1])
@@ -214,9 +246,10 @@
 
 def attn_kernel(sp, seqs, heads, ids, *refs):
     xs, cots = refs[:sp], refs[sp : 2 * sp]
-    jw_mine, jw_got, dw, vec, jadd, cos_ref, sin_ref, posc, posr = refs[2 * sp : 2 * sp + 9]
-    out_part, in_part, m_sums, g_keep, g_send, keep, send = refs[2 * sp + 9 : 2 * sp + 16]
-    x, cot, jw, hid, rot, cg, ctx, jgf, jgb, ctk, gr, sums, small, sem = refs[2 * sp + 16 :]
+    jw_mine, jw_got, dw, cos_ref, sin_ref = refs[2 * sp : 2 * sp + 5]
+    out_part, in_part, m_sums, vecs, jadd = refs[2 * sp + 5 : 2 * sp + 10]
+    g_keep, g_send, keep, send = refs[2 * sp + 10 : 2 * sp + 14]
+    x, cot, jw, hid, rot, cg, ctx, jgf, jgb, ctk, gr, sums, small, sem = refs[2 * sp + 14 :]
     width = x.shape[1]
     wide = jw.shape[1]
     cols = heads * 3 * HD
@@ -236,7 +269,7 @@
     sums[...] = jnp.zeros_like(sums)
     jgf[:, cols:] = jnp.zeros((jgf.shape[0], wide - cols), F32)
     finish(gets)
-    gain, shift = vec[0:1, :], vec[1:2, :]
+    gain, shift = vecs[4:5, :], vecs[5:6, :]
 
     def tables(g, k):
         at = pl.ds(pl.multiple_of(k * part, part), part)
@@ -258,11 +291,12 @@
 
     def spread(ref, k, lanes, value):
         for b in range(seqs):
-            at = pl.ds(pl.multiple_of(b * full + k * part, part), part)
+            at = pl.ds(pl.multiple_of(b * full + ids[2 * half + k] * part, part), part)
             ref[at, lanes] = value[b * part : (b + 1) * part]
 
     def collect(ref, k, lanes):
-        at = [pl.ds(pl.multiple_of(b * full + k * part, part), part) for b in range(seqs)]
+        row = ids[2 * half + k] * part
+        at = [pl.ds(pl.multiple_of(b * full + row, part), part) for b in range(seqs)]
         return jnp.concatenate([ref[a, lanes] for a in at], axis=0)
 
     @pl.loop(0, sp)
@@ -271,34 +305,51 @@
         normed, _ = layer_norm(x[at, :].astype(F32))
         hidden = (normed * gain + shift).astype(BF)
         hid[at, :] = hidden
-        joined = dot(hidden, jw[...], 1, 0) + jadd[...]
+        joined = dot(hidden, jw[...], 1, 0) + jadd[0:1, :]
         for g in range(wide // LANES):
             lanes = slice(g * LANES, (g + 1) * LANES)
             spread(rot, k, lanes, rotate(joined[:, lanes], g, k, 1.0).astype(BF))
         spread(cg, k, slice(None), dot(cot[at, :], dw[...], 1, 1).astype(BF))
 
-    allowed = posc[...] >= posr[...]
+    step = full // SPLITS
+    row = lax.broadcasted_iota(jnp.int32, (step, step), 0)
+    allowed = row <= lax.broadcasted_iota(jnp.int32, (step, step), 1)
+
+    def stripe(b, i):
+        at = pl.ds(pl.multiple_of(b * full + i * step, step), step)
+        seen = pl.ds(pl.multiple_of(b * full, full), (i + 1) * step)
+        every = range(heads)
+        starts = [h * 3 * HD for h in every]
+        query = [(rot[at, q : q + HD].astype(F32) * scale).astype(BF) for q in starts]
+        key = [rot[seen, q + HD : q + 2 * HD] for q in starts]
+        value = [rot[seen, q + 2 * HD : q + 3 * HD] for q in starts]
+        grad = [cg[at, h * HD : (h + 1) * HD] for h in every]
+        scores = [dot(key[h], query[h], 1, 1) for h in every]
+        weight_grad = [dot(value[h], grad[h], 1, 1) for h in every]
+        for h in every:
+            last = jnp.where(allowed, scores[h][i * step :], -jnp.inf)
+            scores[h] = jnp.concatenate([scores[h][: i * step], last], axis=0) if i else last
+        total = [row_sum(jnp.exp(scores[h])) for h in every]
+        probs = [jnp.exp(scores[h] - jnp.log(total[h])) for h in every]
+        weights = [probs[h].astype(BF) for h in every]
+        context = [dot(value[h], weights[h], 0, 0) for h in every]
+        delta = [row_sum(grad[h].astype(F32).T * context[h]) for h in every]
+        inner = [(probs[h] * (weight_grad[h] - delta[h])).astype(BF) for h in every]
+        for h in every:
+            q = starts[h]
+            ctx[at, h * HD : (h + 1) * HD] = context[h].T.astype(BF)
+            jgf[at, q : q + HD] = dot(key[h], inner[h], 0, 0).T * scale
+            both = [dot(inner[h], query[h], 1, 0), dot(weights[h], grad[h], 1, 0)]
+            both = jnp.concatenate(both, axis=1)
+            if i == SPLITS - 1:
+                jgf[seen, q + HD : q + 3 * HD] = both
+            else:
+                jgf[seen, q + HD : q + 3 * HD] += both
 
     @pl.loop(0, seqs)
     def _(b):
-        at = pl.ds(pl.multiple_of(b * full, full), full)
-        for h in range(heads):
-            q0 = h * 3 * HD
-            query = rot[at, q0 : q0 + HD]
-            key = rot[at, q0 + HD : q0 + 2 * HD]
-            value = rot[at, q0 + 2 * HD : q0 + 3 * HD]
-            grad = cg[at, h * HD : (h + 1) * HD]
-            scores = dot(query, key, 1, 1) * scale
-            total = jnp.sum(jnp.where(allowed, jnp.exp(scores), 0.0), axis=-1, keepdims=True)
-            probs = jnp.where(allowed, jnp.exp(scores - jnp.log(total)), 0.0)
-            weights = probs.astype(BF)
-            context = dot(weights, value, 1, 0)
-            ctx[at, h * HD : (h + 1) * HD] = context.astype(BF)
-            delta = jnp.sum(grad.astype(F32) * context, axis=-1, keepdims=True)
-            jgf[at, q0 + 2 * HD : q0 + 3 * HD] = dot(weights, grad, 0, 0)
-            score_grad = (probs * (dot(grad, value, 1, 1) - delta) * scale).astype(BF)
-            jgf[at, q0 : q0 + HD] = dot(score_grad, key, 1, 0)
-            jgf[at, q0 + HD : q0 + 2 * HD] = dot(score_grad, query, 0, 0)
+        for i in reversed(range(SPLITS)):
+            stripe(b, i)
 
     @pl.loop(0, sp)
     def _(k):
@@ -372,7 +423,8 @@
     return call(body, args, specs, outs, [IN_VMEM] * len(outs), [], 0)
 
 
-def split_weights(sp, dp, expand, joined, out):
+def split_weights(sp, dp, expand, joined, *refs):
+    vectors, out = refs[:-1], refs[-1]
     rows = expand.shape[0]
     each = expand.shape[1] // (sp * dp)
     cols = joined.shape[1] // sp
@@ -380,51 +432,63 @@
         for d in range(dp):
             at = (d * sp + s) * each
             out[s, :rows, d * each : (d + 1) * each] = expand[:, at : at + each]
-        out[s, rows:, :cols] = joined[:, s * cols : (s + 1) * cols]
-        out[s, rows:, cols:] = jnp.zeros((rows, out.shape[2] - cols), out.dtype)
-
-
-def split_grads(sp, cols, keep, got, last, dense):
+        out[s, rows : 2 * rows, :cols] = joined[:, s * cols : (s + 1) * cols]
+        out[s, rows : 2 * rows, cols:] = jnp.zeros((rows, out.shape[2] - cols), out.dtype)
+        out[s, 2 * rows :, :] = jnp.zeros((8, out.shape[2]), out.dtype)
+        for i, vector in enumerate(vectors):
+            out[s, 2 * rows + i : 2 * rows + i + 1, : vector.shape[0]] = vector[...][None, :]
+
+
+def pack_weights(wide, both, pack, joined):
+    sp = both.shape[0]
+    rows = joined.shape[0] // sp
+    pack[sp * rows :, :] = jnp.zeros((8, pack.shape[1]), pack.dtype)
+    for s in range(sp):
+        pack[s * rows : (s + 1) * rows, :] = both[s, :rows]
+        joined[s * rows : (s + 1) * rows, :] = both[s, rows : 2 * rows, :wide]
+        pack[sp * rows :, s * LANES : (s + 1) * LANES] = both[s, 2 * rows :, :LANES]
+
+
+def split_grads(sp, cols, keep, got, e_keep, e_got, last, dense):
     value = (keep[...] + got[...].astype(F32)).astype(BF)
+    expand = (e_keep[...] + e_got[...].astype(F32)).astype(BF)
     rows = value.shape[0] - 8
     per = rows // sp
     lanes = value.shape[1] - cols
     for s in range(sp):
         last[s, :per] = value[s * per : (s + 1) * per]
-        last[s, per:] = value[rows:]
+        last[s, per : 2 * per] = expand[s * per : (s + 1) * per]
+        last[s, 2 * per :] = value[rows:]
         dense[:, s * lanes : (s + 1) * lanes] = value[s * per : (s + 1) * per, cols:]
 
 
-def join_grads(sp, cols, at, last, out, small):
+def join_grads(sp, dp, cols, at, last, out, expand, *vectors):
     per = out.shape[0]
     width = last.shape[2]
+    each = width // dp
     total = jnp.zeros((8, width), F32)
     joined = jnp.zeros((8, width), F32)
     for s in range(sp):
         out[:, s * cols : (s + 1) * cols] = last[s, :per, :cols].astype(F32)
-        block = last[s, per:].astype(F32)
+        for d in range(dp):
+            to = (d * sp + s) * each
+            expand[:, to : to + each] = last[s, per : 2 * per, d * each : (d + 1) * each].astype(F32)
+        block = last[s, 2 * per :].astype(F32)
         total = total + block
         joined = joined + jnp.where(at[0] == s, block, 0.0)
-    row = lax.broadcasted_iota(jnp.int32, (8, LANES), 0)
-    mine = last[at[4], per:].astype(F32)
+    mine = last[at[4], 2 * per :].astype(F32)
     sums = pltpu.roll(total, at[1], 1)[:, :LANES]
     joined = pltpu.roll(joined, at[2], 1)[:, :LANES]
     mine = pltpu.roll(mine, at[3], 1)[:, :LANES]
-    small[...] = jnp.where(row < 5, sums, jnp.where(row == 5, joined, mine))
-
-
-def join_expand(sp, dp, parts, out):
-    each = parts.shape[2] // dp
-    for s in range(sp):
-        for d in range(dp):
-            at = (d * sp + s) * each
-            out[:, at : at + each] = parts[s, :, d * each : (d + 1) * each].astype(F32)
+    for i, vector in enumerate(vectors):
+        source = (sums,) * 5 + (joined, mine, sums)
+        vector[...] = source[i][i if i < 7 else 4, : vector.shape[0]]
 
 
 def finish_tokens(x, cot, keep, got, add, out, grad):
     rows = x[...].astype(F32)
     sums = keep[...].astype(F32) + got[...].astype(F32)
-    out[...] = (rows + sums[0] + add[...]).astype(BF)
+    out[...] = (rows + sums[0] + (add[1:2, :] + add[3:4, :])).astype(BF)
     scaled = sums[1]
     normed, inv = layer_norm(rows)
     first = jnp.mean(scaled, axis=-1, keepdims=True)
@@ -432,11 +496,11 @@
     grad[...] = cot[...].astype(F32) + inv * (scaled - first - normed * second)
 
 
-def attention(ids, xs, cots, jw, dw, vec, jadd, tables, poss, parts, seqs, heads):
+def attention(ids, xs, cots, jw, dw, tables, parts, seqs, heads):
     sp = len(xs)
     chunk, width = parts[0].shape[1:]
     tokens = sp * chunk
-    wide = jadd.shape[1]
+    wide = jw[0].shape[2]
     dp = 2 * jw[0].shape[0]
     rows = width // dp
     shape = jax.ShapeDtypeStruct
@@ -464,8 +528,8 @@
     ]
     return call(
         functools.partial(attn_kernel, sp, seqs, heads),
-        [ids, *xs, *cots, *jw, dw, vec, jadd, *tables, *poss, *parts],
-        [IN_SMEM] + [ANY] * (2 * sp + 2) + [IN_VMEM] * 10,
+        [ids, *xs, *cots, *jw, dw, *tables, *parts],
+        [IN_SMEM] + [ANY] * (2 * sp + 2) + [IN_VMEM] * 8,
         outs,
         [ANY, ANY, IN_VMEM, IN_VMEM],
         scratch,
@@ -473,13 +537,13 @@
     )
 
 
-def feed_forward(ids, xs, cots, ew, sw, vec, chunk):
+def feed_forward(ids, xs, cots, ew, sw, row_n, own_b, wide):
     sp = len(xs)
-    width = xs[0].shape[1]
+    chunk, width = xs[0].shape
     tokens = sp * chunk
     units = ew[0].shape[2]
     dp = 2 * ew[0].shape[0]
-    rows, per = width // dp, sw[0].shape[1]
+    rows, per = width // dp, units // dp
     shape = jax.ShapeDtypeStruct
     outs = [
         shape((dp // 2, rows, units), BF),
@@ -489,6 +553,8 @@
         shape((sp, chunk, width), BF),
         shape((sp, chunk, width), BF),
         shape((8, width), F32),
+        shape((8, width), F32),
+        shape((8, wide), F32),
     ]
     scratch = [
         pltpu.VMEM((tokens, width), BF),
@@ -500,14 +566,16 @@
         pltpu.VMEM((tokens, units), BF),
         pltpu.VMEM((width, units), BF),
         pltpu.VMEM((units, width), BF),
-        pltpu.SemaphoreType.DMA((4, max(dp, sp))),
+        pltpu.VMEM((dp, 8, width), BF),
+        pltpu.VMEM((1, units), F32),
+        pltpu.SemaphoreType.DMA((5, max(dp, sp))),
     ]
     return call(
-        functools.partial(mlp_kernel, sp),
-        [ids, *xs, *cots, *ew, *sw, vec],
-        [IN_SMEM] + [ANY] * (2 * sp + 4) + [IN_VMEM],
+        functools.partial(mlp_kernel, sp, row_n, own_b),
+        [ids, *xs, *cots, *ew, *sw],
+        [IN_SMEM] + [ANY] * (2 * sp + 4),
         outs,
-        [ANY, ANY, ANY, ANY, IN_VMEM, IN_VMEM, IN_VMEM],
+        [ANY, ANY, ANY, ANY] + [IN_VMEM] * 5,
         scratch,
         20 * tokens * width * units,
     )
@@ -540,16 +608,13 @@
     rows_d = row_n * sp
     ff_n = shrink_weight.shape[0]
     units = ff_n * dp
-    sp_order, dp_order = cube_order(sp), cube_order(dp)
-    ids = jnp.asarray(dp_order, jnp.int32) ^ dp_me
-
-    shape = jax.ShapeDtypeStruct
-    split = functools.partial(split_weights, sp, dp)
-    outs = [shape((sp, 2 * row_n, units), BF)]
-    (both,) = tidy(split, [expand_weight, joined_weight], outs)
-    both = lax.all_to_all(both, "sp", split_axis=0, concat_axis=0, tiled=True)
-    expand_part = both[:, :row_n].reshape(rows_d, units)
-    joined_part = both[:, row_n:, :wide].reshape(rows_d, wide)
+    sp_order = cube_order(bits_of(sp))
+    dp_order, side_order = cube_order(bits_of(dp)), cube_order(side_first(dp))
+    nat = jnp.asarray(sp_order, jnp.int32) ^ me
+    near = jnp.asarray(dp_order, jnp.int32) ^ dp_me
+    side = jnp.asarray(side_order, jnp.int32) ^ dp_me
+    ids = jnp.concatenate([near, nat, me[None], side])
+    own_b = joined_bias.shape[0]
 
     small_parts = (
         joined_bias,
@@ -561,52 +626,40 @@
         mlp_gain,
         mlp_shift,
     )
-    sizes = [part.shape[0] for part in small_parts]
-    row = jnp.arange(8, dtype=jnp.int32)[:, None]
-    small = jnp.zeros((8, width), BF)
-    for i, part in enumerate(small_parts):
-        small = jnp.where(row == i, jnp.pad(part, (0, width - part.shape[0]))[None], small)
+    shape = jax.ShapeDtypeStruct
+    (both,) = tidy(
+        functools.partial(split_weights, sp, dp),
+        [expand_weight, joined_weight, *small_parts],
+        [shape((sp, 2 * row_n + 8, units), BF)],
+    )
+    both = lax.all_to_all(both, "sp", split_axis=0, concat_axis=0, tiled=True)
+    dense_part = transposed(dense_weight, False)
+    expand_pack, joined_part = tidy(
+        functools.partial(pack_weights, wide),
+        [both],
+        [shape((rows_d + 8, units), BF), shape((rows_d, wide), BF)],
+    )
+
     xs = token_blocks(inputs.reshape(local, width), "sp")
-    cots = token_blocks(jnp.concatenate([cotangent.reshape(local, width), small]), "sp")
-    small = jnp.stack([block[local:, :LANES] for block in cots])
-    small = flip_bits(turn_bits(small), "sp").transpose(1, 0, 2).reshape(8, sp * LANES)
-    small = halves(small, "dp")
-    small = flip_bits(turn_bits(jnp.concatenate(small, axis=0)), "dp")
-    small = small.reshape(dp, 8, sp, LANES).astype(F32)
-
-    dense_part = transposed(dense_weight, False)
-    shrink_w = halves(shrink_weight, "dp")
-    expand_w = halves(jnp.concatenate([expand_part, dense_part]), "dp")
-    joined_w = halves(joined_part, "dp")
-
-    dense_w = jnp.concatenate([half[:, rows_d:] for half in expand_w], axis=0)
+    cots = token_blocks(cotangent.reshape(local, width), "sp")
+    shrink_w = halves(shrink_weight, "dp", bits_of(dp))
+    expand_w = halves(expand_pack, "dp", bits_of(dp))
+    joined_w = halves(joined_part, "dp", bits_of(dp))
+    dense_w = jnp.concatenate(halves(dense_part, "dp", bits_of(dp)), axis=0)
     dense_w = flip_bits(turn_bits(dense_w), "dp").reshape(heads * HD, width)
-
-    def whole(index):
-        return small[:, index, :, : sizes[index]].reshape(-1)
-
-    joined_add = lax.dynamic_slice_in_dim(whole(0), me * cols, cols)
-    out_add = whole(1) + whole(3)
-    expand_add = lax.dynamic_index_in_dim(small[:, 2], me, 1, keepdims=False)[:, : sizes[2]]
-
-    def stacked(vectors):
-        vectors = [jnp.pad(v.reshape(-1), (0, width - v.size)) for v in vectors]
-        return jnp.stack(vectors + [jnp.zeros((width,), F32)] * (8 - len(vectors)))
-
-    starts = (jnp.asarray(sp_order, jnp.int32) ^ me) * local_len
-    pos = (starts[:, None] + jnp.arange(local_len, dtype=jnp.int32)).reshape(-1)
+    pos = (nat[:, None] * local_len + jnp.arange(local_len, dtype=jnp.int32)).reshape(-1)
     lane = jnp.arange(LANES, dtype=jnp.int32) % (ROT // 2)
     freq = 1.0 / 10000.0 ** ((2 * lane).astype(F32) / ROT)
     angles = pos.astype(F32)[:, None] * freq[None, :]
-    joined_row = jnp.pad(joined_add, (0, wide - cols))[None]
     e_keep, e_send, s_keep, s_send, *parts = feed_forward(
         ids,
         xs,
         cots,
         expand_w,
         shrink_w,
-        stacked([whole(6), whole(7), expand_add]),
-        local,
+        row_n,
+        own_b,
+        wide,
     )
     a_keep, a_send, keep, send = attention(
         ids,
@@ -614,16 +667,13 @@
         cots,
         joined_w,
         dense_w,
-        stacked([whole(4), whole(5)]),
-        joined_row,
         (jnp.cos(angles), jnp.sin(angles)),
-        (pos[:, None], pos[None, :]),
         parts,
         seqs,
         heads,
     )
 
-    keep, got = cube_scatter(keep, send, "sp")
+    keep, got = cube_scatter(keep, send, "sp", bits_of(sp))
     output, input_grad = tidy(
         finish_tokens,
         [
@@ -631,51 +681,46 @@
             cotangent.reshape(local, width),
             keep,
             got,
-            out_add[None],
+            parts[3],
         ],
         [shape((local, width), BF), shape((local, width), F32)],
     )
     output, input_grad = output.reshape(inputs.shape), input_grad.reshape(inputs.shape)
 
-    keep, got = cube_scatter(s_keep, s_send, "dp")
+    keep, got = cube_scatter(s_keep, s_send, "dp", bits_of(dp))
     shrink_g = keep + got.astype(F32)
-    keep, got = cube_scatter(e_keep, e_send, "dp")
-    expand_g = (keep + got.astype(F32)).astype(BF).reshape(sp, row_n, units)
-    expand_g = lax.all_to_all(expand_g, "sp", split_axis=0, concat_axis=0, tiled=True)
-    (expand_g,) = tidy(
-        functools.partial(join_expand, sp, dp), [expand_g], [shape(expand_weight.shape, F32)]
-    )
-    keep, got = cube_scatter(a_keep, a_send, "dp")
+    keep, got = cube_scatter(e_keep, e_send, "dp", side_first(dp))
+    expands = (keep, got)
+    keep, got = cube_scatter(a_keep, a_send, "dp", bits_of(dp))
     last, dense_g = tidy(
         functools.partial(split_grads, sp, cols),
-        [keep, got],
-        [shape((sp, row_n + 8, width), BF), shape((row_n, width), BF)],
+        [keep, got, *expands],
+        [shape((sp, 2 * row_n + 8, width), BF), shape((row_n, width), BF)],
     )
     last = lax.all_to_all(last, "sp", split_axis=0, concat_axis=0, tiled=True)
     dense_g = transposed(dense_g, True)
-    own_b = joined_bias.shape[0]
     linear = dp_me * sp + me
     holder = linear * own_b // cols
     starts = [linear * row_n, linear * own_b - holder * cols, dp_me * ff_n]
     at = [holder] + [(width - start) % width for start in starts] + [me]
-    joined_g, small_g = tidy(
-        functools.partial(join_grads, sp, cols),
+    joined_g, expand_g, *vectors = tidy(
+        functools.partial(join_grads, sp, dp, cols),
         [jnp.stack(at).astype(jnp.int32), last],
-        [shape(joined_weight.shape, F32), shape((8, LANES), F32)],
-    )
-    joined_bg, expand_bg = small_g[5, :own_b], small_g[6, :ff_n]
-    gain_ag, shift_ag, gain_bg, shift_bg, out_bg = [small_g[i, :row_n] for i in range(5)]
+        [shape(joined_weight.shape, F32), shape(expand_weight.shape, F32)]
+        + [shape((n,), F32) for n in [row_n] * 5 + [own_b, ff_n, row_n]],
+    )
+    gain_ag, shift_ag, gain_bg, shift_bg, dense_bg, joined_bg, expand_bg, shrink_bg = vectors
     return (
         output,
         input_grad,
         joined_g,
         joined_bg,
         dense_g.astype(F32),
-        out_bg,
+        dense_bg,
         expand_g,
         expand_bg,
         shrink_g,
-        out_bg,
+        shrink_bg,
         gain_ag,
         shift_ag,
         gain_bg,

time: 241 us -> 219 us (0.909)
  local copies, waits for them, and re-layouts: 18.7 us -> 5.33 us
  waiting for transfers between devices: 107 us -> 100 us
  other arithmetic: 14.5 us -> 9.21 us
  starting transfers between devices: 43.4 us -> 47.3 us
  Pallas kernels: 54.8 us -> 52.3 us
    all_to_all x1, waiting for transfers between devices: 12.5 us -> 3.35 us  [on_device(): last = lax.all_to_all(last, 'sp', split_axis=0, concat_axis=0, tiled=True)]
    ppermute x29, starting transfers between devices: 31.1 us -> 37.6 us  [swap(): return lax.ppermute(value, axis, [(i, i ^ bit) for i in range(count)])]
    pad x9 -> x0, local copies, waits for them, and re-layouts: 5.36 us -> none  [the longest x8 5.36 us: on_device(): jnp.pad(part, (0, width - part.shape[0]))[None]]
    squeeze x3 -> x0, local copies, waits for them, and re-layouts: 3.8 us -> none  [the longest x2 2.4 us: on_device(): joined_bg, expand_bg = (small_g[5, :own_b], small_g[6, :ff_n])]
    all_to_all x1 -> x0, starting transfers between devices: 3.34 us -> none  [on_device(): lax.all_to_all(expand_g, 'sp', split_axis=0, concat_axis=0, tiled=True)]
    pallas_call x7, Pallas kernels: 54.8 us -> 52.3 us  [call(): pl.pallas_call(body, in_specs=specs, out_shape=outs, out_specs=out_specs,...]
    convert_element_type x7, other arithmetic: 5.94 us -> 3.5 us  [cube_scatter(): send = (keep[half:].astype(F32) + got[half:].astype(F32)).astype(BF)]
  transfers between devices with their start and end apart: 34 -> 33, of which waited for: 12 -> 13; matrix products, arithmetic and copies ran while one was open for 10% -> 5% of each run, Pallas kernels for 21% -> 23%
where the time goes in v2:
time: 219 us; the launch traced here: 216 us
  waiting for transfers between devices  100 us (46%)
  Pallas kernels  52.3 us (24%)
  starting transfers between devices  47.3 us (22%)
  other arithmetic  9.21 us (4%)
  local copies, waits for them, and re-layouts  5.33 us (2%)
    ppermute x29, waiting for transfers between devices, swap(): return lax.ppermute(value, axis, [(i, i ^ bit) for i in range(count)])  97 us
    pallas_call x7, Pallas kernels, call(): pl.pallas_call(body, in_specs=specs, out_shape=outs, out_specs=out_specs,...  52.3 us
    ppermute x29, starting transfers between devices, swap(): return lax.ppermute(value, axis, [(i, i ^ bit) for i in range(count)])  37.6 us
    unnamed x50, local copies, waits for them, and re-layouts  4.71 us
  transfers between devices with their start and end apart: 33, of which 13 were waited for; matrix products, arithmetic and copies ran while one was open for 5% of the time, Pallas kernels for 23%

profile of v2, /device:TPU:0, one launch (start us, length us, event | category | flops | bytes accessed | tf_op | source)
XLA Modules:
  0.0 215.6 jit_solution(5901422256215579491)
XLA Ops:
  0.7 3.1 %collective-permute-start = (bf16[256,768]{1,0:T(8,128)(2,1)}, bf16[256,768]{1,0:T(8,128)(2,1)S(1)}, u32[]{:S(2)}, u32[]{:S(2)}) collective-permute-start(bf16[256,768]{1,0:T(8,128)(2,1)} %bitcast.47), channel_id=1, source_target_pairs={{0,2},{1,3},{2,0},{3,1},{4,6},{5,7},{6,4},{7,5},{8,10},{9,11},{10,... | collective-permute-start | bytes 1179656 | tf_op jit(solution)/shard_map/ppermute | solution.py:46
  3.8 1.9 shard_map.272
  5.7 3.5 %all-to-all-start = ((bf16[4,56,768]{2,1,0:T(8,128)(2,1)}), bf16[4,56,768]{2,1,0:T(8,128)(2,1)S(1)}, u32[]{:S(2)}, u32[]{:S(2)}) async-start(bf16[4,56,768]{2,1,0:T(8,128)(2,1)} %shard_map.272), calls=%async_computation | async-start | bytes 688128 | tf_op jit(solution)/shard_map/all_to_all | solution.py:635
  9.1 2.7 %collective-permute-start.16 = (bf16[1,96,768]{2,1,0:T(8,128)(2,1)}, bf16[1,96,768]{2,1,0:T(8,128)(2,1)S(1)}, u32[]{:S(2)}, u32[]{:S(2)}) collective-permute-start(bf16[1,96,768]{2,1,0:T(8,128)(2,1)} %bitcast.41), channel_id=1, source_target_pairs={{0,16},{4,20},{8,24},{12,28},{16,0},{20,4},{24,8},{28,12},{1,17},{... | collective-permute-start | bytes 442376 | tf_op jit(solution)/shard_map/ppermute | solution.py:46
  11.8 1.9 collective-permute-start.3
  13.7 1.4 collective-permute-start.9
  15.1 0.7 broadcast_multiply_fusion
  15.9 6.0 %collective-permute-start.10 = (bf16[1,24,768]{2,1,0:T(8,128)(2,1)S(1)}, bf16[1,24,768]{2,1,0:T(8,128)(2,1)S(1)}, u32[]{:S(2)}, u32[]{:S(2)}) collective-permute-start(bf16[1,24,768]{2,1,0:T(8,128)(2,1)S(1)} %bitcast.57), channel_id=1, source_target_pairs={{0,16},{4,20},{8,24},{12,28},{16,0},{20,4},{24,8},{28,12},{1,17},{... | collective-permute-start | bytes 110600 | tf_op jit(solution)/shard_map/ppermute | solution.py:46
  21.9 1.8 multiply_sine_fusion
  23.7 0.2 collective-permute-done.10
  23.9 3.5 %collective-permute-start.11 = (bf16[2,24,768]{2,1,0:T(8,128)(2,1)S(1)}, bf16[2,24,768]{2,1,0:T(8,128)(2,1)S(1)}, u32[]{:S(2)}, u32[]{:S(2)}) collective-permute-start(bf16[2,24,768]{2,1,0:T(8,128)(2,1)S(1)} %pad_maximum_fusion.8), channel_id=1, source_target_pairs={{0,8},{4,12},{8,0},{12,4},{16,24},{20,28},{24,16},{28,20},{1,9},{5... | collective-permute-start | bytes 221192 | tf_op jit(solution)/shard_map/ppermute | solution.py:46
  27.4 2.3 %collective-permute-done.11 = bf16[2,24,768]{2,1,0:T(8,128)(2,1)S(1)} collective-permute-done((bf16[2,24,768]{2,1,0:T(8,128)(2,1)S(1)}, bf16[2,24,768]{2,1,0:T(8,128)(2,1)S(1)}, u32[]{:S(2)}, u32[]{:S(2)}) %collective-permute-start.11) | collective-permute-done | bytes 73760 | tf_op jit(solution)/shard_map/ppermute | solution.py:46
  29.8 2.0 collective-permute-start.12
  31.7 0.6 pad_add_fusion.ids
  32.3 0.7 copy-done.2
  33.0 1.7 shard_map.273
  34.7 1.3 collective-permute-start.13
  36.0 3.3 %collective-permute-start.6 = (bf16[1,96,640]{2,1,0:T(8,128)(2,1)}, bf16[1,96,640]{2,1,0:T(8,128)(2,1)S(1)}, u32[]{:S(2)}, u32[]{:S(2)}) collective-permute-start(bf16[1,96,640]{2,1,0:T(8,128)(2,1)} %bitcast.44), channel_id=1, source_target_pairs={{0,16},{4,20},{8,24},{12,28},{16,0},{20,4},{24,8},{28,12},{1,17},{... | collective-permute-start | bytes 368648 | tf_op jit(solution)/shard_map/ppermute | solution.py:46
  39.4 8.9 %collective-permute-done.13 = bf16[1,104,768]{2,1,0:T(8,128)(2,1)S(1)} collective-permute-done((bf16[1,104,768]{2,1,0:T(8,128)(2,1)}, bf16[1,104,768]{2,1,0:T(8,128)(2,1)S(1)}, u32[]{:S(2)}, u32[]{:S(2)}) %collective-permute-start.13) | collective-permute-done | bytes 159776 | tf_op jit(solution)/shard_map/ppermute | solution.py:46
  48.2 0.1 collective-permute-start.17
  48.4 2.5 %collective-permute-done.6 = bf16[1,96,640]{2,1,0:T(8,128)(2,1)S(1)} collective-permute-done((bf16[1,96,640]{2,1,0:T(8,128)(2,1)}, bf16[1,96,640]{2,1,0:T(8,128)(2,1)S(1)}, u32[]{:S(2)}, u32[]{:S(2)}) %collective-permute-start.6) | collective-permute-done | bytes 122912 | tf_op jit(solution)/shard_map/ppermute | solution.py:46
  50.9 0.1 collective-permute-start.14
  51.1 13.3 %collective-permute-done.14 = bf16[2,104,768]{2,1,0:T(8,128)(2,1)S(1)} collective-permute-done((bf16[2,104,768]{2,1,0:T(8,128)(2,1)S(1)}, bf16[2,104,768]{2,1,0:T(8,128)(2,1)S(1)}, u32[]{:S(2)}, u32[]{:S(2)}) %collective-permute-start.14) | collective-permute-done | bytes 319520 | tf_op jit(solution)/shard_map/ppermute | solution.py:46
  64.5 2.1 collective-permute-start.15
  66.8 0.5 collective-permute-start.2
  67.3 0.1 collective-permute-start.5
  67.4 5.3 %collective-permute-done.7 = bf16[2,96,640]{2,1,0:T(8,128)(2,1)S(1)} collective-permute-done((bf16[2,96,640]{2,1,0:T(8,128)(2,1)S(1)}, bf16[2,96,640]{2,1,0:T(8,128)(2,1)S(1)}, u32[]{:S(2)}, u32[]{:S(2)}) %collective-permute-start.7) | collective-permute-done | bytes 245792 | tf_op jit(solution)/shard_map/ppermute | solution.py:46
  72.7 0.2 collective-permute-start.18
  72.9 0.8 reverse_select_fusion
  73.8 1.9 collective-permute-start.8
  75.7 18.8 %collective-permute-done.18.refs_11_ = bf16[4,96,768]{2,1,0:T(8,128)(2,1)S(1)} collective-permute-done((bf16[4,96,768]{2,1,0:T(8,128)(2,1)S(1)}, bf16[4,96,768]{2,1,0:T(8,128)(2,1)S(1)}, u32[]{:S(2)}, u32[]{:S(2)}) %collective-permute-start.18) | collective-permute-done | bytes 589856 | tf_op jit(solution)/shard_map/ppermute | solution.py:46
  94.5 0.8 copy-done.19
  95.3 17.1 %shard_map.274 = (bf16[4,96,768]{2,1,0:T(8,128)(2,1)}, bf16[4,96,768]{2,1,0:T(8,128)(2,1)}, bf16[4,96,768]{2,1,0:T(8,128)(2,1)}, bf16[4,96,768]{2,1,0:T(8,128)(2...) custom-call(s32[21]{0:T(128)} %pad_add_fusion.ids, ...), custom_call_target="tpu_custom_call" | custom-call | flops 12079595520 | bytes 11178068 | tf_op jit(solution)/shard_map/pallas_call | solution.py:410
  112.4 2.1 collective-permute-start.24
  114.5 0.8 copy-done.20
  115.3 24.2 %shard_map.275 = (bf16[4,104,768]{2,1,0:T(8,128)(2,1)}, bf16[4,104,768]{2,1,0:T(8,128)(2,1)}, bf16[2,2,256,768]{3,2,1,0:T(8,128)(2,1)}, bf16[2,2,256,768]{3,2,1,0:T(8,128)(2,1)}) custom-call(s32[21]{0:T(128)} %pad_add_fusion.ids, bf16[256,768]{1,0:T(8,128)(2,1)} %bitcast.50, bf16[256,768]{1,0:T(8,128)(2,1)} %copy-done.21, ...), custom_call_target="tpu_custom_call" | custom-call | flops 12079595520 | bytes 12587092 | tf_op jit(solution)/shard_map/pallas_call | solution.py:410
  139.8 2.0 collective-permute-start.21
  141.8 0.1 add_convert_fusion.3
  141.9 0.1 collective-permute-start.25
  142.0 13.9 %collective-permute-done.28 = bf16[4,96,768]{2,1,0:T(8,128)(2,1)S(1)} collective-permute-done((bf16[4,96,768]{2,1,0:T(8,128)(2,1)S(1)}, bf16[4,96,768]{2,1,0:T(8,128)(2,1)S(1)}, u32[]{:S(2)}, u32[]{:S(2)}) %collective-permute-start.28) | collective-permute-done | bytes 589856 | tf_op jit(solution)/shard_map/ppermute | solution.py:46
  155.9 0.1 add_convert_fusion.2
  156.2 13.5 %collective-permute-done.21 = bf16[4,104,768]{2,1,0:T(8,128)(2,1)S(1)} collective-permute-done((bf16[4,104,768]{2,1,0:T(8,128)(2,1)}, bf16[4,104,768]{2,1,0:T(8,128)(2,1)S(1)}, u32[]{:S(2)}, u32[]{:S(2)}) %collective-permute-start.21) | collective-permute-done | bytes 639008 | tf_op jit(solution)/shard_map/ppermute | solution.py:46
  169.6 0.1 add_convert_fusion.1
  169.9 5.6 %collective-permute-done.25 = bf16[2,96,768]{2,1,0:T(8,128)(2,1)S(1)} collective-permute-done((bf16[2,96,768]{2,1,0:T(8,128)(2,1)S(1)}, bf16[2,96,768]{2,1,0:T(8,128)(2,1)S(1)}, u32[]{:S(2)}, u32[]{:S(2)}) %collective-permute-start.25) | collective-permute-done | bytes 294944 | tf_op jit(solution)/shard_map/ppermute | solution.py:46
  175.4 0.8 fusion.5
  176.2 1.3 collective-permute-start.26
  177.5 1.5 add_convert_fusion
  179.1 0.8 fusion
  179.8 1.6 collective-permute-start.23
  181.5 1.4 collective-permute-start.30
  182.9 9.4 %collective-permute-done.26 = bf16[1,96,768]{2,1,0:T(8,128)(2,1)S(1)} collective-permute-done((bf16[1,96,768]{2,1,0:T(8,128)(2,1)S(1)}, bf16[1,96,768]{2,1,0:T(8,128)(2,1)S(1)}, u32[]{:S(2)}, u32[]{:S(2)}) %collective-permute-start.26) | collective-permute-done | bytes 147488 | tf_op jit(solution)/shard_map/ppermute | solution.py:46
  192.3 3.4 %collective-permute-done.23 = bf16[1,104,768]{2,1,0:T(8,128)(2,1)S(1)} collective-permute-done((bf16[1,104,768]{2,1,0:T(8,128)(2,1)S(1)}, bf16[1,104,768]{2,1,0:T(8,128)(2,1)S(1)}, u32[]{:S(2)}, u32[]{:S(2)}) %collective-permute-start.23) | collective-permute-done | bytes 159776 | tf_op jit(solution)/shard_map/ppermute | solution.py:46
  195.7 0.7 copy-done.14
  196.4 2.0 shard_map.277
  198.4 3.5 %all-to-all-start.1 = ((bf16[4,56,768]{2,1,0:T(8,128)(2,1)}), bf16[4,56,768]{2,1,0:T(8,128)(2,1)S(1)}, u32[]{:S(2)}, u32[]{:S(2)}) async-start(bf16[4,56,768]{2,1,0:T(8,128)(2,1)} %get-tuple-element.58), calls=%async_computation.1 | async-start | bytes 688128 | tf_op jit(solution)/shard_map/all_to_all | solution.py:700
  201.9 0.6 stack.20.at
  202.5 1.4 collective-permute-start.27
  203.9 0.8 fusion.4
  204.7 0.6 convert_element_type.135
  205.3 3.4 %all-to-all-done.1.last = bf16[4,56,768]{2,1,0:T(8,128)(2,1)S(1)} async-done(((bf16[4,56,768]{2,1,0:T(8,128)(2,1)}), bf16[4,56,768]{2,1,0:T(8,128)(2,1)S(1)}, u32[]{:S(2)}, u32[]{:S(2)}) %all-to-all-start.1) | async-done | bytes 344096 | tf_op jit(solution)/shard_map/all_to_all | solution.py:700
  208.7 0.7 copy-done.1
  209.4 1.9 shard_map.278
  211.4 0.9 copy-done.3
  212.2 3.4 %shard_map.276 = (bf16[256,768]{1,0:T(8,128)(2,1)}, f32[256,768]{1,0:T(8,128)}) custom-call(bf16[256,768]{1,0:T(8,128)(2,1)} %bitcast.51, bf16[256,768]{1,0:T(8,128)(2,1)} %bitcast.55, f32[2,256,768]{2,1,0:T(8,128)} %get-tuple-element.73.keep, bf16[2,256,768]{2,1,0:T(8,128)(2,1)} %bitcast.37, f32[8,768]{1,0:T(8,128)} %get-tuple-element.48.refs_16_.add), custom_call_target="tpu_custom_call" | custom-call | bytes 4349952 | tf_op jit(solution)/shard_map/pallas_call | solution.py:410
  (88 shorter events, 1.1 us)
Async XLA Ops:
  0.6 26.8 %copy-start.16 = (s32[8]{0:T(128)S(1)}, s32[8]{0:T(128)}, u32[]{:S(2)}) copy-start(s32[8]{0:T(128)} %constant.76.clone) | copy-start | bytes 100
  0.7 26.7 %copy-start.17 = (s32[8]{0:T(128)S(1)}, s32[8]{0:T(128)}, u32[]{:S(2)}) copy-start(s32[8]{0:T(128)} %constant.77.clone) | copy-start | bytes 100
  0.7 35.3 %copy-start.7 = (bf16[96,768]{1,0:T(8,128)(2,1)S(1)}, bf16[96,768]{1,0:T(8,128)(2,1)}, u32[]{:S(2)}) copy-start(bf16[96,768]{1,0:T(8,128)(2,1)} %param.25) | copy-start | bytes 442372
  0.7 66.0 %collective-permute-start = (bf16[256,768]{1,0:T(8,128)(2,1)}, bf16[256,768]{1,0:T(8,128)(2,1)S(1)}, u32[]{:S(2)}, u32[]{:S(2)}) collective-permute-start(bf16[256,768]{1,0:T(8,128)(2,1)} %bitcast.47), channel_id=1, source_target_pairs={{0,2},{1,3},{2,0},{3,1},{4,6},{5,7},{6,4},{7,5},{8,10},{9,11},{10,... | collective-permute-start | bytes 1179656 | tf_op jit(solution)/shard_map/ppermute | solution.py:46
  3.7 63.5 %collective-permute-start.1 = (bf16[256,768]{1,0:T(8,128)(2,1)}, bf16[256,768]{1,0:T(8,128)(2,1)}, u32[]{:S(2)}, u32[]{:S(2)}) collective-permute-start(bf16[256,768]{1,0:T(8,128)(2,1)} %bitcast.48), channel_id=1, source_target_pairs={{0,1},{1,0},{2,3},{3,2},{4,5},{5,4},{6,7},{7,6},{8,9},{9,8},{10,11... | collective-permute-start | bytes 1179656 | tf_op jit(solution)/shard_map/ppermute | solution.py:46
  5.7 26.6 %all-to-all-start = ((bf16[4,56,768]{2,1,0:T(8,128)(2,1)}), bf16[4,56,768]{2,1,0:T(8,128)(2,1)S(1)}, u32[]{:S(2)}, u32[]{:S(2)}) async-start(bf16[4,56,768]{2,1,0:T(8,128)(2,1)} %shard_map.272), calls=%async_computation | async-start | bytes 688128 | tf_op jit(solution)/shard_map/all_to_all | solution.py:635
  9.1 25.6 %collective-permute-start.16 = (bf16[1,96,768]{2,1,0:T(8,128)(2,1)}, bf16[1,96,768]{2,1,0:T(8,128)(2,1)S(1)}, u32[]{:S(2)}, u32[]{:S(2)}) collective-permute-start(bf16[1,96,768]{2,1,0:T(8,128)(2,1)} %bitcast.41), channel_id=1, source_target_pairs={{0,16},{4,20},{8,24},{12,28},{16,0},{20,4},{24,8},{28,12},{1,17},{... | collective-permute-start | bytes 442376 | tf_op jit(solution)/shard_map/ppermute | solution.py:46
  11.8 55.0 %collective-permute-start.3 = (bf16[256,768]{1,0:T(8,128)(2,1)}, bf16[256,768]{1,0:T(8,128)(2,1)}, u32[]{:S(2)}, u32[]{:S(2)}) collective-permute-start(bf16[256,768]{1,0:T(8,128)(2,1)} %bitcast.52), channel_id=1, source_target_pairs={{0,2},{1,3},{2,0},{3,1},{4,6},{5,7},{6,4},{7,5},{8,10},{9,11},{10,... | collective-permute-start | bytes 1179656 | tf_op jit(solution)/shard_map/ppermute | solution.py:46
  13.7 2.2 %collective-permute-start.9 = (bf16[24,768]{1,0:T(8,128)(2,1)}, bf16[24,768]{1,0:T(8,128)(2,1)S(1)}, u32[]{:S(2)}, u32[]{:S(2)}) collective-permute-start(bf16[24,768]{1,0:T(8,128)(2,1)} %param.21), channel_id=1, source_target_pairs={{0,0},{1,4},{2,8},{3,12},{4,16},{5,20},{6,24},{7,28},{8,1},{9,5},{... | collective-permute-start | bytes 110600 | tf_op jit(solution)/shard_map/ppermute | solution.py:72
  15.9 8.0 %collective-permute-start.10 = (bf16[1,24,768]{2,1,0:T(8,128)(2,1)S(1)}, bf16[1,24,768]{2,1,0:T(8,128)(2,1)S(1)}, u32[]{:S(2)}, u32[]{:S(2)}) collective-permute-start(bf16[1,24,768]{2,1,0:T(8,128)(2,1)S(1)} %bitcast.57), channel_id=1, source_target_pairs={{0,16},{4,20},{8,24},{12,28},{16,0},{20,4},{24,8},{28,12},{1,17},{... | collective-permute-start | bytes 110600 | tf_op jit(solution)/shard_map/ppermute | solution.py:46
  23.9 5.9 %collective-permute-start.11 = (bf16[2,24,768]{2,1,0:T(8,128)(2,1)S(1)}, bf16[2,24,768]{2,1,0:T(8,128)(2,1)S(1)}, u32[]{:S(2)}, u32[]{:S(2)}) collective-permute-start(bf16[2,24,768]{2,1,0:T(8,128)(2,1)S(1)} %pad_maximum_fusion.8), channel_id=1, source_target_pairs={{0,8},{4,12},{8,0},{12,4},{16,24},{20,28},{24,16},{28,20},{1,9},{5... | collective-permute-start | bytes 221192 | tf_op jit(solution)/shard_map/ppermute | solution.py:46
  29.8 6.3 %collective-permute-start.12 = (bf16[4,24,768]{2,1,0:T(8,128)(2,1)S(1)}, bf16[4,24,768]{2,1,0:T(8,128)(2,1)S(1)}, u32[]{:S(2)}, u32[]{:S(2)}) collective-permute-start(bf16[4,24,768]{2,1,0:T(8,128)(2,1)S(1)} %pad_maximum_fusion.7), channel_id=1, source_target_pairs={{0,4},{4,0},{8,12},{12,8},{16,20},{20,16},{24,28},{28,24},{1,5},{5... | collective-permute-start | bytes 442376 | tf_op jit(solution)/shard_map/ppermute | solution.py:46
  32.3 0.7 copy-start.2
  34.7 13.6 %copy-start.4 = (bf16[104,768]{1,0:T(8,128)(2,1)S(1)}, bf16[104,768]{1,0:T(8,128)(2,1)}, u32[]{:S(2)}) copy-start(bf16[104,768]{1,0:T(8,128)(2,1)} %get-tuple-element.44) | copy-start | bytes 479236
  34.7 16.3 %copy-start.12 = (bf16[96,640]{1,0:T(8,128)(2,1)S(1)}, bf16[96,640]{1,0:T(8,128)(2,1)}, u32[]{:S(2)}) copy-start(bf16[96,640]{1,0:T(8,128)(2,1)} %get-tuple-element.43) | copy-start | bytes 368644
  34.7 13.5 %collective-permute-start.13 = (bf16[1,104,768]{2,1,0:T(8,128)(2,1)}, bf16[1,104,768]{2,1,0:T(8,128)(2,1)S(1)}, u32[]{:S(2)}, u32[]{:S(2)}) collective-permute-start(bf16[1,104,768]{2,1,0:T(8,128)(2,1)} %bitcast.38), channel_id=1, source_target_pairs={{0,16},{4,20},{8,24},{12,28},{16,0},{20,4},{24,8},{28,12},{1,17},{... | collective-permute-start | bytes 479240 | tf_op jit(solution)/shard_map/ppermute | solution.py:46
  36.0 14.8 %collective-permute-start.6 = (bf16[1,96,640]{2,1,0:T(8,128)(2,1)}, bf16[1,96,640]{2,1,0:T(8,128)(2,1)S(1)}, u32[]{:S(2)}, u32[]{:S(2)}) collective-permute-start(bf16[1,96,640]{2,1,0:T(8,128)(2,1)} %bitcast.44), channel_id=1, source_target_pairs={{0,16},{4,20},{8,24},{12,28},{16,0},{20,4},{24,8},{28,12},{1,17},{... | collective-permute-start | bytes 368648 | tf_op jit(solution)/shard_map/ppermute | solution.py:46
  48.2 16.2 %collective-permute-start.17 = (bf16[2,96,768]{2,1,0:T(8,128)(2,1)S(1)}, bf16[2,96,768]{2,1,0:T(8,128)(2,1)S(1)}, u32[]{:S(2)}, u32[]{:S(2)}) collective-permute-start(bf16[2,96,768]{2,1,0:T(8,128)(2,1)S(1)} %pad_maximum_fusion.5), channel_id=1, source_target_pairs={{0,8},{4,12},{8,0},{12,4},{16,24},{20,28},{24,16},{28,20},{1,9},{5... | collective-permute-start | bytes 884744 | tf_op jit(solution)/shard_map/ppermute | solution.py:46
  50.9 13.5 %collective-permute-start.14 = (bf16[2,104,768]{2,1,0:T(8,128)(2,1)S(1)}, bf16[2,104,768]{2,1,0:T(8,128)(2,1)S(1)}, u32[]{:S(2)}, u32[]{:S(2)}) collective-permute-start(bf16[2,104,768]{2,1,0:T(8,128)(2,1)S(1)} %pad_maximum_fusion.3), channel_id=1, source_target_pairs={{0,8},{4,12},{8,0},{12,4},{16,24},{20,28},{24,16},{28,20},{1,9},{5... | collective-permute-start | bytes 958472 | tf_op jit(solution)/shard_map/ppermute | solution.py:46
  51.0 15.6 %copy-start.13 = (bf16[2,128,768]{2,1,0:T(8,128)(2,1)S(1)}, bf16[2,128,768]{2,1,0:T(8,128)(2,1)}, u32[]{:S(2)}) copy-start(bf16[2,128,768]{2,1,0:T(8,128)(2,1)} %param.18) | copy-start | bytes 1179652
  64.4 8.3 %collective-permute-start.7 = (bf16[2,96,640]{2,1,0:T(8,128)(2,1)S(1)}, bf16[2,96,640]{2,1,0:T(8,128)(2,1)S(1)}, u32[]{:S(2)}, u32[]{:S(2)}) collective-permute-start(bf16[2,96,640]{2,1,0:T(8,128)(2,1)S(1)} %pad_maximum_fusion.6), channel_id=1, source_target_pairs={{0,8},{4,12},{8,0},{12,4},{16,24},{20,28},{24,16},{28,20},{1,9},{5... | collective-permute-start | bytes 737288 | tf_op jit(solution)/shard_map/ppermute | solution.py:46
  64.5 9.2 %copy-start.5 = (bf16[4,104,768]{2,1,0:T(8,128)(2,1)}, bf16[4,104,768]{2,1,0:T(8,128)(2,1)S(1)}, u32[]{:S(2)}) copy-start(bf16[4,104,768]{2,1,0:T(8,128)(2,1)S(1)} %pad_maximum_fusion.refs_8_) | copy-start | bytes 1916932
  64.5 30.8 %collective-permute-start.15 = (bf16[4,104,768]{2,1,0:T(8,128)(2,1)S(1)}, bf16[4,104,768]{2,1,0:T(8,128)(2,1)}, u32[]{:S(2)}, u32[]{:S(2)}) collective-permute-start(bf16[4,104,768]{2,1,0:T(8,128)(2,1)S(1)} %pad_maximum_fusion.refs_8_), channel_id=1, source_target_pairs={{0,4},{4,0},{8,12},{12,8},{16,20},{20,16},{24,28},{28,24},{1,5},{5... | collective-permute-start | bytes 1916936 | tf_op jit(solution)/shard_map/ppermute | solution.py:46
  66.6 28.7 %copy-start.8 = (bf16[4,96,768]{2,1,0:T(8,128)(2,1)}, bf16[4,96,768]{2,1,0:T(8,128)(2,1)S(1)}, u32[]{:S(2)}) copy-start(bf16[4,96,768]{2,1,0:T(8,128)(2,1)S(1)} %pad_maximum_fusion.1.refs_10_) | copy-start | bytes 1769476
  66.7 28.6 %copy-start.21 = (bf16[256,768]{1,0:T(8,128)(2,1)}, bf16[256,768]{1,0:T(8,128)(2,1)S(1)}, u32[]{:S(2)}) copy-start(bf16[256,768]{1,0:T(8,128)(2,1)S(1)} %collective-permute-done.refs_1_) | copy-start | bytes 1179652
  66.7 7.1 %collective-permute-start.4 = (bf16[256,768]{1,0:T(8,128)(2,1)S(1)}, bf16[256,768]{1,0:T(8,128)(2,1)S(1)}, u32[]{:S(2)}, u32[]{:S(2)}) collective-permute-start(bf16[256,768]{1,0:T(8,128)(2,1)S(1)} %bitcast.56), channel_id=1, source_target_pairs={{0,1},{1,0},{2,3},{3,2},{4,5},{5,4},{6,7},{7,6},{8,9},{9,8},{10,11... | collective-permute-start | bytes 1179656 | tf_op jit(solution)/shard_map/ppermute | solution.py:46
  66.8 8.9 %collective-permute-start.2 = (bf16[256,768]{1,0:T(8,128)(2,1)S(1)}, bf16[256,768]{1,0:T(8,128)(2,1)S(1)}, u32[]{:S(2)}, u32[]{:S(2)}) collective-permute-start(bf16[256,768]{1,0:T(8,128)(2,1)S(1)} %collective-permute-done.refs_1_), channel_id=1, source_target_pairs={{0,1},{1,0},{2,3},{3,2},{4,5},{5,4},{6,7},{7,6},{8,9},{9,8},{10,11... | collective-permute-start | bytes 1179656 | tf_op jit(solution)/shard_map/ppermute | solution.py:46
  67.3 8.4 %collective-permute-start.5 = (bf16[256,768]{1,0:T(8,128)(2,1)}, bf16[256,768]{1,0:T(8,128)(2,1)S(1)}, u32[]{:S(2)}, u32[]{:S(2)}) collective-permute-start(bf16[256,768]{1,0:T(8,128)(2,1)} %collective-permute-done.3.refs_5_), channel_id=1, source_target_pairs={{0,1},{1,0},{2,3},{3,2},{4,5},{5,4},{6,7},{7,6},{8,9},{9,8},{10,11... | collective-permute-start | bytes 1179656 | tf_op jit(solution)/shard_map/ppermute | solution.py:46
  72.7 21.8 %collective-permute-start.18 = (bf16[4,96,768]{2,1,0:T(8,128)(2,1)S(1)}, bf16[4,96,768]{2,1,0:T(8,128)(2,1)S(1)}, u32[]{:S(2)}, u32[]{:S(2)}) collective-permute-start(bf16[4,96,768]{2,1,0:T(8,128)(2,1)S(1)} %pad_maximum_fusion.1.refs_10_), channel_id=1, source_target_pairs={{0,4},{4,0},{8,12},{12,8},{16,20},{20,16},{24,28},{28,24},{1,5},{5... | collective-permute-start | bytes 1769480 | tf_op jit(solution)/shard_map/ppermute | solution.py:46
  73.7 38.7 %copy-start.11 = (bf16[4,96,640]{2,1,0:T(8,128)(2,1)}, bf16[4,96,640]{2,1,0:T(8,128)(2,1)S(1)}, u32[]{:S(2)}) copy-start(bf16[4,96,640]{2,1,0:T(8,128)(2,1)S(1)} %pad_maximum_fusion.2.refs_8_) | copy-start | bytes 1474564
  73.8 20.7 %copy-start.22 = (bf16[256,768]{1,0:T(8,128)(2,1)}, bf16[256,768]{1,0:T(8,128)(2,1)S(1)}, u32[]{:S(2)}) copy-start(bf16[256,768]{1,0:T(8,128)(2,1)S(1)} %collective-permute-done.4.refs_6_) | copy-start | bytes 1179652
  73.8 40.8 %collective-permute-start.8 = (bf16[4,96,640]{2,1,0:T(8,128)(2,1)S(1)}, bf16[4,96,640]{2,1,0:T(8,128)(2,1)S(1)}, u32[]{:S(2)}, u32[]{:S(2)}) collective-permute-start(bf16[4,96,640]{2,1,0:T(8,128)(2,1)S(1)} %pad_maximum_fusion.2.refs_8_), channel_id=1, source_target_pairs={{0,4},{4,0},{8,12},{12,8},{16,20},{20,16},{24,28},{28,24},{1,5},{5... | collective-permute-start | bytes 1474568 | tf_op jit(solution)/shard_map/ppermute | solution.py:46
  75.7 18.8 %copy-start.23 = (bf16[256,768]{1,0:T(8,128)(2,1)}, bf16[256,768]{1,0:T(8,128)(2,1)S(1)}, u32[]{:S(2)}) copy-start(bf16[256,768]{1,0:T(8,128)(2,1)S(1)} %collective-permute-done.2.refs_3_) | copy-start | bytes 1179652
  75.7 18.8 %copy-start.24 = (bf16[256,768]{1,0:T(8,128)(2,1)}, bf16[256,768]{1,0:T(8,128)(2,1)S(1)}, u32[]{:S(2)}) copy-start(bf16[256,768]{1,0:T(8,128)(2,1)S(1)} %collective-permute-done.5.refs_7_) | copy-start | bytes 1179652
  94.5 0.8 copy-start.19
  112.4 29.3 %collective-permute-start.24 = (bf16[4,96,768]{2,1,0:T(8,128)(2,1)}, bf16[4,96,768]{2,1,0:T(8,128)(2,1)S(1)}, u32[]{:S(2)}, u32[]{:S(2)}) collective-permute-start(bf16[4,96,768]{2,1,0:T(8,128)(2,1)} %get-tuple-element.57), channel_id=1, source_target_pairs={{0,8},{4,12},{8,0},{12,4},{16,24},{20,28},{24,16},{28,20},{1,9},{5... | collective-permute-start | bytes 1769480 | tf_op jit(solution)/shard_map/ppermute | solution.py:46
  114.5 0.8 copy-start.20
  115.3 24.3 %copy-start.18 = (bf16[4,96,768]{2,1,0:T(8,128)(2,1)S(1)}, bf16[4,96,768]{2,1,0:T(8,128)(2,1)}, u32[]{:S(2)}) copy-start(bf16[4,96,768]{2,1,0:T(8,128)(2,1)} %get-tuple-element.66) | copy-start | bytes 1769476
  115.3 26.4 %copy-start.10 = (bf16[4,96,768]{2,1,0:T(8,128)(2,1)S(1)}, bf16[4,96,768]{2,1,0:T(8,128)(2,1)}, u32[]{:S(2)}) copy-start(bf16[4,96,768]{2,1,0:T(8,128)(2,1)} %get-tuple-element.56) | copy-start | bytes 1769476
  139.6 16.4 %copy-start.9 = (bf16[4,96,768]{2,1,0:T(8,128)(2,1)S(1)}, bf16[4,96,768]{2,1,0:T(8,128)(2,1)}, u32[]{:S(2)}) copy-start(bf16[4,96,768]{2,1,0:T(8,128)(2,1)} %get-tuple-element.65) | copy-start | bytes 1769476
  139.6 37.9 %collective-permute-start.19 = (bf16[2,2,256,768]{3,2,1,0:T(8,128)(2,1)}, bf16[2,2,256,768]{3,2,1,0:T(8,128)(2,1)S(1)}, u32[]{:S(2)}, u32[]{:S(2)}) collective-permute-start(bf16[2,2,256,768]{3,2,1,0:T(8,128)(2,1)} %get-tuple-element.51), channel_id=1, source_target_pairs={{0,1},{1,0},{2,3},{3,2},{4,5},{5,4},{6,7},{7,6},{8,9},{9,8},{10,11... | collective-permute-start | bytes 4718600 | tf_op jit(solution)/shard_map/ppermute | solution.py:46
  139.7 16.3 %collective-permute-start.28 = (bf16[4,96,768]{2,1,0:T(8,128)(2,1)S(1)}, bf16[4,96,768]{2,1,0:T(8,128)(2,1)S(1)}, u32[]{:S(2)}, u32[]{:S(2)}) collective-permute-start(bf16[4,96,768]{2,1,0:T(8,128)(2,1)S(1)} %copy-done.18), channel_id=1, source_target_pairs={{0,4},{4,0},{8,12},{12,8},{16,20},{20,16},{24,28},{28,24},{1,5},{5... | collective-permute-start | bytes 1769480 | tf_op jit(solution)/shard_map/ppermute | solution.py:46
  139.8 29.9 %collective-permute-start.21 = (bf16[4,104,768]{2,1,0:T(8,128)(2,1)}, bf16[4,104,768]{2,1,0:T(8,128)(2,1)S(1)}, u32[]{:S(2)}, u32[]{:S(2)}) collective-permute-start(bf16[4,104,768]{2,1,0:T(8,128)(2,1)} %get-tuple-element.55), channel_id=1, source_target_pairs={{0,4},{4,0},{8,12},{12,8},{16,20},{20,16},{24,28},{28,24},{1,5},{5... | collective-permute-start | bytes 1916936 | tf_op jit(solution)/shard_map/ppermute | solution.py:46
  141.8 27.9 %copy-start.6 = (bf16[4,104,768]{2,1,0:T(8,128)(2,1)S(1)}, bf16[4,104,768]{2,1,0:T(8,128)(2,1)}, u32[]{:S(2)}) copy-start(bf16[4,104,768]{2,1,0:T(8,128)(2,1)} %get-tuple-element.54) | copy-start | bytes 1916932
  141.9 33.5 %collective-permute-start.25 = (bf16[2,96,768]{2,1,0:T(8,128)(2,1)S(1)}, bf16[2,96,768]{2,1,0:T(8,128)(2,1)S(1)}, u32[]{:S(2)}, u32[]{:S(2)}) collective-permute-start(bf16[2,96,768]{2,1,0:T(8,128)(2,1)S(1)} %get-tuple-element.78), channel_id=1, source_target_pairs={{0,4},{4,0},{8,12},{12,8},{16,20},{20,16},{24,28},{28,24},{1,5},{5... | collective-permute-start | bytes 884744 | tf_op jit(solution)/shard_map/ppermute | solution.py:46
  156.1 25.4 %collective-permute-start.29 = (bf16[2,96,768]{2,1,0:T(8,128)(2,1)S(1)}, bf16[2,96,768]{2,1,0:T(8,128)(2,1)S(1)}, u32[]{:S(2)}, u32[]{:S(2)}) collective-permute-start(bf16[2,96,768]{2,1,0:T(8,128)(2,1)S(1)} %get-tuple-element.76), channel_id=1, source_target_pairs={{0,8},{4,12},{8,0},{12,4},{16,24},{20,28},{24,16},{28,20},{1,9},{5... | collective-permute-start | bytes 884744 | tf_op jit(solution)/shard_map/ppermute | solution.py:46
  169.6 7.9 %copy-start = (bf16[2,2,256,768]{3,2,1,0:T(8,128)(2,1)S(1)}, bf16[2,2,256,768]{3,2,1,0:T(8,128)(2,1)}, u32[]{:S(2)}) copy-start(bf16[2,2,256,768]{3,2,1,0:T(8,128)(2,1)} %get-tuple-element.50) | copy-start | bytes 4718596
  169.8 9.3 %collective-permute-start.22 = (bf16[2,104,768]{2,1,0:T(8,128)(2,1)S(1)}, bf16[2,104,768]{2,1,0:T(8,128)(2,1)S(1)}, u32[]{:S(2)}, u32[]{:S(2)}) collective-permute-start(bf16[2,104,768]{2,1,0:T(8,128)(2,1)S(1)} %get-tuple-element.74), channel_id=1, source_target_pairs={{0,8},{4,12},{8,0},{12,4},{16,24},{20,28},{24,16},{28,20},{1,9},{5... | collective-permute-start | bytes 958472 | tf_op jit(solution)/shard_map/ppermute | solution.py:46
  176.2 16.1 %collective-permute-start.26 = (bf16[1,96,768]{2,1,0:T(8,128)(2,1)S(1)}, bf16[1,96,768]{2,1,0:T(8,128)(2,1)S(1)}, u32[]{:S(2)}, u32[]{:S(2)}) collective-permute-start(bf16[1,96,768]{2,1,0:T(8,128)(2,1)S(1)} %get-tuple-element.82), channel_id=1, source_target_pairs={{0,16},{4,20},{8,24},{12,28},{16,0},{20,4},{24,8},{28,12},{1,17},{... | collective-permute-start | bytes 442376 | tf_op jit(solution)/shard_map/ppermute | solution.py:46
  179.1 32.3 %collective-permute-start.20 = (bf16[1,2,256,768]{3,2,1,0:T(8,128)(2,1)S(1)}, bf16[1,2,256,768]{3,2,1,0:T(8,128)(2,1)S(1)}, u32[]{:S(2)}, u32[]{:S(2)}) collective-permute-start(bf16[1,2,256,768]{3,2,1,0:T(8,128)(2,1)S(1)} %get-tuple-element.72), channel_id=1, source_target_pairs={{0,2},{1,3},{2,0},{3,1},{4,6},{5,7},{6,4},{7,5},{8,10},{9,11},{10,... | collective-permute-start | bytes 2359304 | tf_op jit(solution)/shard_map/ppermute | solution.py:46
  179.8 15.9 %collective-permute-start.23 = (bf16[1,104,768]{2,1,0:T(8,128)(2,1)S(1)}, bf16[1,104,768]{2,1,0:T(8,128)(2,1)S(1)}, u32[]{:S(2)}, u32[]{:S(2)}) collective-permute-start(bf16[1,104,768]{2,1,0:T(8,128)(2,1)S(1)} %get-tuple-element.80), channel_id=1, source_target_pairs={{0,16},{4,20},{8,24},{12,28},{16,0},{20,4},{24,8},{28,12},{1,17},{... | collective-permute-start | bytes 479240 | tf_op jit(solution)/shard_map/ppermute | solution.py:46
  181.5 22.5 %collective-permute-start.30 = (bf16[1,96,768]{2,1,0:T(8,128)(2,1)S(1)}, bf16[1,96,768]{2,1,0:T(8,128)(2,1)S(1)}, u32[]{:S(2)}, u32[]{:S(2)}) collective-permute-start(bf16[1,96,768]{2,1,0:T(8,128)(2,1)S(1)} %fusion.2), channel_id=1, source_target_pairs={{0,16},{4,20},{8,24},{12,28},{16,0},{20,4},{24,8},{28,12},{1,17},{... | collective-permute-start | bytes 442376 | tf_op jit(solution)/shard_map/ppermute | solution.py:46
  192.3 3.4 %copy-start.15 = (bf16[1,96,768]{2,1,0:T(8,128)(2,1)}, bf16[1,96,768]{2,1,0:T(8,128)(2,1)S(1)}, u32[]{:S(2)}) copy-start(bf16[1,96,768]{2,1,0:T(8,128)(2,1)S(1)} %collective-permute-done.26) | copy-start | bytes 442372
  195.7 0.7 copy-start.14
  198.4 10.3 %all-to-all-start.1 = ((bf16[4,56,768]{2,1,0:T(8,128)(2,1)}), bf16[4,56,768]{2,1,0:T(8,128)(2,1)S(1)}, u32[]{:S(2)}, u32[]{:S(2)}) async-start(bf16[4,56,768]{2,1,0:T(8,128)(2,1)} %get-tuple-element.58), calls=%async_computation.1 | async-start | bytes 688128 | tf_op jit(solution)/shard_map/all_to_all | solution.py:700
  202.5 2.2 %collective-permute-start.27 = (bf16[24,768]{1,0:T(8,128)(2,1)}, bf16[24,768]{1,0:T(8,128)(2,1)S(1)}, u32[]{:S(2)}, u32[]{:S(2)}) collective-permute-start(bf16[24,768]{1,0:T(8,128)(2,1)} %get-tuple-element.61), channel_id=1, source_target_pairs={{0,0},{4,1},{8,2},{12,3},{16,4},{20,5},{24,6},{28,7},{1,8},{5,9},{... | collective-permute-start | bytes 110600 | tf_op jit(solution)/shard_map/ppermute | solution.py:72
  208.7 0.7 copy-start.1
  211.4 0.9 copy-start.3

commit v3 on v2

--- a/solution.py
+++ b/solution.py
@@ -54,6 +54,15 @@
     return mine, got
 
 
+def pieces(block, axis, bits):
+    parts = [block[None]]
+    for bit in reversed(bits[1:]):
+        parts.append(swap(jnp.concatenate(parts, axis=0), axis, bit))
+    early = swap(parts[0], axis, bits[0])
+    rest = swap(jnp.concatenate(parts[1:], axis=0), axis, bits[0])
+    return [*parts, early, rest]
+
+
 def token_blocks(block, axis):
     blocks = [block]
     for bit in reversed(bits_of(lax.axis_size(axis))):
@@ -125,14 +134,16 @@
     return out
 
 
-def placed(ids, mine, got, target, rows, width, sem, first=0):
+def blocks_of(stacks):
+    return [stack.at[i] for stack in stacks for i in range(stack.shape[0])]
+
+
+def placed(ids, stacks, target, rows, width, sem):
     out = []
-    half = mine.shape[0]
-    for p in range(2 * half):
-        source = mine.at[p] if p < half else got.at[p - half]
+    for p, source in enumerate(blocks_of(stacks)):
         if source.shape != (rows, width):
             source = source.at[pl.ds(0, rows), pl.ds(0, width)]
-        to = pl.multiple_of(ids[first + p] * rows, 8)
+        to = pl.multiple_of(ids[p] * rows, 8)
         out.append(pltpu.make_async_copy(source, target.at[pl.ds(to, rows)], sem.at[p]))
     return out
 
@@ -186,32 +197,32 @@
             jadd[0:1, at : at + own_b] = block[0:1, s * LANES : s * LANES + own_b]
 
 
-def mlp_kernel(sp, row_n, own_b, ids, *refs):
+def mlp_kernel(sp, row_n, own_b, stacks, ids, *refs):
     xs, cots = refs[:sp], refs[sp : 2 * sp]
-    ew_mine, ew_got, sw_mine, sw_got = refs[2 * sp : 2 * sp + 4]
-    outs = refs[2 * sp + 4 : 2 * sp + 13]
+    refs, ew_in, sw_in = refs[2 * sp :], refs[2 * sp : 2 * sp + stacks], refs[2 * sp + stacks :]
+    sw_in, refs = sw_in[:stacks], refs[2 * stacks :]
+    outs = refs[:9]
     eg_keep, eg_send, sg_keep, sg_send, out_part, in_part, sums, vecs, jadd = outs
-    x, cot, ew, sw, hid, act, pgr, eg, sg, small, eadd, sem = refs[2 * sp + 13 :]
+    x, cot, ew, sw, hid, act, pgr, eg, sg, small, eadd, sem = refs[9:]
     width = x.shape[1]
     chunk = x.shape[0] // sp
     rows, units = eg_keep.shape[1], sg_keep.shape[1]
-    half = ew_mine.shape[0]
-    side = 2 * half + sp + 1
+    dp = small.shape[0]
+    side = dp + sp + 1
     gets = (
         copies_in([b.at[pl.ds(0, chunk)] for b in xs], x, chunk, sem.at[0])
         + copies_in([b.at[pl.ds(0, chunk)] for b in cots], cot, chunk, sem.at[1])
-        + placed(ids, ew_mine, ew_got, ew, rows, ew.shape[1], sem.at[2])
-        + placed(ids, sw_mine, sw_got, sw, units, width, sem.at[3])
-    )
-    for p in range(2 * half):
-        block = ew_mine.at[p] if p < half else ew_got.at[p - half]
-        block = block.at[pl.ds(ew_mine.shape[1] - 8, 8)]
+        + placed(ids, ew_in, ew, rows, ew.shape[1], sem.at[2])
+        + placed(ids, sw_in, sw, units, width, sem.at[3])
+    )
+    for p, block in enumerate(blocks_of(ew_in)):
+        block = block.at[pl.ds(block.shape[0] - 8, 8)]
         gets.append(pltpu.make_async_copy(block, small.at[ids[p]], sem.at[4, p]))
     run(gets)
     sums[...] = jnp.zeros_like(sums)
     jadd[...] = jnp.zeros_like(jadd)
     finish(gets)
-    unpack(sp, ids[2 * half + sp], small, row_n, own_b, vecs, eadd, jadd)
+    unpack(sp, ids[dp + sp], small, row_n, own_b, vecs, eadd, jadd)
     gain, shift, add = vecs[6:7, :], vecs[7:8, :], eadd[...]
 
     @pl.loop(0, sp)
@@ -263,7 +274,7 @@
     gets = (
         copies_in([b.at[pl.ds(0, chunk)] for b in xs], x, chunk, sem.at[0])
         + copies_in([b.at[pl.ds(0, chunk)] for b in cots], cot, chunk, sem.at[1])
-        + placed(ids, jw_mine, jw_got, jw, rows, wide, sem.at[2])
+        + placed(ids, (jw_mine, jw_got), jw, rows, wide, sem.at[2])
     )
     run(gets)
     sums[...] = jnp.zeros_like(sums)
@@ -542,7 +553,7 @@
     chunk, width = xs[0].shape
     tokens = sp * chunk
     units = ew[0].shape[2]
-    dp = 2 * ew[0].shape[0]
+    dp = sum(stack.shape[0] for stack in ew)
     rows, per = width // dp, units // dp
     shape = jax.ShapeDtypeStruct
     outs = [
@@ -571,9 +582,9 @@
         pltpu.SemaphoreType.DMA((5, max(dp, sp))),
     ]
     return call(
-        functools.partial(mlp_kernel, sp, row_n, own_b),
+        functools.partial(mlp_kernel, sp, row_n, own_b, len(ew)),
         [ids, *xs, *cots, *ew, *sw],
-        [IN_SMEM] + [ANY] * (2 * sp + 4),
+        [IN_SMEM] + [ANY] * (2 * sp + 2 * len(ew)),
         outs,
         [ANY, ANY, ANY, ANY] + [IN_VMEM] * 5,
         scratch,
@@ -642,8 +653,8 @@
 
     xs = token_blocks(inputs.reshape(local, width), "sp")
     cots = token_blocks(cotangent.reshape(local, width), "sp")
-    shrink_w = halves(shrink_weight, "dp", bits_of(dp))
-    expand_w = halves(expand_pack, "dp", bits_of(dp))
+    shrink_w = pieces(shrink_weight, "dp", bits_of(dp))
+    expand_w = pieces(expand_pack, "dp", bits_of(dp))
     joined_w = halves(joined_part, "dp", bits_of(dp))
     dense_w = jnp.concatenate(halves(dense_part, "dp", bits_of(dp)), axis=0)
     dense_w = flip_bits(turn_bits(dense_w), "dp").reshape(heads * HD, width)

time: 219 us -> 216 us (0.986)
  waiting for transfers between devices: 100 us -> 84.9 us
  starting transfers between devices: 47.3 us -> 58.3 us
    ppermute x29 -> x31, waiting for transfers between devices: 97 us -> 81.6 us  [swap(): return lax.ppermute(value, axis, [(i, i ^ bit) for i in range(count)])]
    ppermute x29 -> x31, starting transfers between devices: 37.6 us -> 48.5 us  [swap(): return lax.ppermute(value, axis, [(i, i ^ bit) for i in range(count)])]
    unnamed x50 -> x66, local copies, waits for them, and re-layouts: 4.71 us -> 6.3 us
  transfers between devices with their start and end apart: 33 -> 35, of which waited for: 13 -> 12; matrix products, arithmetic and copies ran while one was open for 5% -> 5% of each run, Pallas kernels for 23% -> 23%
where the time goes in v3:
time: 216 us; the launch traced here: 214 us
  waiting for transfers between devices  84.9 us (39%)
  starting transfers between devices  58.3 us (27%)
  Pallas kernels  52.2 us (24%)
  other arithmetic  10 us (5%)
  local copies, waits for them, and re-layouts  6.93 us (3%)
    ppermute x31, waiting for transfers between devices, swap(): return lax.ppermute(value, axis, [(i, i ^ bit) for i in range(count)])  81.6 us
    pallas_call x7, Pallas kernels, call(): pl.pallas_call(body, in_specs=specs, out_shape=outs, out_specs=out_specs,...  52.2 us
    ppermute x31, starting transfers between devices, swap(): return lax.ppermute(value, axis, [(i, i ^ bit) for i in range(count)])  48.5 us
    unnamed x66, local copies, waits for them, and re-layouts  6.3 us
  transfers between devices with their start and end apart: 35, of which 12 were waited for; matrix products, arithmetic and copies ran while one was open for 5% of the time, Pallas kernels for 23%

profile of v3, /device:TPU:0, one launch (start us, length us, event | category | flops | bytes accessed | tf_op | source)
XLA Modules:
  0.0 213.5 jit_solution(17999809689739963842)
XLA Ops:
  0.7 4.1 %collective-permute-start.17 = (bf16[1,96,768]{2,1,0:T(8,128)(2,1)}, bf16[1,96,768]{2,1,0:T(8,128)(2,1)S(1)}, u32[]{:S(2)}, u32[]{:S(2)}) collective-permute-start(bf16[1,96,768]{2,1,0:T(8,128)(2,1)} %bitcast.62), channel_id=1, source_target_pairs={{0,16},{4,20},{8,24},{12,28},{16,0},{20,4},{24,8},{28,12},{1,17},{... | collective-permute-start | bytes 442376 | tf_op jit(solution)/shard_map/ppermute | solution.py:46
  4.8 1.5 collective-permute-start.19
  6.3 1.9 shard_map.272
  8.2 3.5 %all-to-all-start = ((bf16[4,56,768]{2,1,0:T(8,128)(2,1)}), bf16[4,56,768]{2,1,0:T(8,128)(2,1)S(1)}, u32[]{:S(2)}, u32[]{:S(2)}) async-start(bf16[4,56,768]{2,1,0:T(8,128)(2,1)} %shard_map.272), calls=%async_computation | async-start | bytes 688128 | tf_op jit(solution)/shard_map/all_to_all | solution.py:646
  11.7 2.0 collective-permute-start
  13.7 1.4 collective-permute-start.9
  15.1 0.7 broadcast_multiply_fusion
  15.8 6.0 %collective-permute-start.10 = (bf16[1,24,768]{2,1,0:T(8,128)(2,1)S(1)}, bf16[1,24,768]{2,1,0:T(8,128)(2,1)S(1)}, u32[]{:S(2)}, u32[]{:S(2)}) collective-permute-start(bf16[1,24,768]{2,1,0:T(8,128)(2,1)S(1)} %bitcast.51), channel_id=1, source_target_pairs={{0,16},{4,20},{8,24},{12,28},{16,0},{20,4},{24,8},{28,12},{1,17},{... | collective-permute-start | bytes 110600 | tf_op jit(solution)/shard_map/ppermute | solution.py:46
  21.9 1.8 multiply_sine_fusion
  23.8 3.5 %collective-permute-start.11 = (bf16[2,24,768]{2,1,0:T(8,128)(2,1)S(1)}, bf16[2,24,768]{2,1,0:T(8,128)(2,1)S(1)}, u32[]{:S(2)}, u32[]{:S(2)}) collective-permute-start(bf16[2,24,768]{2,1,0:T(8,128)(2,1)S(1)} %pad_maximum_fusion.8), channel_id=1, source_target_pairs={{0,8},{4,12},{8,0},{12,4},{16,24},{20,28},{24,16},{28,20},{1,9},{5... | collective-permute-start | bytes 221192 | tf_op jit(solution)/shard_map/ppermute | solution.py:46
  27.4 2.3 %collective-permute-done.11 = bf16[2,24,768]{2,1,0:T(8,128)(2,1)S(1)} collective-permute-done((bf16[2,24,768]{2,1,0:T(8,128)(2,1)S(1)}, bf16[2,24,768]{2,1,0:T(8,128)(2,1)S(1)}, u32[]{:S(2)}, u32[]{:S(2)}) %collective-permute-start.11) | collective-permute-done | bytes 73760 | tf_op jit(solution)/shard_map/ppermute | solution.py:46
  29.7 0.8 collective-permute-start.12
  30.6 2.2 %collective-permute-start.18 = (bf16[2,96,768]{2,1,0:T(8,128)(2,1)S(1)}, bf16[2,96,768]{2,1,0:T(8,128)(2,1)S(1)}, u32[]{:S(2)}, u32[]{:S(2)}) collective-permute-start(bf16[2,96,768]{2,1,0:T(8,128)(2,1)S(1)} %pad_maximum_fusion.5), channel_id=1, source_target_pairs={{0,8},{4,12},{8,0},{12,4},{16,24},{20,28},{24,16},{28,20},{1,9},{5... | collective-permute-start | bytes 884744 | tf_op jit(solution)/shard_map/ppermute | solution.py:46
  32.8 0.7 copy-done.2
  33.5 1.7 shard_map.273
  35.2 2.1 collective-permute-start.13
  37.3 0.6 pad_add_fusion.ids
  37.9 0.8 collective-permute-start.6
  38.8 3.7 %collective-permute-done.13.refs_9_ = bf16[1,104,768]{2,1,0:T(8,128)(2,1)S(1)} collective-permute-done((bf16[1,104,768]{2,1,0:T(8,128)(2,1)}, bf16[1,104,768]{2,1,0:T(8,128)(2,1)S(1)}, u32[]{:S(2)}, u32[]{:S(2)}) %collective-permute-start.13) | collective-permute-done | bytes 159776 | tf_op jit(solution)/shard_map/ppermute | solution.py:46
  42.5 8.0 %collective-permute-start.1 = (bf16[256,768]{1,0:T(8,128)(2,1)S(1)}, bf16[256,768]{1,0:T(8,128)(2,1)S(1)}, u32[]{:S(2)}, u32[]{:S(2)}) collective-permute-start(bf16[256,768]{1,0:T(8,128)(2,1)S(1)} %bitcast.45), channel_id=1, source_target_pairs={{0,1},{1,0},{2,3},{3,2},{4,5},{5,4},{6,7},{7,6},{8,9},{9,8},{10,11... | collective-permute-start | bytes 1179656 | tf_op jit(solution)/shard_map/ppermute | solution.py:46
  50.5 0.9 pad_maximum_fusion.3
  51.5 1.1 collective-permute-start.3
  53.0 9.6 %collective-permute-done.14.refs_10_ = bf16[2,104,768]{2,1,0:T(8,128)(2,1)S(1)} collective-permute-done((bf16[2,104,768]{2,1,0:T(8,128)(2,1)S(1)}, bf16[2,104,768]{2,1,0:T(8,128)(2,1)S(1)}, u32[]{:S(2)}, u32[]{:S(2)}) %collective-permute-start.14) | collective-permute-done | bytes 319520 | tf_op jit(solution)/shard_map/ppermute | solution.py:46
  63.0 0.5 collective-permute-start.5
  63.5 2.0 collective-permute-start.20
  65.7 4.2 %collective-permute-done.7 = bf16[2,96,640]{2,1,0:T(8,128)(2,1)S(1)} collective-permute-done((bf16[2,96,640]{2,1,0:T(8,128)(2,1)S(1)}, bf16[2,96,640]{2,1,0:T(8,128)(2,1)S(1)}, u32[]{:S(2)}, u32[]{:S(2)}) %collective-permute-start.7) | collective-permute-done | bytes 245792 | tf_op jit(solution)/shard_map/ppermute | solution.py:46
  69.9 2.0 collective-permute-start.15
  71.9 0.8 reverse_select_fusion
  72.7 16.9 %collective-permute-done.15.refs_11_ = bf16[1,104,768]{2,1,0:T(8,128)(2,1)S(1)} collective-permute-done((bf16[1,104,768]{2,1,0:T(8,128)(2,1)S(1)}, bf16[1,104,768]{2,1,0:T(8,128)(2,1)S(1)}, u32[]{:S(2)}, u32[]{:S(2)}) %collective-permute-start.15) | collective-permute-done | bytes 159776 | tf_op jit(solution)/shard_map/ppermute | solution.py:46
  89.7 1.7 collective-permute-start.8
  91.5 0.7 copy-done.29
  92.4 0.7 copy-done.24
  93.2 0.8 copy-done.23
  93.9 17.1 %shard_map.274 = (bf16[4,96,768]{2,1,0:T(8,128)(2,1)}, bf16[4,96,768]{2,1,0:T(8,128)(2,1)}, bf16[4,96,768]{2,1,0:T(8,128)(2,1)}, bf16[4,96,768]{2,1,0:T(8,128)(2...) custom-call(s32[21]{0:T(128)} %pad_add_fusion.ids, ...), custom_call_target="tpu_custom_call" | custom-call | flops 12079595520 | bytes 11178068 | tf_op jit(solution)/shard_map/pallas_call | solution.py:421
  111.0 1.8 collective-permute-start.26
  112.8 0.8 copy-done.22
  113.6 24.2 %shard_map.275 = (bf16[4,104,768]{2,1,0:T(8,128)(2,1)}, bf16[4,104,768]{2,1,0:T(8,128)(2,1)}, bf16[2,2,256,768]{3,2,1,0:T(8,128)(2,1)}, bf16[2,2,256,768]{3,2,1,0:T(8,128)(2,1)}) custom-call(s32[21]{0:T(128)} %pad_add_fusion.ids, bf16[256,768]{1,0:T(8,128)(2,1)} %bitcast.43, bf16[256,768]{1,0:T(8,128)(2,1)} %copy-done.25, bf16[256,768]{1,0:T(8,128)(2,1)} %copy-done.26, ...), custom_call_target="tpu_custom_call" | custom-call | flops 12079595520 | bytes 12587092 | tf_op jit(solution)/shard_map/pallas_call | solution.py:421
  137.9 0.3 collective-permute-start.30
  138.3 1.7 collective-permute-start.23
  140.5 13.7 %collective-permute-done.30 = bf16[4,96,768]{2,1,0:T(8,128)(2,1)S(1)} collective-permute-done((bf16[4,96,768]{2,1,0:T(8,128)(2,1)S(1)}, bf16[4,96,768]{2,1,0:T(8,128)(2,1)S(1)}, u32[]{:S(2)}, u32[]{:S(2)}) %collective-permute-start.30) | collective-permute-done | bytes 589856 | tf_op jit(solution)/shard_map/ppermute | solution.py:46
  154.3 0.4 collective-permute-start.31
  154.7 13.2 %collective-permute-done.23 = bf16[4,104,768]{2,1,0:T(8,128)(2,1)S(1)} collective-permute-done((bf16[4,104,768]{2,1,0:T(8,128)(2,1)}, bf16[4,104,768]{2,1,0:T(8,128)(2,1)S(1)}, u32[]{:S(2)}, u32[]{:S(2)}) %collective-permute-start.23) | collective-permute-done | bytes 639008 | tf_op jit(solution)/shard_map/ppermute | solution.py:46
  168.0 0.4 collective-permute-start.24
  168.4 5.3 %collective-permute-done.27 = bf16[2,96,768]{2,1,0:T(8,128)(2,1)S(1)} collective-permute-done((bf16[2,96,768]{2,1,0:T(8,128)(2,1)S(1)}, bf16[2,96,768]{2,1,0:T(8,128)(2,1)S(1)}, u32[]{:S(2)}, u32[]{:S(2)}) %collective-permute-start.27) | collective-permute-done | bytes 294944 | tf_op jit(solution)/shard_map/ppermute | solution.py:46
  173.6 0.8 fusion.5
  174.5 1.5 add_convert_fusion
  175.9 1.4 collective-permute-start.22
  177.4 0.8 fusion
  178.1 2.5 %collective-permute-start.25 = (bf16[1,104,768]{2,1,0:T(8,128)(2,1)S(1)}, bf16[1,104,768]{2,1,0:T(8,128)(2,1)S(1)}, u32[]{:S(2)}, u32[]{:S(2)}) collective-permute-start(bf16[1,104,768]{2,1,0:T(8,128)(2,1)S(1)} %get-tuple-element.80), channel_id=1, source_target_pairs={{0,16},{4,20},{8,24},{12,28},{16,0},{20,4},{24,8},{28,12},{1,17},{... | collective-permute-start | bytes 479240 | tf_op jit(solution)/shard_map/ppermute | solution.py:46
  180.7 0.5 collective-permute-start.32
  181.2 9.0 %collective-permute-done.28 = bf16[1,96,768]{2,1,0:T(8,128)(2,1)S(1)} collective-permute-done((bf16[1,96,768]{2,1,0:T(8,128)(2,1)S(1)}, bf16[1,96,768]{2,1,0:T(8,128)(2,1)S(1)}, u32[]{:S(2)}, u32[]{:S(2)}) %collective-permute-start.28) | collective-permute-done | bytes 147488 | tf_op jit(solution)/shard_map/ppermute | solution.py:46
  190.2 3.4 %collective-permute-done.25 = bf16[1,104,768]{2,1,0:T(8,128)(2,1)S(1)} collective-permute-done((bf16[1,104,768]{2,1,0:T(8,128)(2,1)S(1)}, bf16[1,104,768]{2,1,0:T(8,128)(2,1)S(1)}, u32[]{:S(2)}, u32[]{:S(2)}) %collective-permute-start.25) | collective-permute-done | bytes 159776 | tf_op jit(solution)/shard_map/ppermute | solution.py:46
  193.6 0.7 copy-done.16
  194.3 2.0 shard_map.277
  196.3 3.5 %all-to-all-start.1 = ((bf16[4,56,768]{2,1,0:T(8,128)(2,1)}), bf16[4,56,768]{2,1,0:T(8,128)(2,1)S(1)}, u32[]{:S(2)}, u32[]{:S(2)}) async-start(bf16[4,56,768]{2,1,0:T(8,128)(2,1)} %get-tuple-element.58), calls=%async_computation.1 | async-start | bytes 688128 | tf_op jit(solution)/shard_map/all_to_all | solution.py:711
  199.8 0.6 stack.20.at
  200.4 1.4 collective-permute-start.29
  201.8 0.8 fusion.4
  202.6 0.6 convert_element_type.135
  203.2 3.4 %all-to-all-done.1.last = bf16[4,56,768]{2,1,0:T(8,128)(2,1)S(1)} async-done(((bf16[4,56,768]{2,1,0:T(8,128)(2,1)}), bf16[4,56,768]{2,1,0:T(8,128)(2,1)S(1)}, u32[]{:S(2)}, u32[]{:S(2)}) %all-to-all-start.1) | async-done | bytes 344096 | tf_op jit(solution)/shard_map/all_to_all | solution.py:711
  206.6 0.7 copy-done.1
  207.3 1.9 shard_map.278
  209.2 0.9 copy-done.3
  210.1 3.4 %shard_map.276 = (bf16[256,768]{1,0:T(8,128)(2,1)}, f32[256,768]{1,0:T(8,128)}) custom-call(bf16[256,768]{1,0:T(8,128)(2,1)} %bitcast.44, bf16[256,768]{1,0:T(8,128)(2,1)} %bitcast.48, f32[2,256,768]{2,1,0:T(8,128)} %get-tuple-element.73.keep, bf16[2,256,768]{2,1,0:T(8,128)(2,1)} %bitcast.37, f32[8,768]{1,0:T(8,128)} %get-tuple-element.48.refs_16_.add), custom_call_target="tpu_custom_call" | custom-call | bytes 4349952 | tf_op jit(solution)/shard_map/pallas_call | solution.py:421
  (108 shorter events, 2.5 us)
Async XLA Ops:
  0.6 26.7 %copy-start.19 = (s32[8]{0:T(128)S(1)}, s32[8]{0:T(128)}, u32[]{:S(2)}) copy-start(s32[8]{0:T(128)} %constant.76.clone) | copy-start | bytes 100
  0.7 26.7 %copy-start.20 = (s32[8]{0:T(128)S(1)}, s32[8]{0:T(128)}, u32[]{:S(2)}) copy-start(s32[8]{0:T(128)} %constant.77.clone) | copy-start | bytes 100
  0.7 29.9 %copy-start.18 = (bf16[96,768]{1,0:T(8,128)(2,1)S(1)}, bf16[96,768]{1,0:T(8,128)(2,1)}, u32[]{:S(2)}) copy-start(bf16[96,768]{1,0:T(8,128)(2,1)} %param.25) | copy-start | bytes 442372
  0.7 29.9 %collective-permute-start.17 = (bf16[1,96,768]{2,1,0:T(8,128)(2,1)}, bf16[1,96,768]{2,1,0:T(8,128)(2,1)S(1)}, u32[]{:S(2)}, u32[]{:S(2)}) collective-permute-start(bf16[1,96,768]{2,1,0:T(8,128)(2,1)} %bitcast.62), channel_id=1, source_target_pairs={{0,16},{4,20},{8,24},{12,28},{16,0},{20,4},{24,8},{28,12},{1,17},{... | collective-permute-start | bytes 442376 | tf_op jit(solution)/shard_map/ppermute | solution.py:46
  4.8 46.7 %collective-permute-start.19 = (bf16[1,96,768]{2,1,0:T(8,128)(2,1)}, bf16[1,96,768]{2,1,0:T(8,128)(2,1)S(1)}, u32[]{:S(2)}, u32[]{:S(2)}) collective-permute-start(bf16[1,96,768]{2,1,0:T(8,128)(2,1)} %bitcast.63), channel_id=1, source_target_pairs={{0,4},{4,0},{8,12},{12,8},{16,20},{20,16},{24,28},{28,24},{1,5},{5... | collective-permute-start | bytes 442376 | tf_op jit(solution)/shard_map/ppermute | solution.py:46
  8.2 24.5 %all-to-all-start = ((bf16[4,56,768]{2,1,0:T(8,128)(2,1)}), bf16[4,56,768]{2,1,0:T(8,128)(2,1)S(1)}, u32[]{:S(2)}, u32[]{:S(2)}) async-start(bf16[4,56,768]{2,1,0:T(8,128)(2,1)} %shard_map.272), calls=%async_computation | async-start | bytes 688128 | tf_op jit(solution)/shard_map/all_to_all | solution.py:646
  11.7 30.8 %copy-start.11 = (bf16[2,128,768]{2,1,0:T(8,128)(2,1)S(1)}, bf16[2,128,768]{2,1,0:T(8,128)(2,1)}, u32[]{:S(2)}) copy-start(bf16[2,128,768]{2,1,0:T(8,128)(2,1)} %param.17) | copy-start | bytes 1179652
  11.7 51.2 %collective-permute-start = (bf16[256,768]{1,0:T(8,128)(2,1)}, bf16[256,768]{1,0:T(8,128)(2,1)S(1)}, u32[]{:S(2)}, u32[]{:S(2)}) collective-permute-start(bf16[256,768]{1,0:T(8,128)(2,1)} %bitcast.41), channel_id=1, source_target_pairs={{0,2},{1,3},{2,0},{3,1},{4,6},{5,7},{6,4},{7,5},{8,10},{9,11},{10,... | collective-permute-start | bytes 1179656 | tf_op jit(solution)/shard_map/ppermute | solution.py:46
  13.7 2.2 %collective-permute-start.9 = (bf16[24,768]{1,0:T(8,128)(2,1)}, bf16[24,768]{1,0:T(8,128)(2,1)S(1)}, u32[]{:S(2)}, u32[]{:S(2)}) collective-permute-start(bf16[24,768]{1,0:T(8,128)(2,1)} %param.21), channel_id=1, source_target_pairs={{0,0},{1,4},{2,8},{3,12},{4,16},{5,20},{6,24},{7,28},{8,1},{9,5},{... | collective-permute-start | bytes 110600 | tf_op jit(solution)/shard_map/ppermute | solution.py:81
  15.8 8.0 %collective-permute-start.10 = (bf16[1,24,768]{2,1,0:T(8,128)(2,1)S(1)}, bf16[1,24,768]{2,1,0:T(8,128)(2,1)S(1)}, u32[]{:S(2)}, u32[]{:S(2)}) collective-permute-start(bf16[1,24,768]{2,1,0:T(8,128)(2,1)S(1)} %bitcast.51), channel_id=1, source_target_pairs={{0,16},{4,20},{8,24},{12,28},{16,0},{20,4},{24,8},{28,12},{1,17},{... | collective-permute-start | bytes 110600 | tf_op jit(solution)/shard_map/ppermute | solution.py:46
  23.8 27.7 %copy-start.12 = (bf16[2,128,768]{2,1,0:T(8,128)(2,1)S(1)}, bf16[2,128,768]{2,1,0:T(8,128)(2,1)}, u32[]{:S(2)}) copy-start(bf16[2,128,768]{2,1,0:T(8,128)(2,1)} %param.18) | copy-start | bytes 1179652
  23.8 5.9 %collective-permute-start.11 = (bf16[2,24,768]{2,1,0:T(8,128)(2,1)S(1)}, bf16[2,24,768]{2,1,0:T(8,128)(2,1)S(1)}, u32[]{:S(2)}, u32[]{:S(2)}) collective-permute-start(bf16[2,24,768]{2,1,0:T(8,128)(2,1)S(1)} %pad_maximum_fusion.8), channel_id=1, source_target_pairs={{0,8},{4,12},{8,0},{12,4},{16,24},{20,28},{24,16},{28,20},{1,9},{5... | collective-permute-start | bytes 221192 | tf_op jit(solution)/shard_map/ppermute | solution.py:46
  29.7 8.2 %collective-permute-start.12 = (bf16[4,24,768]{2,1,0:T(8,128)(2,1)S(1)}, bf16[4,24,768]{2,1,0:T(8,128)(2,1)S(1)}, u32[]{:S(2)}, u32[]{:S(2)}) collective-permute-start(bf16[4,24,768]{2,1,0:T(8,128)(2,1)S(1)} %pad_maximum_fusion.7), channel_id=1, source_target_pairs={{0,4},{4,0},{8,12},{12,8},{16,20},{20,16},{24,28},{28,24},{1,5},{5... | collective-permute-start | bytes 442376 | tf_op jit(solution)/shard_map/ppermute | solution.py:46
  30.6 22.3 %copy-start.6 = (bf16[1,96,768]{2,1,0:T(8,128)(2,1)}, bf16[1,96,768]{2,1,0:T(8,128)(2,1)S(1)}, u32[]{:S(2)}) copy-start(bf16[1,96,768]{2,1,0:T(8,128)(2,1)S(1)} %collective-permute-done.17.refs_14_) | copy-start | bytes 442372
  30.6 22.2 %collective-permute-start.18 = (bf16[2,96,768]{2,1,0:T(8,128)(2,1)S(1)}, bf16[2,96,768]{2,1,0:T(8,128)(2,1)S(1)}, u32[]{:S(2)}, u32[]{:S(2)}) collective-permute-start(bf16[2,96,768]{2,1,0:T(8,128)(2,1)S(1)} %pad_maximum_fusion.5), channel_id=1, source_target_pairs={{0,8},{4,12},{8,0},{12,4},{16,24},{20,28},{24,16},{28,20},{1,9},{5... | collective-permute-start | bytes 884744 | tf_op jit(solution)/shard_map/ppermute | solution.py:46
  35.2 17.6 %copy-start.10 = (bf16[96,640]{1,0:T(8,128)(2,1)S(1)}, bf16[96,640]{1,0:T(8,128)(2,1)}, u32[]{:S(2)}) copy-start(bf16[96,640]{1,0:T(8,128)(2,1)} %get-tuple-element.43) | copy-start | bytes 368644
  35.2 7.3 %collective-permute-start.13 = (bf16[1,104,768]{2,1,0:T(8,128)(2,1)}, bf16[1,104,768]{2,1,0:T(8,128)(2,1)S(1)}, u32[]{:S(2)}, u32[]{:S(2)}) collective-permute-start(bf16[1,104,768]{2,1,0:T(8,128)(2,1)} %bitcast.56), channel_id=1, source_target_pairs={{0,16},{4,20},{8,24},{12,28},{16,0},{20,4},{24,8},{28,12},{1,17},{... | collective-permute-start | bytes 479240 | tf_op jit(solution)/shard_map/ppermute | solution.py:46
  37.9 14.7 %collective-permute-start.6 = (bf16[1,96,640]{2,1,0:T(8,128)(2,1)}, bf16[1,96,640]{2,1,0:T(8,128)(2,1)S(1)}, u32[]{:S(2)}, u32[]{:S(2)}) collective-permute-start(bf16[1,96,640]{2,1,0:T(8,128)(2,1)} %bitcast.38), channel_id=1, source_target_pairs={{0,16},{4,20},{8,24},{12,28},{16,0},{20,4},{24,8},{28,12},{1,17},{... | collective-permute-start | bytes 368648 | tf_op jit(solution)/shard_map/ppermute | solution.py:46
  42.5 20.4 %copy-start.4 = (bf16[1,104,768]{2,1,0:T(8,128)(2,1)}, bf16[1,104,768]{2,1,0:T(8,128)(2,1)S(1)}, u32[]{:S(2)}) copy-start(bf16[1,104,768]{2,1,0:T(8,128)(2,1)S(1)} %collective-permute-done.13.refs_9_) | copy-start | bytes 479236
  42.5 21.0 %collective-permute-start.1 = (bf16[256,768]{1,0:T(8,128)(2,1)S(1)}, bf16[256,768]{1,0:T(8,128)(2,1)S(1)}, u32[]{:S(2)}, u32[]{:S(2)}) collective-permute-start(bf16[256,768]{1,0:T(8,128)(2,1)S(1)} %bitcast.45), channel_id=1, source_target_pairs={{0,1},{1,0},{2,3},{3,2},{4,5},{5,4},{6,7},{7,6},{8,9},{9,8},{10,11... | collective-permute-start | bytes 1179656 | tf_op jit(solution)/shard_map/ppermute | solution.py:46
  51.5 12.0 %copy-start.32 = (bf16[1,96,768]{2,1,0:T(8,128)(2,1)}, bf16[1,96,768]{2,1,0:T(8,128)(2,1)S(1)}, u32[]{:S(2)}) copy-start(bf16[1,96,768]{2,1,0:T(8,128)(2,1)S(1)} %collective-permute-done.19.refs_16_) | copy-start | bytes 442372
  51.5 11.5 %collective-permute-start.3 = (bf16[256,768]{1,0:T(8,128)(2,1)S(1)}, bf16[256,768]{1,0:T(8,128)(2,1)S(1)}, u32[]{:S(2)}, u32[]{:S(2)}) collective-permute-start(bf16[256,768]{1,0:T(8,128)(2,1)S(1)} %bitcast.49), channel_id=1, source_target_pairs={{0,2},{1,3},{2,0},{3,1},{4,6},{5,7},{6,4},{7,5},{8,10},{9,11},{10,... | collective-permute-start | bytes 1179656 | tf_op jit(solution)/shard_map/ppermute | solution.py:46
  52.6 13.0 %collective-permute-start.4 = (bf16[256,768]{1,0:T(8,128)(2,1)S(1)}, bf16[256,768]{1,0:T(8,128)(2,1)S(1)}, u32[]{:S(2)}, u32[]{:S(2)}) collective-permute-start(bf16[256,768]{1,0:T(8,128)(2,1)S(1)} %bitcast.50), channel_id=1, source_target_pairs={{0,1},{1,0},{2,3},{3,2},{4,5},{5,4},{6,7},{7,6},{8,9},{9,8},{10,11... | collective-permute-start | bytes 1179656 | tf_op jit(solution)/shard_map/ppermute | solution.py:46
  52.8 12.9 %copy-start.14 = (bf16[2,96,768]{2,1,0:T(8,128)(2,1)}, bf16[2,96,768]{2,1,0:T(8,128)(2,1)S(1)}, u32[]{:S(2)}) copy-start(bf16[2,96,768]{2,1,0:T(8,128)(2,1)S(1)} %collective-permute-done.18.refs_15_) | copy-start | bytes 884740
  52.8 9.8 %collective-permute-start.14 = (bf16[2,104,768]{2,1,0:T(8,128)(2,1)S(1)}, bf16[2,104,768]{2,1,0:T(8,128)(2,1)S(1)}, u32[]{:S(2)}, u32[]{:S(2)}) collective-permute-start(bf16[2,104,768]{2,1,0:T(8,128)(2,1)S(1)} %pad_maximum_fusion.3), channel_id=1, source_target_pairs={{0,8},{4,12},{8,0},{12,4},{16,24},{20,28},{24,16},{28,20},{1,9},{5... | collective-permute-start | bytes 958472 | tf_op jit(solution)/shard_map/ppermute | solution.py:46
  52.9 17.1 %copy-start.15 = (bf16[104,768]{1,0:T(8,128)(2,1)S(1)}, bf16[104,768]{1,0:T(8,128)(2,1)}, u32[]{:S(2)}) copy-start(bf16[104,768]{1,0:T(8,128)(2,1)} %get-tuple-element.44) | copy-start | bytes 479236
  62.6 29.8 %copy-start.13 = (bf16[2,104,768]{2,1,0:T(8,128)(2,1)}, bf16[2,104,768]{2,1,0:T(8,128)(2,1)S(1)}, u32[]{:S(2)}) copy-start(bf16[2,104,768]{2,1,0:T(8,128)(2,1)S(1)} %collective-permute-done.14.refs_10_) | copy-start | bytes 958468
  62.6 7.3 %collective-permute-start.7 = (bf16[2,96,640]{2,1,0:T(8,128)(2,1)S(1)}, bf16[2,96,640]{2,1,0:T(8,128)(2,1)S(1)}, u32[]{:S(2)}, u32[]{:S(2)}) collective-permute-start(bf16[2,96,640]{2,1,0:T(8,128)(2,1)S(1)} %pad_maximum_fusion.6), channel_id=1, source_target_pairs={{0,8},{4,12},{8,0},{12,4},{16,24},{20,28},{24,16},{28,20},{1,9},{5... | collective-permute-start | bytes 737288 | tf_op jit(solution)/shard_map/ppermute | solution.py:46
  62.9 29.5 %copy-start.25 = (bf16[256,768]{1,0:T(8,128)(2,1)}, bf16[256,768]{1,0:T(8,128)(2,1)S(1)}, u32[]{:S(2)}) copy-start(bf16[256,768]{1,0:T(8,128)(2,1)S(1)} %collective-permute-done.refs_1_) | copy-start | bytes 1179652
  62.9 28.5 %collective-permute-start.2 = (bf16[256,768]{1,0:T(8,128)(2,1)S(1)}, bf16[256,768]{1,0:T(8,128)(2,1)S(1)}, u32[]{:S(2)}, u32[]{:S(2)}) collective-permute-start(bf16[256,768]{1,0:T(8,128)(2,1)S(1)} %collective-permute-done.refs_1_), channel_id=1, source_target_pairs={{0,1},{1,0},{2,3},{3,2},{4,5},{5,4},{6,7},{7,6},{8,9},{9,8},{10,11... | collective-permute-start | bytes 1179656 | tf_op jit(solution)/shard_map/ppermute | solution.py:46
  63.0 28.4 %copy-start.27 = (bf16[256,768]{1,0:T(8,128)(2,1)}, bf16[256,768]{1,0:T(8,128)(2,1)S(1)}, u32[]{:S(2)}) copy-start(bf16[256,768]{1,0:T(8,128)(2,1)S(1)} %collective-permute-done.3.refs_5_) | copy-start | bytes 1179652
  63.0 28.4 %collective-permute-start.5 = (bf16[256,768]{1,0:T(8,128)(2,1)S(1)}, bf16[256,768]{1,0:T(8,128)(2,1)S(1)}, u32[]{:S(2)}, u32[]{:S(2)}) collective-permute-start(bf16[256,768]{1,0:T(8,128)(2,1)S(1)} %collective-permute-done.3.refs_5_), channel_id=1, source_target_pairs={{0,1},{1,0},{2,3},{3,2},{4,5},{5,4},{6,7},{7,6},{8,9},{9,8},{10,11... | collective-permute-start | bytes 1179656 | tf_op jit(solution)/shard_map/ppermute | solution.py:46
  63.5 28.9 %copy-start.26 = (bf16[256,768]{1,0:T(8,128)(2,1)}, bf16[256,768]{1,0:T(8,128)(2,1)S(1)}, u32[]{:S(2)}) copy-start(bf16[256,768]{1,0:T(8,128)(2,1)S(1)} %collective-permute-done.1.refs_2_) | copy-start | bytes 1179652
  63.5 27.9 %collective-permute-start.20 = (bf16[3,96,768]{2,1,0:T(8,128)(2,1)S(1)}, bf16[3,96,768]{2,1,0:T(8,128)(2,1)S(1)}, u32[]{:S(2)}, u32[]{:S(2)}) collective-permute-start(bf16[3,96,768]{2,1,0:T(8,128)(2,1)S(1)} %pad_maximum_fusion.2), channel_id=1, source_target_pairs={{0,4},{4,0},{8,12},{12,8},{16,20},{20,16},{24,28},{28,24},{1,5},{5... | collective-permute-start | bytes 1327112 | tf_op jit(solution)/shard_map/ppermute | solution.py:46
  65.6 25.9 %copy-start.28 = (bf16[256,768]{1,0:T(8,128)(2,1)}, bf16[256,768]{1,0:T(8,128)(2,1)S(1)}, u32[]{:S(2)}) copy-start(bf16[256,768]{1,0:T(8,128)(2,1)S(1)} %collective-permute-done.4.refs_6_) | copy-start | bytes 1179652
  65.6 26.8 %collective-permute-start.16 = (bf16[3,104,768]{2,1,0:T(8,128)(2,1)S(1)}, bf16[3,104,768]{2,1,0:T(8,128)(2,1)S(1)}, u32[]{:S(2)}, u32[]{:S(2)}) collective-permute-start(bf16[3,104,768]{2,1,0:T(8,128)(2,1)S(1)} %pad_maximum_fusion.1), channel_id=1, source_target_pairs={{0,4},{4,0},{8,12},{12,8},{16,20},{20,16},{24,28},{28,24},{1,5},{5... | collective-permute-start | bytes 1437704 | tf_op jit(solution)/shard_map/ppermute | solution.py:46
  69.9 19.8 %collective-permute-start.15 = (bf16[1,104,768]{2,1,0:T(8,128)(2,1)S(1)}, bf16[1,104,768]{2,1,0:T(8,128)(2,1)S(1)}, u32[]{:S(2)}, u32[]{:S(2)}) collective-permute-start(bf16[1,104,768]{2,1,0:T(8,128)(2,1)S(1)} %bitcast.59), channel_id=1, source_target_pairs={{0,4},{4,0},{8,12},{12,8},{16,20},{20,16},{24,28},{28,24},{1,5},{5... | collective-permute-start | bytes 479240 | tf_op jit(solution)/shard_map/ppermute | solution.py:46
  72.7 38.3 %copy-start.9 = (bf16[4,96,640]{2,1,0:T(8,128)(2,1)}, bf16[4,96,640]{2,1,0:T(8,128)(2,1)S(1)}, u32[]{:S(2)}) copy-start(bf16[4,96,640]{2,1,0:T(8,128)(2,1)S(1)} %pad_maximum_fusion.refs_8_) | copy-start | bytes 1474564
  89.7 2.7 %copy-start.31 = (bf16[1,104,768]{2,1,0:T(8,128)(2,1)}, bf16[1,104,768]{2,1,0:T(8,128)(2,1)S(1)}, u32[]{:S(2)}) copy-start(bf16[1,104,768]{2,1,0:T(8,128)(2,1)S(1)} %collective-permute-done.15.refs_11_) | copy-start | bytes 479236
  89.7 23.1 %collective-permute-start.8 = (bf16[4,96,640]{2,1,0:T(8,128)(2,1)S(1)}, bf16[4,96,640]{2,1,0:T(8,128)(2,1)S(1)}, u32[]{:S(2)}, u32[]{:S(2)}) collective-permute-start(bf16[4,96,640]{2,1,0:T(8,128)(2,1)S(1)} %pad_maximum_fusion.refs_8_), channel_id=1, source_target_pairs={{0,4},{4,0},{8,12},{12,8},{16,20},{20,16},{24,28},{28,24},{1,5},{5... | collective-permute-start | bytes 1474568 | tf_op jit(solution)/shard_map/ppermute | solution.py:46
  91.4 0.8 copy-start.29
  91.4 0.9 copy-start.30
  93.2 0.8 copy-start.23
  111.0 29.0 %collective-permute-start.26 = (bf16[4,96,768]{2,1,0:T(8,128)(2,1)}, bf16[4,96,768]{2,1,0:T(8,128)(2,1)S(1)}, u32[]{:S(2)}, u32[]{:S(2)}) collective-permute-start(bf16[4,96,768]{2,1,0:T(8,128)(2,1)} %get-tuple-element.57), channel_id=1, source_target_pairs={{0,8},{4,12},{8,0},{12,4},{16,24},{20,28},{24,16},{28,20},{1,9},{5... | collective-permute-start | bytes 1769480 | tf_op jit(solution)/shard_map/ppermute | solution.py:46
  112.8 0.8 copy-start.22
  113.6 24.3 %copy-start.21 = (bf16[4,96,768]{2,1,0:T(8,128)(2,1)S(1)}, bf16[4,96,768]{2,1,0:T(8,128)(2,1)}, u32[]{:S(2)}) copy-start(bf16[4,96,768]{2,1,0:T(8,128)(2,1)} %get-tuple-element.66) | copy-start | bytes 1769476
  113.6 26.4 %copy-start.8 = (bf16[4,96,768]{2,1,0:T(8,128)(2,1)S(1)}, bf16[4,96,768]{2,1,0:T(8,128)(2,1)}, u32[]{:S(2)}) copy-start(bf16[4,96,768]{2,1,0:T(8,128)(2,1)} %get-tuple-element.56) | copy-start | bytes 1769476
  137.8 16.4 %copy-start.7 = (bf16[4,96,768]{2,1,0:T(8,128)(2,1)S(1)}, bf16[4,96,768]{2,1,0:T(8,128)(2,1)}, u32[]{:S(2)}) copy-start(bf16[4,96,768]{2,1,0:T(8,128)(2,1)} %get-tuple-element.65) | copy-start | bytes 1769476
  137.8 36.6 %collective-permute-start.21 = (bf16[2,2,256,768]{3,2,1,0:T(8,128)(2,1)}, bf16[2,2,256,768]{3,2,1,0:T(8,128)(2,1)S(1)}, u32[]{:S(2)}, u32[]{:S(2)}) collective-permute-start(bf16[2,2,256,768]{3,2,1,0:T(8,128)(2,1)} %get-tuple-element.51), channel_id=1, source_target_pairs={{0,1},{1,0},{2,3},{3,2},{4,5},{5,4},{6,7},{7,6},{8,9},{9,8},{10,11... | collective-permute-start | bytes 4718600 | tf_op jit(solution)/shard_map/ppermute | solution.py:46
  137.9 16.3 %collective-permute-start.30 = (bf16[4,96,768]{2,1,0:T(8,128)(2,1)S(1)}, bf16[4,96,768]{2,1,0:T(8,128)(2,1)S(1)}, u32[]{:S(2)}, u32[]{:S(2)}) collective-permute-start(bf16[4,96,768]{2,1,0:T(8,128)(2,1)S(1)} %copy-done.21), channel_id=1, source_target_pairs={{0,4},{4,0},{8,12},{12,8},{16,20},{20,16},{24,28},{28,24},{1,5},{5... | collective-permute-start | bytes 1769480 | tf_op jit(solution)/shard_map/ppermute | solution.py:46
  138.3 29.6 %collective-permute-start.23 = (bf16[4,104,768]{2,1,0:T(8,128)(2,1)}, bf16[4,104,768]{2,1,0:T(8,128)(2,1)S(1)}, u32[]{:S(2)}, u32[]{:S(2)}) collective-permute-start(bf16[4,104,768]{2,1,0:T(8,128)(2,1)} %get-tuple-element.55), channel_id=1, source_target_pairs={{0,4},{4,0},{8,12},{12,8},{16,20},{20,16},{24,28},{28,24},{1,5},{5... | collective-permute-start | bytes 1916936 | tf_op jit(solution)/shard_map/ppermute | solution.py:46
  140.0 27.9 %copy-start.5 = (bf16[4,104,768]{2,1,0:T(8,128)(2,1)S(1)}, bf16[4,104,768]{2,1,0:T(8,128)(2,1)}, u32[]{:S(2)}) copy-start(bf16[4,104,768]{2,1,0:T(8,128)(2,1)} %get-tuple-element.54) | copy-start | bytes 1916932
  140.1 33.5 %collective-permute-start.27 = (bf16[2,96,768]{2,1,0:T(8,128)(2,1)S(1)}, bf16[2,96,768]{2,1,0:T(8,128)(2,1)S(1)}, u32[]{:S(2)}, u32[]{:S(2)}) collective-permute-start(bf16[2,96,768]{2,1,0:T(8,128)(2,1)S(1)} %get-tuple-element.78), channel_id=1, source_target_pairs={{0,4},{4,0},{8,12},{12,8},{16,20},{20,16},{24,28},{28,24},{1,5},{5... | collective-permute-start | bytes 884744 | tf_op jit(solution)/shard_map/ppermute | solution.py:46
  154.3 26.3 %collective-permute-start.31 = (bf16[2,96,768]{2,1,0:T(8,128)(2,1)S(1)}, bf16[2,96,768]{2,1,0:T(8,128)(2,1)S(1)}, u32[]{:S(2)}, u32[]{:S(2)}) collective-permute-start(bf16[2,96,768]{2,1,0:T(8,128)(2,1)S(1)} %get-tuple-element.76), channel_id=1, source_target_pairs={{0,8},{4,12},{8,0},{12,4},{16,24},{20,28},{24,16},{28,20},{1,9},{5... | collective-permute-start | bytes 884744 | tf_op jit(solution)/shard_map/ppermute | solution.py:46
  167.9 6.6 %copy-start = (bf16[2,2,256,768]{3,2,1,0:T(8,128)(2,1)S(1)}, bf16[2,2,256,768]{3,2,1,0:T(8,128)(2,1)}, u32[]{:S(2)}) copy-start(bf16[2,2,256,768]{3,2,1,0:T(8,128)(2,1)} %get-tuple-element.50) | copy-start | bytes 4718596
  168.0 9.4 %collective-permute-start.24 = (bf16[2,104,768]{2,1,0:T(8,128)(2,1)S(1)}, bf16[2,104,768]{2,1,0:T(8,128)(2,1)S(1)}, u32[]{:S(2)}, u32[]{:S(2)}) collective-permute-start(bf16[2,104,768]{2,1,0:T(8,128)(2,1)S(1)} %get-tuple-element.74), channel_id=1, source_target_pairs={{0,8},{4,12},{8,0},{12,4},{16,24},{20,28},{24,16},{28,20},{1,9},{5... | collective-permute-start | bytes 958472 | tf_op jit(solution)/shard_map/ppermute | solution.py:46
  174.4 15.8 %collective-permute-start.28 = (bf16[1,96,768]{2,1,0:T(8,128)(2,1)S(1)}, bf16[1,96,768]{2,1,0:T(8,128)(2,1)S(1)}, u32[]{:S(2)}, u32[]{:S(2)}) collective-permute-start(bf16[1,96,768]{2,1,0:T(8,128)(2,1)S(1)} %get-tuple-element.82), channel_id=1, source_target_pairs={{0,16},{4,20},{8,24},{12,28},{16,0},{20,4},{24,8},{28,12},{1,17},{... | collective-permute-start | bytes 442376 | tf_op jit(solution)/shard_map/ppermute | solution.py:46
  175.9 33.3 %collective-permute-start.22 = (bf16[1,2,256,768]{3,2,1,0:T(8,128)(2,1)S(1)}, bf16[1,2,256,768]{3,2,1,0:T(8,128)(2,1)S(1)}, u32[]{:S(2)}, u32[]{:S(2)}) collective-permute-start(bf16[1,2,256,768]{3,2,1,0:T(8,128)(2,1)S(1)} %get-tuple-element.72), channel_id=1, source_target_pairs={{0,2},{1,3},{2,0},{3,1},{4,6},{5,7},{6,4},{7,5},{8,10},{9,11},{10,... | collective-permute-start | bytes 2359304 | tf_op jit(solution)/shard_map/ppermute | solution.py:46
  178.1 15.5 %collective-permute-start.25 = (bf16[1,104,768]{2,1,0:T(8,128)(2,1)S(1)}, bf16[1,104,768]{2,1,0:T(8,128)(2,1)S(1)}, u32[]{:S(2)}, u32[]{:S(2)}) collective-permute-start(bf16[1,104,768]{2,1,0:T(8,128)(2,1)S(1)} %get-tuple-element.80), channel_id=1, source_target_pairs={{0,16},{4,20},{8,24},{12,28},{16,0},{20,4},{24,8},{28,12},{1,17},{... | collective-permute-start | bytes 479240 | tf_op jit(solution)/shard_map/ppermute | solution.py:46
  180.7 21.1 %collective-permute-start.32 = (bf16[1,96,768]{2,1,0:T(8,128)(2,1)S(1)}, bf16[1,96,768]{2,1,0:T(8,128)(2,1)S(1)}, u32[]{:S(2)}, u32[]{:S(2)}) collective-permute-start(bf16[1,96,768]{2,1,0:T(8,128)(2,1)S(1)} %fusion.2), channel_id=1, source_target_pairs={{0,16},{4,20},{8,24},{12,28},{16,0},{20,4},{24,8},{28,12},{1,17},{... | collective-permute-start | bytes 442376 | tf_op jit(solution)/shard_map/ppermute | solution.py:46
  190.2 3.4 %copy-start.17 = (bf16[1,96,768]{2,1,0:T(8,128)(2,1)}, bf16[1,96,768]{2,1,0:T(8,128)(2,1)S(1)}, u32[]{:S(2)}) copy-start(bf16[1,96,768]{2,1,0:T(8,128)(2,1)S(1)} %collective-permute-done.28) | copy-start | bytes 442372
  196.3 10.3 %all-to-all-start.1 = ((bf16[4,56,768]{2,1,0:T(8,128)(2,1)}), bf16[4,56,768]{2,1,0:T(8,128)(2,1)S(1)}, u32[]{:S(2)}, u32[]{:S(2)}) async-start(bf16[4,56,768]{2,1,0:T(8,128)(2,1)} %get-tuple-element.58), calls=%async_computation.1 | async-start | bytes 688128 | tf_op jit(solution)/shard_map/all_to_all | solution.py:711
  200.4 2.2 %collective-permute-start.29 = (bf16[24,768]{1,0:T(8,128)(2,1)}, bf16[24,768]{1,0:T(8,128)(2,1)S(1)}, u32[]{:S(2)}, u32[]{:S(2)}) collective-permute-start(bf16[24,768]{1,0:T(8,128)(2,1)} %get-tuple-element.61), channel_id=1, source_target_pairs={{0,0},{4,1},{8,2},{12,3},{16,4},{20,5},{24,6},{28,7},{1,8},{5,9},{... | collective-permute-start | bytes 110600 | tf_op jit(solution)/shard_map/ppermute | solution.py:81
  209.2 0.9 copy-start.3
  (4 other events, 2.9 us)
